TPU v7x, 32 devices: a whole 2x2x4 slice. The times are simulated.
32 devices in a mesh: dp: 4 (over y, x), seq: 8 (over z, core).
Axes of the slice: x: 2, y: 2, z: 4, core: 2. Of those that a mesh axis runs over, the one named last changes fastest.
Arguments:
- tokens: bfloat16 [4, 2352, 1536], P('dp', 'seq'), may hold values from -6 to 6
- condition: float32 [4, 1024], P(None, ('dp', 'seq')), may hold values from -6 to 6
- caption: bfloat16 [4, 256, 4096], P(None, None, ('dp', 'seq')), may hold values from -6 to 6
- caption_len: int32 [4], replicated, may hold values from 1 to 256, as said below
- image_shape: int32 [4, 2], replicated, may hold values from 12 to 48, as said below
- cotangent: bfloat16 [4, 2352, 1536], P('dp', 'seq'), may hold values from -6 to 6
- joint_weight: bfloat16 [1536, 4608], P(('dp', 'seq')), may hold values from -0.15625 to 0.15625
- mixer_weight: bfloat16 [1536, 1536], P(('dp', 'seq')), may hold values from -0.15625 to 0.15625
- gate_up_weight: bfloat16 [1536, 8192], P(('dp', 'seq')), may hold values from -0.15625 to 0.15625
- down_weight: bfloat16 [4096, 1536], P(('dp', 'seq')), may hold values from -0.09375 to 0.09375
- text_weight: bfloat16 [4096, 3072], P(('dp', 'seq')), may hold values from -0.09375 to 0.09375
- modulation_weight: bfloat16 [1024, 9216], P(('dp', 'seq')), may hold values from -0.1875 to 0.1875
- modulation_bias: float32 [9216], P(('dp', 'seq')), may hold values from -3 to 3
- norm_gains: bfloat16 [7, 1536], P(None, ('dp', 'seq')), may hold values from 0.25 to 1.75
- head_gates: float32 [24], replicated, may hold values from -1.5 to 1.5
Outputs:
- output: bfloat16 [4, 2352, 1536], P('dp', 'seq')
- tokens_grad: bfloat16 [4, 2352, 1536], P('dp', 'seq')
- joint_grad: float32 [1536, 4608], P(('dp', 'seq'))
- mixer_grad: float32 [1536, 1536], P(('dp', 'seq'))
- gate_up_grad: float32 [1536, 8192], P(('dp', 'seq'))
- down_grad: float32 [4096, 1536], P(('dp', 'seq'))
- text_grad: float32 [4096, 3072], P(('dp', 'seq'))
- modulation_grad: float32 [1024, 9216], P(('dp', 'seq'))
- bias_grad: float32 [9216], P(('dp', 'seq'))
- gains_grad: float32 [7, 1536], P(None, ('dp', 'seq'))
- gates_grad: float32 [24], replicated
Inputs may be any that keep to these rules, and one draw needn't show every extreme that they name: `caption_len`: text tokens at or beyond an item's caption length are padding; some item's caption has all 256 tokens in every draw. `image_shape`: row (height, width) of an item: its first height * (width + 1) tokens are height image rows of width tokens, each followed by a nextline marker, and the tokens after them are padding; height >= 24; some item has height = width = 48 in every draw.
All inputs are finite; a program needn't handle non-finite values.
Results may differ from a plain program's by a relative error of at most 0.04.
Values may be sent and summed in bfloat16 or wider, within the bound.
No kernel may reach another device: no remote copies, remote signals or barrier semaphores. Data moves between devices by JAX's collectives and lax.ppermute only.
A program may use at most 448 MiB of HBM per device.

v0:
```python
import jax
import jax.numpy as jnp
from jax import lax
from jax.sharding import PartitionSpec as P

HEADS = 24
HEAD_DIM = 64
TEXT = 256


EPS = 1e-06


def norm_rows(v, gain):
    return v * lax.rsqrt(jnp.mean(v * v, axis=-1, keepdims=True) + EPS) * gain


def rotate(v, positions):
    half = HEAD_DIM // 2
    freq = jnp.exp(jnp.arange(half).astype(jnp.float32) * (-jnp.log(10000.0) / half))
    angle = positions.astype(jnp.float32)[:, None] * freq[None, :]
    cosine = jnp.cos(angle)[:, None, :]
    sine = jnp.sin(angle)[:, None, :]
    heads = v.reshape(v.shape[0], HEADS, HEAD_DIM)
    first = heads[..., :half]
    second = heads[..., half:]
    turned = jnp.concatenate(
        [first * cosine - second * sine, first * sine + second * cosine], axis=-1
    )
    return turned.reshape(v.shape[0], HEADS * HEAD_DIM)


def modulate(v, gain, scale, shift):
    return norm_rows(v, gain) * (1.0 + scale) + shift


def branch_out(v, gain, gate):
    return gate * norm_rows(v, gain)


def swiglu(gate_up):
    half = gate_up.shape[-1] // 2
    return jax.nn.silu(gate_up[:, :half]) * gate_up[:, half:]


def product(left, right):
    return jnp.dot(left, right, preferred_element_type=jnp.float32)


def product_left(left, right):
    return lax.dot_general(
        left, right, (((0,), (0,)), ((), ())), preferred_element_type=jnp.float32
    )


def product_right(left, right):
    return lax.dot_general(
        left, right, (((1,), (1,)), ((), ())), preferred_element_type=jnp.float32
    )


def head_block(full, index, size):
    return lax.dynamic_slice_in_dim(full, index * size, size, 0).reshape(size, HEADS, HEAD_DIM)


def scores_of(query_heads, keys, index, size, valid, scale):
    raw = (
        jnp.einsum(
            "qhd,khd->hqk",
            query_heads,
            head_block(keys, index, size),
            preferred_element_type=jnp.float32,
        )
        * scale
    )
    live = index * size + jnp.arange(size) < valid
    return jnp.where(live[None, None, :], raw, -1e30)


def attend_forward(queries, keys, values, valid, scale, count):
    rows = queries.shape[0]
    size = keys.shape[0] // count
    query_heads = queries.reshape(rows, HEADS, HEAD_DIM)

    def stat_step(carry, index):
        highest, totals = carry
        scores = scores_of(query_heads, keys, index, size, valid, scale)
        new_high = jnp.maximum(highest, jnp.max(scores, axis=-1))
        totals = totals * jnp.exp(highest - new_high) + jnp.sum(
            jnp.exp(scores - new_high[..., None]), axis=-1
        )
        return ((new_high, totals), None)

    begin = (jnp.full((HEADS, rows), -1e30, jnp.float32), jnp.zeros((HEADS, rows), jnp.float32))
    (highest, totals), _ = lax.scan(stat_step, begin, jnp.arange(count))
    spread = highest + jnp.log(totals)

    def mix_step(carry, index):
        weights = jnp.exp(
            scores_of(query_heads, keys, index, size, valid, scale) - spread[..., None]
        )
        weights = weights.astype(jnp.bfloat16)
        carry = carry + jnp.einsum(
            "hqk,khd->qhd",
            weights,
            head_block(values, index, size),
            preferred_element_type=jnp.float32,
        )
        return (carry, None)

    mixed, _ = lax.scan(
        mix_step, jnp.zeros((rows, HEADS, HEAD_DIM), jnp.float32), jnp.arange(count)
    )
    return (mixed.reshape(rows, HEADS * HEAD_DIM), spread)


def row_center(query_heads, upstream_heads, keys, values, valid, scale, count, spread, size):

    def center_step(carry, index):
        weights = jnp.exp(
            scores_of(query_heads, keys, index, size, valid, scale) - spread[..., None]
        )
        pushed = jnp.einsum(
            "qhd,khd->hqk",
            upstream_heads,
            head_block(values, index, size),
            preferred_element_type=jnp.float32,
        )
        return (carry + jnp.sum(weights * pushed, axis=-1), None)

    rows = query_heads.shape[0]
    center, _ = lax.scan(center_step, jnp.zeros((HEADS, rows), jnp.float32), jnp.arange(count))
    return center


def attend_backward(queries, keys, values, valid, scale, count, spread, upstream):
    rows = queries.shape[0]
    size = keys.shape[0] // count
    query_heads = queries.reshape(rows, HEADS, HEAD_DIM)
    upstream_heads = upstream.reshape(rows, HEADS, HEAD_DIM)
    center = row_center(
        query_heads, upstream_heads, keys, values, valid, scale, count, spread, size
    )

    def grad_step(carry, index):
        weights = jnp.exp(
            scores_of(query_heads, keys, index, size, valid, scale) - spread[..., None]
        )
        pushed = jnp.einsum(
            "qhd,khd->hqk",
            upstream_heads,
            head_block(values, index, size),
            preferred_element_type=jnp.float32,
        )
        score_grad = (weights * (pushed - center[..., None]) * scale).astype(jnp.bfloat16)
        carry = carry + jnp.einsum(
            "hqk,khd->qhd",
            score_grad,
            head_block(keys, index, size),
            preferred_element_type=jnp.float32,
        )
        key_grad = jnp.einsum(
            "hqk,qhd->khd", score_grad, query_heads, preferred_element_type=jnp.float32
        )
        value_grad = jnp.einsum(
            "hqk,qhd->khd",
            weights.astype(jnp.bfloat16),
            upstream_heads,
            preferred_element_type=jnp.float32,
        )
        return (carry, (key_grad, value_grad))

    query_grad, (key_grads, value_grads) = lax.scan(
        grad_step, jnp.zeros((rows, HEADS, HEAD_DIM), jnp.float32), jnp.arange(count)
    )
    width = HEADS * HEAD_DIM
    return (
        query_grad.reshape(rows, width),
        key_grads.reshape(count * size, width),
        value_grads.reshape(count * size, width),
    )


def local(
    tokens,
    condition,
    caption,
    caption_len,
    image_shape,
    cotangent,
    joint_weight,
    mixer_weight,
    gate_up_weight,
    down_weight,
    text_weight,
    modulation_weight,
    modulation_bias,
    norm_gains,
    head_gates,
):
    width = HEADS * HEAD_DIM
    items = tokens.shape[0]
    rows = tokens.shape[1]
    total_rows = items * rows
    first_item = lax.axis_index("dp") * items
    seq_start = lax.axis_index("seq") * rows
    scale = float(HEAD_DIM) ** (-0.5)
    soft_cond = jax.nn.silu(condition).astype(jnp.bfloat16)
    partial_mods = product(soft_cond, modulation_weight)
    bias_width = modulation_bias.shape[0]
    bias_start = lax.axis_index(("dp", "seq")) * bias_width
    with_bias = (
        lax.dynamic_slice_in_dim(partial_mods, bias_start, bias_width, 1) + modulation_bias[None, :]
    )
    partial_mods = lax.dynamic_update_slice_in_dim(partial_mods, with_bias, bias_start, 1)
    all_mods = lax.psum(partial_mods, ("dp", "seq"))
    mods = lax.dynamic_slice_in_dim(all_mods, first_item, items, 0)
    flat_text = caption.reshape(-1, caption.shape[2])
    text_raw = lax.psum_scatter(
        product(flat_text, text_weight), ("dp", "seq"), scatter_dimension=0, tiled=True
    )
    joint_full, mixer_full, gate_up_full, down_full, gains_full = (
        lax.all_gather(joint_weight, ("dp", "seq"), axis=0, tiled=True),
        lax.all_gather(mixer_weight, ("dp", "seq"), axis=0, tiled=True),
        lax.all_gather(gate_up_weight, ("dp", "seq"), axis=0, tiled=True),
        lax.all_gather(down_weight, ("dp", "seq"), axis=0, tiled=True),
        lax.all_gather(norm_gains, ("dp", "seq"), axis=1, tiled=True),
    )
    gains = gains_full.astype(jnp.float32)
    text_keys, text_key_pull = jax.vjp(norm_rows, text_raw[:, :width], gains[6])
    text_send = jnp.concatenate(
        [text_keys.astype(jnp.bfloat16), text_raw[:, width:].astype(jnp.bfloat16)], axis=1
    )
    text_group = lax.all_gather(text_send, "seq", axis=0, tiled=True).reshape(
        items, TEXT, 2 * width
    )
    xfloat = tokens.reshape(total_rows, width).astype(jnp.float32)
    mod_rows = jnp.repeat(mods, rows, axis=0)
    shift_a = mod_rows[:, 0:width]
    scale_a = mod_rows[:, width : 2 * width]
    gate_a = mod_rows[:, 2 * width : 3 * width]
    shift_f = mod_rows[:, 3 * width : 4 * width]
    scale_f = mod_rows[:, 4 * width : 5 * width]
    gate_f = mod_rows[:, 5 * width : 6 * width]
    normed_in, normed_pull = jax.vjp(modulate, xfloat, gains[0], scale_a, shift_a)
    normed_low = normed_in.astype(jnp.bfloat16)
    joint = product(normed_low, joint_full)
    positions = jnp.tile(seq_start + jnp.arange(rows), items)
    query_float, query_pull = jax.vjp(
        lambda value, gain: rotate(norm_rows(value, gain), positions), joint[:, :width], gains[4]
    )
    key_float, key_pull = jax.vjp(
        lambda value, gain: rotate(norm_rows(value, gain), positions),
        joint[:, width : 2 * width],
        gains[5],
    )
    queries = query_float.astype(jnp.bfloat16)
    own_keys = key_float.astype(jnp.bfloat16).reshape(items, rows, width)
    own_values = joint[:, 2 * width :].astype(jnp.bfloat16).reshape(items, rows, width)
    keys_all, values_all = (
        lax.all_gather(own_keys, "seq", axis=1, tiled=True),
        lax.all_gather(own_values, "seq", axis=1, tiled=True),
    )
    tanh_gates = jnp.tanh(head_gates)
    gate_cols = jnp.repeat(tanh_gates, HEAD_DIM)
    item = 0
    shape_row = image_shape[first_item + item]
    valid = shape_row[0] * (shape_row[1] + 1)
    length = caption_len[first_item + item]
    own_out, own_lse = attend_forward(queries, keys_all[item], values_all[item], valid, scale, 8)
    cross_out, cross_lse = attend_forward(
        queries, text_group[item, :, :width], text_group[item, :, width:], length, scale, 1
    )
    valid_list = [valid]
    length_list = [length]
    own_spread = [own_lse]
    cross_spread = [cross_lse]
    cross_list = [cross_out]
    mixed_list = own_out + gate_cols * cross_out
    mixed = mixed_list.astype(jnp.bfloat16)
    proj = product(mixed, mixer_full)
    branch_a, branch_a_pull = jax.vjp(branch_out, proj, gains[1], gate_a)
    hstate = xfloat + branch_a
    ffn_in, ffn_in_pull = jax.vjp(modulate, hstate, gains[2], scale_f, shift_f)
    ffn_low = ffn_in.astype(jnp.bfloat16)
    gate_up = product(ffn_low, gate_up_full)
    hidden, swiglu_pull = jax.vjp(swiglu, gate_up)
    hidden_low = hidden.astype(jnp.bfloat16)
    ffn = product(hidden_low, down_full)
    branch_f, branch_f_pull = jax.vjp(branch_out, ffn, gains[3], gate_f)
    output = (hstate + branch_f).astype(jnp.bfloat16).reshape(items, rows, width)
    upstream = cotangent.reshape(total_rows, width).astype(jnp.float32)
    joint_back, mixer_back, gate_up_back, down_back = (
        lax.all_gather(joint_weight, ("dp", "seq"), axis=0, tiled=True),
        lax.all_gather(mixer_weight, ("dp", "seq"), axis=0, tiled=True),
        lax.all_gather(gate_up_weight, ("dp", "seq"), axis=0, tiled=True),
        lax.all_gather(down_weight, ("dp", "seq"), axis=0, tiled=True),
    )
    ffn_grad, gain3_grad, gate_f_grad = branch_f_pull(upstream)
    ffn_grad_low = ffn_grad.astype(jnp.bfloat16)
    down_grad = product_left(hidden_low, ffn_grad_low)
    (gate_up_grad_rows,) = swiglu_pull(product_right(ffn_grad_low, down_back))
    gate_up_low = gate_up_grad_rows.astype(jnp.bfloat16)
    gate_up_grad = product_left(ffn_low, gate_up_low)
    state_part, gain2_grad, scale_f_grad, shift_f_grad = ffn_in_pull(
        product_right(gate_up_low, gate_up_back)
    )
    state_grad = upstream + state_part
    proj_grad, gain1_grad, gate_a_grad = branch_a_pull(state_grad)
    proj_low = proj_grad.astype(jnp.bfloat16)
    mixer_grad = product_left(mixed, proj_low)
    mixed_grad = product_right(proj_low, mixer_back).astype(jnp.bfloat16)
    keys_back, values_back = (
        lax.all_gather(own_keys, "seq", axis=1, tiled=True),
        lax.all_gather(own_values, "seq", axis=1, tiled=True),
    )
    item = 0
    upstream_float = mixed_grad.astype(jnp.float32)
    gate_cols_grad = jnp.sum(upstream_float * cross_list[item], axis=0)
    cross_upstream = (gate_cols * upstream_float).astype(jnp.bfloat16)
    own_q, own_k, own_v = attend_backward(
        queries,
        keys_back[item],
        values_back[item],
        valid_list[item],
        scale,
        8,
        own_spread[item],
        mixed_grad,
    )
    key_grad_list = [own_k]
    value_grad_list = [own_v]
    cross_q, cross_k, cross_v = attend_backward(
        queries,
        text_group[item, :, :width],
        text_group[item, :, width:],
        length_list[item],
        scale,
        1,
        cross_spread[item],
        cross_upstream,
    )
    query_grads = own_q + cross_q
    text_grad_list = jnp.concatenate([cross_k, cross_v], axis=1)
    gates_partial = jnp.sum(gate_cols_grad.reshape(HEADS, HEAD_DIM), axis=1) * (
        1.0 - tanh_gates * tanh_gates
    )
    key_sum, value_sum = (
        lax.psum_scatter(
            jnp.stack(key_grad_list).astype(jnp.bfloat16), "seq", scatter_dimension=1, tiled=True
        ).astype(jnp.float32),
        lax.psum_scatter(
            jnp.stack(value_grad_list).astype(jnp.bfloat16), "seq", scatter_dimension=1, tiled=True
        ).astype(jnp.float32),
    )
    query_raw_grad, gain4_grad = query_pull(query_grads)
    key_raw_grad, gain5_grad = key_pull(key_sum.reshape(total_rows, width))
    joint_grad_rows = jnp.concatenate(
        [query_raw_grad, key_raw_grad, value_sum.reshape(total_rows, width)], axis=1
    ).astype(jnp.bfloat16)
    joint_grad = product_left(normed_low, joint_grad_rows)
    input_part, gain0_grad, scale_a_grad, shift_a_grad = normed_pull(
        product_right(joint_grad_rows, joint_back)
    )
    tokens_grad = (state_grad + input_part).astype(jnp.bfloat16).reshape(items, rows, width)
    text_sum = lax.psum_scatter(
        text_grad_list.astype(jnp.bfloat16), "seq", scatter_dimension=0, tiled=True
    ).astype(jnp.float32)
    text_key_grad, gain6_grad = text_key_pull(text_sum[:, :width])
    text_grad_rows = jnp.concatenate([text_key_grad, text_sum[:, width:]], axis=1).astype(
        jnp.bfloat16
    )
    text_grad_all = lax.all_gather(text_grad_rows, ("dp", "seq"), axis=0, tiled=True)
    text_grad = product_left(flat_text, text_grad_all)

    def per_item(value):
        return jnp.sum(value.reshape(items, rows, width), axis=1)

    mods_own = jnp.concatenate(
        [
            per_item(shift_a_grad),
            per_item(scale_a_grad),
            per_item(gate_a_grad),
            per_item(shift_f_grad),
            per_item(scale_f_grad),
            per_item(gate_f_grad),
        ],
        axis=1,
    )
    mods_grad_all = lax.dynamic_update_slice_in_dim(
        jnp.zeros(all_mods.shape, jnp.float32), mods_own, first_item, 0
    )
    mods_sum, gates_grad = lax.psum((mods_grad_all, gates_partial), ("dp", "seq"))
    mods_low = mods_sum.astype(jnp.bfloat16)
    modulation_grad = product_left(soft_cond, mods_low)
    bias_grad = lax.dynamic_slice_in_dim(
        jnp.sum(mods_low.astype(jnp.float32), axis=0), bias_start, bias_width, 0
    )
    gains_partial = jnp.stack(
        [gain0_grad, gain1_grad, gain2_grad, gain3_grad, gain4_grad, gain5_grad, gain6_grad]
    )
    joint_out, mixer_out, gate_up_out, down_out, gains_grad = (
        lax.psum_scatter(joint_grad, ("dp", "seq"), scatter_dimension=0, tiled=True),
        lax.psum_scatter(mixer_grad, ("dp", "seq"), scatter_dimension=0, tiled=True),
        lax.psum_scatter(gate_up_grad, ("dp", "seq"), scatter_dimension=0, tiled=True),
        lax.psum_scatter(down_grad, ("dp", "seq"), scatter_dimension=0, tiled=True),
        lax.psum_scatter(gains_partial, ("dp", "seq"), scatter_dimension=1, tiled=True),
    )
    return (
        output,
        tokens_grad,
        joint_out,
        mixer_out,
        gate_up_out,
        down_out,
        text_grad,
        modulation_grad,
        bias_grad,
        gains_grad,
        gates_grad,
    )


def solution(mesh):
    in_specs = (
        P("dp", "seq", None),
        P(None, ("dp", "seq")),
        P(None, None, ("dp", "seq")),
        P(),
        P(),
        P("dp", "seq", None),
        P(("dp", "seq"), None),
        P(("dp", "seq"), None),
        P(("dp", "seq"), None),
        P(("dp", "seq"), None),
        P(("dp", "seq"), None),
        P(("dp", "seq"), None),
        P(("dp", "seq")),
        P(None, ("dp", "seq")),
        P(),
    )
    out_specs = (
        P("dp", "seq", None),
        P("dp", "seq", None),
        P(("dp", "seq"), None),
        P(("dp", "seq"), None),
        P(("dp", "seq"), None),
        P(("dp", "seq"), None),
        P(("dp", "seq"), None),
        P(("dp", "seq"), None),
        P(("dp", "seq")),
        P(None, ("dp", "seq")),
        P(),
    )
    return jax.shard_map(local, mesh=mesh, in_specs=in_specs, out_specs=out_specs, check_vma=False)
```

profile of v0, /device:TPU:0, one launch (start us, length us, event | category | flops | bytes accessed | tf_op | source)
XLA Modules:
  0.0 3011.1 jit_solution(14206747077686862348)
XLA Ops:
  18.6 43.6 %all-gather.1 = bf16[32,48,7]{1,2,0:T(8,128)(2,1)S(1)} all-gather(bf16[1,48,7]{1,2,0:T(8,128)(2,1)S(1)} %bitcast.262), channel_id=1, replica_groups=mesh['dp'=4,'seq'=8] {'dp','seq'}, dimensions={0}, use_global_device_ids=true | all-gather | bytes 22176 | tf_op jit(solution)/shard_map/all_gather | solution.py:227
  62.5 111.7 %reduce-scatter.14.cloned.1.call-done = f32[32,3072]{1,0:T(8,128)} async-done(((f32[1024,3072]{1,0:T(8,128)}), f32[32,3072]{1,0:T(8,128)}) %reduce-scatter.14.cloned.1.call-update) | async-done | bytes 393232 | tf_op jit(solution)/shard_map/reduce_scatter | solution.py:219
  178.9 122.2 %all-reduce.14.cloned.1.call-done = f32[4,9216]{1,0:T(4,128)} async-done(((f32[4,9216]{1,0:T(4,128)}), f32[4,9216]{1,0:T(4,128)}) %all-reduce.14.cloned.1.call-update) | async-done | bytes 147472 | tf_op jit(solution)/shard_map/psum | solution.py:216
  302.1 107.7 %all-gather.12.cloned.1.call-done = bf16[1536,4608]{1,0:T(8,128)(2,1)} async-done(((bf16[48,4608]{1,0:T(8,128)(2,1)}), bf16[1536,4608]{1,0:T(8,128)(2,1)}) %all-gather.12.cloned.1.call-update) | async-done | bytes 14155792 | tf_op jit(solution)/shard_map/all_gather | solution.py:223
  464.5 45.3 %all-gather.26.cloned.1.call-done = bf16[8,294,1536]{2,1,0:T(8,128)(2,1)} async-done(((bf16[1,294,1536]{2,1,0:T(8,128)(2,1)}), bf16[8,294,1536]{2,1,0:T(8,128)(2,1)}) %all-gather.26.cloned.1.call-update) | async-done | bytes 7225360 | tf_op jit(solution)/shard_map/all_gather | solution.py:262
  526.3 115.8 %all-gather.14.cloned.1.call-done = bf16[1,2352,1536]{2,0,1:T(2,128)(2,1)} async-done(((bf16[1,294,1536]{2,0,1:T(2,128)(2,1)}), bf16[1,2352,1536]{2,0,1:T(2,128)(2,1)}) %all-gather.14.cloned.1.call-update) | async-done | bytes 7225360 | tf_op jit(solution)/shard_map/all_gather | solution.py:261
  642.1 30.9 %copy.195 = bf16[1,2352,1536]{1,2,0:T(8,128)(2,1)} copy(bf16[1,2352,1536]{2,0,1:T(2,128)(2,1)} %all-gather.14.cloned.1.call-done) | data formatting | bytes 14450688
  673.0 135.3 %while.12 = (s32[]{:T(128)}, f32[24,294]{1,0:T(8,128)S(1)}, f32[24,294]{1,0:T(8,128)S(1)}, s32[8]{0:T(128)S(1)}, s32[]{:T(128)}, /*index=5*/bf16[2352,1536]{0,1:...) while((s32[]{:T(128)}, f32[24,294]{1,0:T(8,128)S(1)}, ...), condition=%wide.region_7.8_spmd.clone, body=%wide.region_4.7_spmd.clone.sunk | while | flops 280088512 | bytes 20576376 | solution.py:95
  808.3 106.8 %while.13 = (s32[]{:T(128)}, f32[294,24,64]{0,2,1:T(8,128)}, s32[8]{0:T(128)S(1)}, bf16[2352,1536]{0,1:T(8,128)(2,1)}, s32[]{:T(128)}, /*index=5*/bf16[2352,1536...) while((s32[]{:T(128)}, f32[294,24,64]{0,2,1:T(8,128)}, ...), condition=%wide.region_9.10_spmd.clone, body=%wide.region_8.9_spmd.clone.sunk | while | flops 540264384 | bytes 9963865 | solution.py:111
  929.0 13.6 fusion.137
  949.3 12.9 all-gather.22.cloned.1.call-done
  973.6 12.5 fusion.92
  986.1 17.3 multiply_reduce_fusion.4
  1029.6 87.1 %while.14 = (s32[]{:T(128)}, f32[24,294]{1,0:T(8,128)S(1)}, s32[8]{0:T(128)S(1)}, s32[]{:T(128)}, bf16[2352,1536]{0,1:T(8,128)(2,1)}, /*index=5*/bf16[294,24,64]...) while((s32[]{:T(128)}, f32[24,294]{1,0:T(8,128)S(1)}, ...), condition=%wide.region_22.23_spmd.clone, body=%wide.region_20.22_spmd.clone.sunk | while | flops 541442688 | bytes 27575676 | solution.py:132
  1118.1 46.7 %fusion.82 = bf16[24,64,256]{2,1,0:T(8,128)(2,1)} fusion(f32[24,294,256]{2,1,0:T(8,128)} %fusion.145, f32[24,294,256]{2,1,0:T(8,128)} %copy-done.7, f32[24,294]{1,0:T(8,128)S(1)} %copy-done.61, pred[256]{0:T(512)(128)(4,1)S(1)} %copy-done.95, bf16[294,24,32]{0,2,1:T(8,128)(2,1)S(1)} %copy-done.33, bf16[294,24,32]{0,2,1:T(8,128)(2,1)S(1)} %copy-done.31), kind=kOutput, calls=%fused_computation.139 | convolution fusion | flops 253287568 | bytes 16168768 | tf_op jit(solution)/shard_map/while/body/eval_jaxpr/hqk,qhd->khd/dot_general | solution.py:162
  1167.6 242.6 %while.15 = (s32[]{:T(128)}, f32[294,24,64]{0,2,1:T(8,128)}, bf16[8,294,24,64]{1,3,2,0:T(8,128)(2,1)}, bf16[8,294,24,64]{1,3,2,0:T(8,128)(2,1)}, s32[8]{0:T(128)...) while((s32[]{:T(128)}, f32[294,24,64]{0,2,1:T(8,128)}, ...), condition=%wide.region_24.25_spmd.clone, body=%wide.region_23.24_spmd.clone.sunk | while | flops 1351379840 | bytes 145896320 | solution.py:173
  1410.2 17.9 copy.188
  1428.1 19.2 reshape.524
  1447.3 14.6 copy.178
  1462.0 15.4 convert_element_type.169
  1477.5 146.7 %fusion = bf16[296,1536]{1,0:T(8,128)(2,1)} fusion(bf16[1,2352,1536]{2,1,0:T(8,128)(2,1)} %reshape.524), kind=kCustom, calls=%all-reduce-scatter | all-reduce-scatter fusion | flops 3637249 | bytes 8135168
  1626.4 47.2 %bitcast_add_fusion.2 = f32[294,24,64]{0,2,1:T(8,128)} fusion(f32[294,24,64]{0,2,1:T(8,128)S(1)} %copy-done.5, bf16[256,24,64]{0,2,1:T(8,128)(2,1)S(1)} %bitcast.257, f32[24,294,256]{2,1,0:T(8,128)} %fusion.145, f32[24,294,256]{2,1,0:T(8,128)} %copy-done.7, f32[24,294]{1,0:T(8,128)S(1)} %copy-done.61, pred[256]{0:T(512)(128)(4,1)S(1)} %copy-done.95), kind=kOutput, calls=%fused_computation.87 | convolution fusion | flops 251539600 | bytes 18878272 | tf_op jit(solution)/shard_map/while/body/eval_jaxpr/hqk,khd->qhd/dot_general | solution.py:156
  1681.1 17.2 all-reduce.16.cloned.1.call-done
  1742.2 13.7 fusion.147
  1757.4 14.4 fusion.85
  1773.4 24.9 fusion.90
  1800.4 42.8 %all-reduce.17 = (bf16[4,9216]{1,0:T(4,128)(2,1)S(1)}, f32[24]{0:T(128)}) all-reduce(f32[4,9216]{1,0:T(4,128)S(1)} %dynamic_update_slice.19, f32[24]{0:T(128)S(1)} %subtract_multiply_fusion.1), channel_id=1, replica_groups=mesh['dp'=4,'seq'=8] {'dp','seq'}, use_global_device_ids=true, to_apply=%region_43.44 | all-reduce | flops 36888 | bytes 221376 | tf_op jit(solution)/shard_map/psum | solution.py:393
  1849.7 53.5 %all-gather.24.cloned.1.call-done = bf16[1024,3072]{1,0:T(8,128)(2,1)} async-done(((bf16[32,3072]{1,0:T(8,128)(2,1)}), bf16[1024,3072]{1,0:T(8,128)(2,1)}) %all-gather.24.cloned.1.call-update) | async-done | bytes 6291472 | tf_op jit(solution)/shard_map/all_gather | solution.py:373
  1909.5 134.2 %reduce-scatter.18.cloned.1.call-done = f32[48,1536]{1,0:T(8,128)} async-done(((f32[1536,1536]{1,0:T(8,128)}), f32[48,1536]{1,0:T(8,128)}) %reduce-scatter.18.cloned.1.call-update) | async-done | bytes 294928 | tf_op jit(solution)/shard_map/reduce_scatter | solution.py:404
  2043.7 252.4 %reduce-scatter.22.cloned.1.call-done = f32[128,1536]{1,0:T(8,128)} async-done(((f32[4096,1536]{1,0:T(8,128)}), f32[128,1536]{1,0:T(8,128)}) %reduce-scatter.22.cloned.1.call-update) | async-done | bytes 786448 | tf_op jit(solution)/shard_map/reduce_scatter | solution.py:406
  2296.1 270.2 %reduce-scatter.16.cloned.1.call-done = f32[48,4608]{1,0:T(8,128)} async-done(((f32[1536,4608]{1,0:T(8,128)}), f32[48,4608]{1,0:T(8,128)}) %reduce-scatter.16.cloned.1.call-update) | async-done | bytes 884752 | tf_op jit(solution)/shard_map/reduce_scatter | solution.py:403
  2566.3 438.1 %reduce-scatter.20.cloned.1.call-done = f32[48,8192]{1,0:T(8,128)} async-done(((f32[1536,8192]{1,0:T(8,128)}), f32[48,8192]{1,0:T(8,128)}) %reduce-scatter.20.cloned.1.call-update) | async-done | bytes 1572880 | tf_op jit(solution)/shard_map/reduce_scatter | solution.py:405
  (677 shorter events, 767.5 us)
Async XLA Ops:
  7.2 167.0 %reduce-scatter.14.cloned.1.call-start = ((), (), s32[]{:S(2)}) async-start(), calls=%async_computation.10 | async-start | bytes 12976128 | tf_op jit(solution)/shard_map/reduce_scatter | solution.py:219
  15.6 162.4 %copy-start.15 = (bf16[1,294,1536]{2,1,0:T(8,128)(2,1)S(1)}, bf16[1,294,1536]{2,1,0:T(8,128)(2,1)}, u32[]{:S(2)}) copy-start(bf16[1,294,1536]{2,1,0:T(8,128)(2,1)} %param.23) | copy-start | bytes 2709508
  15.6 285.5 %all-reduce.14.cloned.1.call-start = ((), (), s32[]{:S(2)}) async-start(), calls=%async_computation.7 | async-start | bytes 294912 | tf_op jit(solution)/shard_map/psum | solution.py:216
  17.8 392.0 %all-gather.12.cloned.1.call-start = ((), (), s32[]{:S(2)}) async-start(), calls=%async_computation.8 | async-start | bytes 14598144 | tf_op jit(solution)/shard_map/all_gather | solution.py:223
  18.6 429.9 %all-gather.16.cloned.1.call-start = ((), (), s32[]{:S(2)}) async-start(), calls=%async_computation.11 | async-start | bytes 1769472 | tf_op jit(solution)/shard_map/all_gather | solution.py:234
  62.5 355.5 %copy-start.54 = (f32[1536]{0:T(1024)}, f32[1536]{0:T(1024)S(1)}, u32[]{:S(2)}) copy-start(f32[1536]{0:T(1024)S(1)} %get-tuple-element.729) | copy-start | bytes 18436
  62.5 355.5 %copy-start.62 = (f32[1536]{0:T(1024)}, f32[1536]{0:T(1024)S(1)}, u32[]{:S(2)}) copy-start(f32[1536]{0:T(1024)S(1)} %get-tuple-element.726) | copy-start | bytes 18436
  62.5 362.3 %copy-start.66 = (f32[1536]{0:T(1024)}, f32[1536]{0:T(1024)S(1)}, u32[]{:S(2)}) copy-start(f32[1536]{0:T(1024)S(1)} %get-tuple-element.727) | copy-start | bytes 18436
  62.5 362.3 %copy-start.68 = (f32[1536]{0:T(1024)}, f32[1536]{0:T(1024)S(1)}, u32[]{:S(2)}) copy-start(f32[1536]{0:T(1024)S(1)} %get-tuple-element.728) | copy-start | bytes 18436
  62.5 940.9 %copy-start.44 = (f32[1536]{0:T(1024)}, f32[1536]{0:T(1024)S(1)}, u32[]{:S(2)}) copy-start(f32[1536]{0:T(1024)S(1)} %get-tuple-element.724) | copy-start | bytes 18436
  178.0 331.8 %all-gather.26.cloned.1.call-start = ((), (), s32[]{:S(2)}) async-start(), calls=%async_computation.21 | async-start | bytes 8183808 | tf_op jit(solution)/shard_map/all_gather | solution.py:262
  178.9 239.1 %copy-start.70 = (f32[294]{0:T(512)}, f32[294]{0:T(512)S(1)}, u32[]{:S(2)}) copy-start(f32[294]{0:T(512)S(1)} %fusion.109) | copy-start | bytes 3532
  302.1 116.0 %copy-start.56 = (f32[1536]{0:T(1024)}, f32[1536]{0:T(1024)S(1)}, u32[]{:S(2)}) copy-start(f32[1536]{0:T(1024)S(1)} %get-tuple-element.720) | copy-start | bytes 18436
  302.1 116.0 %copy-start.58 = (f32[1536]{0:T(1024)}, f32[1536]{0:T(1024)S(1)}, u32[]{:S(2)}) copy-start(f32[1536]{0:T(1024)S(1)} %get-tuple-element.719) | copy-start | bytes 18436
  302.1 626.9 %copy-start.52 = (f32[1536]{0:T(1024)}, f32[1536]{0:T(1024)S(1)}, u32[]{:S(2)}) copy-start(f32[1536]{0:T(1024)S(1)} %get-tuple-element.722) | copy-start | bytes 18436
  302.1 701.3 %copy-start.46 = (f32[1536]{0:T(1024)}, f32[1536]{0:T(1024)S(1)}, u32[]{:S(2)}) copy-start(f32[1536]{0:T(1024)S(1)} %get-tuple-element.718) | copy-start | bytes 18436
  421.4 220.7 %all-gather.14.cloned.1.call-start = ((), (), s32[]{:S(2)}) async-start(), calls=%async_computation.9 | async-start | bytes 16257024 | tf_op jit(solution)/shard_map/all_gather | solution.py:261
  440.9 480.5 %all-gather.18.cloned.1.call-start = ((), (), s32[]{:S(2)}) async-start(), calls=%async_computation.12 | async-start | bytes 4866048 | tf_op jit(solution)/shard_map/all_gather | solution.py:224
  441.6 487.4 %all-gather.20.cloned.1.call-start = ((), (), s32[]{:S(2)}) async-start(), calls=%async_computation.13 | async-start | bytes 25952256 | tf_op jit(solution)/shard_map/all_gather | solution.py:225
  442.4 519.8 %all-gather.22.cloned.1.call-start = ((), (), s32[]{:S(2)}) async-start(), calls=%async_computation.14 | async-start | bytes 12976128 | tf_op jit(solution)/shard_map/all_gather | solution.py:226
  443.1 1235.9 %reduce-scatter.24.cloned.1.call-start = ((), (), s32[]{:S(2)}) async-start(), calls=%async_computation.19 | async-start | bytes 1769472 | tf_op jit(solution)/shard_map/reduce_scatter | solution.py:366
  1167.6 530.7 %all-reduce.16.cloned.1.call-start = ((), (), s32[]{:S(2)}) async-start(), calls=%async_computation.23 | async-start | bytes 14942208
  1477.4 148.9 %copy-start.5 = (f32[294,24,64]{0,2,1:T(8,128)S(1)}, f32[294,24,64]{0,2,1:T(8,128)}, u32[]{:S(2)}) copy-start(f32[294,24,64]{0,2,1:T(8,128)} %get-tuple-element.302) | copy-start | bytes 5419012
  1477.4 148.9 %copy-start.41 = (bf16[1,256,1536]{1,2,0:T(8,128)(2,1)S(1)}, bf16[1,256,1536]{1,2,0:T(8,128)(2,1)}, u32[]{:S(2)}) copy-start(bf16[1,256,1536]{1,2,0:T(8,128)(2,1)} %copy.168) | copy-start | bytes 2359300
  1477.4 370.9 %reduce-scatter.26.cloned.1.call-start = ((), (), s32[]{:S(2)}) async-start(), calls=%async_computation.22 | async-start | bytes 811008
  1625.0 48.6 %collective-permute-start = (bf16[14,1536]{1,0:T(8,128)(2,1)S(1)}, bf16[14,1536]{1,0:T(8,128)(2,1)S(1)}, u32[]{:S(2)}, u32[]{:S(2)}) collective-permute-start(bf16[14,1536]{1,0:T(8,128)(2,1)S(1)} %slice.177), channel_id=1, source_target_pairs={{0,1},{1,2},{2,3},{3,4},{4,5},{5,6},{6,7},{8,9},{9,10},{10,11},{11... | collective-permute-start | bytes 129032
  1735.2 168.0 %all-gather.24.cloned.1.call-start = ((), (), s32[]{:S(2)}) async-start(), calls=%async_computation.20 | async-start | bytes 6488064 | tf_op jit(solution)/shard_map/all_gather | solution.py:373
  1736.0 307.7 %reduce-scatter.18.cloned.1.call-start = ((), (), s32[]{:S(2)}) async-start(), calls=%async_computation.16 | async-start | bytes 9732096 | tf_op jit(solution)/shard_map/reduce_scatter | solution.py:404
  1741.1 555.0 %reduce-scatter.22.cloned.1.call-start = ((), (), s32[]{:S(2)}) async-start(), calls=%async_computation.18 | async-start | bytes 25952256 | tf_op jit(solution)/shard_map/reduce_scatter | solution.py:406
  1756.0 810.4 %reduce-scatter.16.cloned.1.call-start = ((), (), s32[]{:S(2)}) async-start(), calls=%async_computation.15 | async-start | bytes 29196288 | tf_op jit(solution)/shard_map/reduce_scatter | solution.py:403
  1771.9 1232.5 %reduce-scatter.20.cloned.1.call-start = ((), (), s32[]{:S(2)}) async-start(), calls=%async_computation.17 | async-start | bytes 51904512 | tf_op jit(solution)/shard_map/reduce_scatter | solution.py:405
  1903.2 1101.2 %copy-start.1 = (bf16[128,3072]{1,0:T(8,128)(2,1)S(1)}, bf16[128,3072]{1,0:T(8,128)(2,1)}, u32[]{:S(2)}) copy-start(bf16[128,3072]{1,0:T(8,128)(2,1)} %param.33) | copy-start | bytes 2359300
  (134 other events, 1074.7 us)
Sparse Core Ops, SparseCore 0:
  15.7 158.4 reduce-scatter.13
  181.3 119.7 all-reduce.13
  304.6 105.2 all-gather.11
  412.0 23.1 all-gather.15
  437.4 72.3 all-gather.25
  511.4 130.6 all-gather.13
  645.6 61.8 all-gather.17
  710.9 153.4 all-gather.19
  867.9 94.2 all-gather.21
  1167.7 32.5 reduce-scatter.23
  1477.5 220.7 all-reduce.15
  1735.3 96.0 reduce-scatter.25
  1834.4 68.7 all-gather.23
  1909.5 134.0 reduce-scatter.17
  2051.7 244.3 reduce-scatter.21
  2302.9 263.3 reduce-scatter.15
  2573.2 431.1 reduce-scatter.19
where the time goes:
time: 3020 us; the launch traced here: 3010 us
  waiting for transfers between devices  1680 us (56%)
  matrix products  602 us (20%)
  local copies, waits for them, and re-layouts  336 us (11%)
  blocking collectives  233 us (8%)
  other arithmetic  113 us (4%)
    reduce_scatter x1, waiting for transfers between devices, local(): lax.psum_scatter(gate_up_grad, ('dp', 'seq'), scatter_dimension=0, tiled=...  438 us
    reduce_scatter x1, waiting for transfers between devices, local(): lax.psum_scatter(joint_grad, ('dp', 'seq'), scatter_dimension=0, tiled=True)  270 us
    reduce_scatter x1, waiting for transfers between devices, local(): lax.psum_scatter(down_grad, ('dp', 'seq'), scatter_dimension=0, tiled=True)  252 us
    unnamed x1, blocking collectives  147 us
    reduce_scatter x1, waiting for transfers between devices, local(): lax.psum_scatter(mixer_grad, ('dp', 'seq'), scatter_dimension=0, tiled=True)  134 us
    psum x1, waiting for transfers between devices, local(): all_mods = lax.psum(partial_mods, ('dp', 'seq'))  122 us
    all_gather x1, waiting for transfers between devices, local(): lax.all_gather(own_keys, 'seq', axis=1, tiled=True)  116 us
    reduce_scatter x1, waiting for transfers between devices, local(): lax.psum_scatter(product(flat_text, text_weight), ('dp', 'seq'), scatter_...  112 us
  transfers between devices with their start and end apart: 18, of which 12 were waited for; matrix products, arithmetic and copies ran while one was open for 30% of the time, Pallas kernels for 0%

commit v1 on v0

v1 whole, which is shorter than its diff:
```python
import functools

import jax
import jax.numpy as jnp
from jax import lax
from jax.experimental import pallas as pl
from jax.experimental.pallas import tpu as pltpu
from jax.sharding import Mesh
from jax.sharding import PartitionSpec as P

HEADS = 24
HEAD_DIM = 64
TEXT = 256
WIDTH = HEADS * HEAD_DIM
EPS = 1e-06
NEG = -1e30
SCALE = float(HEAD_DIM) ** (-0.5)
LANES = 128
BF = jnp.bfloat16
F32 = jnp.float32
VMEM_BYTES = 56 << 20


def norm_rows(v, gain):
    return v * lax.rsqrt(jnp.mean(v * v, axis=-1, keepdims=True) + EPS) * gain


def modulate(v, gain, scale, shift):
    return norm_rows(v, gain) * (1.0 + scale) + shift


def branch_out(v, gain, gate):
    return gate * norm_rows(v, gain)


def swiglu(gate_up):
    half = gate_up.shape[-1] // 2
    return jax.nn.silu(gate_up[:, :half]) * gate_up[:, half:]


def product(left, right):
    return jnp.dot(left, right, preferred_element_type=F32)


def contract(left, right, left_dim, right_dim):
    return lax.dot_general(
        left, right, (((left_dim,), (right_dim,)), ((), ())), preferred_element_type=F32
    )


def split3(v):
    high = v.astype(BF)
    rest = v - high.astype(F32)
    mid = rest.astype(BF)
    return [high, mid, (rest - mid.astype(F32)).astype(BF)]


def extend(block, columns):
    rows = block.shape[0]
    fill = HEAD_DIM - len(columns)
    return jnp.concatenate([block] + list(columns) + [jnp.zeros((rows, fill), BF)], axis=1)


def spread_keys(heads, qkv_ref, text_ref, bias_ref, text_bias_ref, outs, key_ones, value_ones):
    wide = heads * HEAD_DIM
    for source, bias, key_out, value_out, start in (
        (qkv_ref, bias_ref, outs[0], outs[1], wide),
        (text_ref, text_bias_ref, outs[2], outs[3], 0),
    ):
        one = jnp.ones((source.shape[0], 1), BF)
        for h in range(heads):
            at = start + h * HEAD_DIM
            key_out[h] = extend(source[:, at : at + HEAD_DIM], [bias[...]] + [one] * key_ones)
            at = at + wide
            value_out[h] = extend(source[:, at : at + HEAD_DIM], [one] * value_ones)


def attend_forward_kernel(
    heads, qkv_ref, text_ref, bias_ref, text_bias_ref, gate_ref, q_ref,
    mixed_ref, own_ref, cross_ref, lse_ref, *spread
):
    @pl.when(pl.program_id(0) == 0)
    def _():
        spread_keys(heads, qkv_ref, text_ref, bias_ref, text_bias_ref, spread, 0, 1)

    one = jnp.ones((q_ref.shape[0], 1), BF)

    def soft(query, keys, values):
        scores = contract(query, keys[...], 1, 1)
        high = jnp.max(scores, axis=1, keepdims=True)
        total = contract(jnp.exp(scores - high).astype(BF), values[...], 1, 0)
        mass = total[:, HEAD_DIM : HEAD_DIM + 1]
        return total[:, :HEAD_DIM] / mass, high + jnp.log(mass)

    own, cross, lse = [], [], []
    for h in range(heads):
        at = h * HEAD_DIM
        query = extend(q_ref[:, at : at + HEAD_DIM] * SCALE, [one])
        mixed, own_lse = soft(query, spread[0].at[h], spread[1].at[h])
        own.append(mixed)
        mixed, cross_lse = soft(query, spread[2].at[h], spread[3].at[h])
        cross.append(mixed)
        lse += [own_lse, cross_lse]
    own = jnp.concatenate(own, axis=1)
    cross = jnp.concatenate(cross, axis=1)
    own_ref[...] = own
    cross_ref[...] = cross
    mixed_ref[...] = (own + gate_ref[...] * cross).astype(BF)
    lse_ref[...] = jnp.concatenate(lse, axis=1)


def attend_backward_kernel(
    heads, qkv_ref, text_ref, bias_ref, text_bias_ref, gate_ref, q_ref, up_ref, own_ref, cross_ref, lse_ref,
    dq_ref, dkv_ref, dtext_ref, dgate_ref, *scratch
):
    spread, sums = scratch[:4], scratch[4:]
    step = pl.program_id(0)

    @pl.when(step == 0)
    def _():
        spread_keys(heads, qkv_ref, text_ref, bias_ref, text_bias_ref, spread, 3, 3)
        for ref in sums + (dgate_ref,):
            ref[...] = jnp.zeros_like(ref)

    one = jnp.ones((q_ref.shape[0], 1), BF)
    up = up_ref[...]
    up_float = up.astype(F32)
    up_cross = (gate_ref[...] * up_float).astype(BF)
    dgate_ref[...] += jnp.sum(up_float * cross_ref[...], axis=0, keepdims=True)
    own_row = up_float * own_ref[...]
    cross_row = up_cross.astype(F32) * cross_ref[...]
    dq = []
    for h in range(heads):
        cut = slice(h * HEAD_DIM, (h + 1) * HEAD_DIM)
        query = q_ref[:, cut]
        scaled = query * SCALE

        def one_soft(upstream, row, lse, keys, values, key_sum, value_sum):
            center = jnp.sum(row, axis=1, keepdims=True)
            left = extend(scaled, [one] + [-part for part in split3(lse)])
            weights = jnp.exp(contract(left, keys[...], 1, 1))
            left = extend(upstream, [-part for part in split3(center)])
            score_grad = (weights * contract(left, values[...], 1, 1)).astype(BF)
            weights = weights.astype(BF)
            key_sum[...] += contract(score_grad, query, 0, 0)
            value_sum[...] += contract(weights, upstream, 0, 0)
            return contract(score_grad, keys[...], 1, 0)[:, :HEAD_DIM]

        part = one_soft(
            up[:, cut], own_row[:, cut], lse_ref[:, 2 * h : 2 * h + 1],
            spread[0].at[h], spread[1].at[h], sums[0].at[h], sums[1].at[h],
        )
        part += one_soft(
            up_cross[:, cut], cross_row[:, cut], lse_ref[:, 2 * h + 1 : 2 * h + 2],
            spread[2].at[h], spread[3].at[h], sums[2].at[h], sums[3].at[h],
        )
        dq.append(part * SCALE)
    dq_ref[...] = jnp.concatenate(dq, axis=1).astype(BF)

    @pl.when(step == pl.num_programs(0) - 1)
    def _():
        for out, key_sum, value_sum in ((dkv_ref, sums[0], sums[1]), (dtext_ref, sums[2], sums[3])):
            parts = [key_sum[h] * SCALE for h in range(heads)] + [value_sum[h] for h in range(heads)]
            out[...] = jnp.concatenate(parts, axis=1).astype(BF)


def whole_block(shape):
    return pl.BlockSpec(shape, lambda i: (0,) * len(shape), pipeline_mode=pl.Buffered(1))


def row_block(rows, columns):
    return pl.BlockSpec((rows, columns), lambda i: (i, 0))


def spread_scratch(heads, slots, text):
    return [pltpu.VMEM((heads, n, 2 * HEAD_DIM), BF) for n in (slots, slots, text, text)]


def attend_forward(qkv, text, bias, text_bias, gate, heads, rows):
    slots, wide, words = qkv.shape[0], heads * HEAD_DIM, text.shape[0]
    return pl.pallas_call(
        functools.partial(attend_forward_kernel, heads),
        grid=(slots // rows,),
        in_specs=[
            whole_block((slots, 3 * wide)), whole_block((words, 2 * wide)), whole_block((slots, 1)),
            whole_block((words, 1)), whole_block((1, wide)), row_block(rows, wide),
        ],
        out_specs=[row_block(rows, wide)] * 3 + [row_block(rows, 2 * heads)],
        out_shape=[
            jax.ShapeDtypeStruct((slots, wide), BF),
            jax.ShapeDtypeStruct((slots, wide), F32),
            jax.ShapeDtypeStruct((slots, wide), F32),
            jax.ShapeDtypeStruct((slots, 2 * heads), F32),
        ],
        scratch_shapes=spread_scratch(heads, slots, words),
        compiler_params=pltpu.CompilerParams(vmem_limit_bytes=VMEM_BYTES),
        cost_estimate=pl.CostEstimate(
            flops=16 * slots * (slots + words) * wide,
            bytes_accessed=slots * wide * 18,
            transcendentals=slots * (slots + words) * heads,
        ),
        name="attend_forward",
    )(qkv, text, bias, text_bias, gate, qkv[:, :wide])


def attend_backward(qkv, text, bias, text_bias, gate, up, own, cross, lse, heads, rows):
    slots, wide, words = qkv.shape[0], heads * HEAD_DIM, text.shape[0]
    return pl.pallas_call(
        functools.partial(attend_backward_kernel, heads),
        grid=(slots // rows,),
        in_specs=[
            whole_block((slots, 3 * wide)), whole_block((words, 2 * wide)), whole_block((slots, 1)),
            whole_block((words, 1)), whole_block((1, wide)),
            row_block(rows, wide), row_block(rows, wide), row_block(rows, wide), row_block(rows, wide),
            row_block(rows, 2 * heads),
        ],
        out_specs=[
            row_block(rows, wide), whole_block((slots, 2 * wide)), whole_block((words, 2 * wide)),
            whole_block((1, wide)),
        ],
        out_shape=[
            jax.ShapeDtypeStruct((slots, wide), BF),
            jax.ShapeDtypeStruct((slots, 2 * wide), BF),
            jax.ShapeDtypeStruct((words, 2 * wide), BF),
            jax.ShapeDtypeStruct((1, wide), F32),
        ],
        scratch_shapes=spread_scratch(heads, slots, words)
        + [pltpu.VMEM((heads, n, HEAD_DIM), F32) for n in (slots, slots, words, words)],
        compiler_params=pltpu.CompilerParams(vmem_limit_bytes=VMEM_BYTES),
        cost_estimate=pl.CostEstimate(
            flops=40 * slots * (slots + words) * wide,
            bytes_accessed=slots * wide * 26,
            transcendentals=slots * (slots + words) * heads,
        ),
        name="attend_backward",
    )(qkv, text, bias, text_bias, gate, qkv[:, :wide], up, own, cross, lse)


def swap_halves(v):
    lane = lax.broadcasted_iota(jnp.int32, v.shape, 1)
    half = HEAD_DIM // 2
    return jnp.where(
        lane % HEAD_DIM < half, pltpu.roll(v, LANES - half, 1), pltpu.roll(v, half, 1)
    )


def tiles_of(v):
    return [v[:, t : t + LANES] for t in range(0, v.shape[1], LANES)]


def group_kernel(heads, groups, joint_ref, gains_ref, cos_ref, sin_ref, out_ref):
    wide = heads * HEAD_DIM
    cosine, sine = cos_ref[...], sin_ref[...]
    parts = []
    for which in range(2):
        raw = joint_ref[:, which * WIDTH : (which + 1) * WIDTH]
        root = lax.rsqrt(jnp.mean(raw * raw, axis=1, keepdims=True) + EPS)
        scaled = raw * root * gains_ref[which : which + 1, :]
        turned = [tile * cosine + swap_halves(tile) * sine for tile in tiles_of(scaled)]
        parts.append(jnp.concatenate(turned, axis=1).astype(BF))
    parts.append(joint_ref[:, 2 * WIDTH :].astype(BF))
    for g in range(groups):
        for which, part in enumerate(parts):
            at = g * wide
            size = max(0, min(wide, WIDTH - at))
            if size:
                out_ref[g, :, which * wide : which * wide + size] = part[:, at : at + size]
            if size < wide:
                out_ref[g, :, which * wide + size : (which + 1) * wide] = jnp.zeros(
                    (part.shape[0], wide - size), BF
                )


def ungroup_kernel(heads, groups, grad_ref, joint_ref, gains_ref, cos_ref, sin_ref, out_ref, dgain_ref):
    wide = heads * HEAD_DIM
    cosine, sine = cos_ref[...], sin_ref[...]

    @pl.when(pl.program_id(0) == 0)
    def _():
        dgain_ref[...] = jnp.zeros_like(dgain_ref)

    def rows_of(which):
        parts = []
        for g in range(groups):
            size = max(0, min(wide, WIDTH - g * wide))
            if size:
                parts.append(grad_ref[g, :, which * wide : which * wide + size])
        return jnp.concatenate(parts, axis=1)

    for which in range(2):
        cut = slice(which * WIDTH, (which + 1) * WIDTH)
        grad = rows_of(which).astype(F32)
        turned = [tile * cosine - swap_halves(tile) * sine for tile in tiles_of(grad)]
        grad = jnp.concatenate(turned, axis=1)
        raw = joint_ref[:, cut]
        root = lax.rsqrt(jnp.mean(raw * raw, axis=1, keepdims=True) + EPS)
        unit = raw * root
        dgain_ref[which : which + 1, :] += jnp.sum(grad * unit, axis=0, keepdims=True)
        grad = grad * gains_ref[which : which + 1, :]
        grad = root * (grad - unit * jnp.mean(grad * unit, axis=1, keepdims=True))
        out_ref[:, cut] = grad.astype(BF)
    out_ref[:, 2 * WIDTH :] = rows_of(2)


def group_heads(joint, gains, cosine, sine, heads, groups):
    rows = joint.shape[0]
    block = rows // 2
    return pl.pallas_call(
        functools.partial(group_kernel, heads, groups),
        grid=(2,),
        in_specs=[
            row_block(block, 3 * WIDTH), whole_block((2, WIDTH)), row_block(block, LANES), row_block(block, LANES)
        ],
        out_specs=pl.BlockSpec((groups, block, 3 * heads * HEAD_DIM), lambda i: (0, i, 0)),
        out_shape=jax.ShapeDtypeStruct((groups, rows, 3 * heads * HEAD_DIM), BF),
        compiler_params=pltpu.CompilerParams(vmem_limit_bytes=VMEM_BYTES),
        cost_estimate=pl.CostEstimate(
            flops=rows * WIDTH * 30, bytes_accessed=rows * WIDTH * 18, transcendentals=rows
        ),
        name="group_heads",
    )(joint, gains, cosine, sine)


def ungroup_heads(grads, joint, gains, cosine, sine, heads):
    groups, rows, wide = grads.shape
    block = rows // 2
    return pl.pallas_call(
        functools.partial(ungroup_kernel, heads, groups),
        grid=(2,),
        in_specs=[
            pl.BlockSpec((groups, block, wide), lambda i: (0, i, 0)),
            row_block(block, 3 * WIDTH), whole_block((2, WIDTH)), row_block(block, LANES), row_block(block, LANES),
        ],
        out_specs=[row_block(block, 3 * WIDTH), whole_block((2, WIDTH))],
        out_shape=[
            jax.ShapeDtypeStruct((rows, 3 * WIDTH), BF),
            jax.ShapeDtypeStruct((2, WIDTH), F32),
        ],
        compiler_params=pltpu.CompilerParams(vmem_limit_bytes=VMEM_BYTES),
        cost_estimate=pl.CostEstimate(
            flops=rows * WIDTH * 50, bytes_accessed=rows * WIDTH * 24, transcendentals=rows
        ),
        name="ungroup_heads",
    )(grads, joint, gains, cosine, sine)


def local(
    sizes,
    tokens,
    condition,
    caption,
    caption_len,
    image_shape,
    cotangent,
    joint_weight,
    mixer_weight,
    gate_up_weight,
    down_weight,
    text_weight,
    modulation_weight,
    modulation_bias,
    norm_gains,
    head_gates,
):
    n_dp, n_z, n_core = sizes
    everyone = ("dp", "z", "core")
    seq = ("z", "core")
    n_seq = n_z * n_core
    heads = -(-HEADS // n_seq)
    wide = heads * HEAD_DIM
    spare = n_seq * heads - HEADS
    rows = tokens.shape[1]
    slots = -(-rows // 16) * 16
    dp = lax.axis_index("dp")
    core = lax.axis_index("core")
    seq_index = lax.axis_index(seq)
    device = lax.axis_index(everyone)

    def swap(v, axis, n, k):
        return lax.ppermute(v, axis, [(i, i ^ k) for i in range(n)])

    def tree(parts):
        while len(parts) > 1:
            parts = [parts[i] + parts[i + 1] for i in range(0, len(parts), 2)]
        return parts[0]

    def sum_over(v, axis, n):
        return tree([v] + [swap(v, axis, n, k) for k in range(1, n)])

    soft_cond = jax.nn.silu(condition).astype(BF)
    partial_mods = product(soft_cond, modulation_weight)
    bias_width = modulation_bias.shape[0]
    bias_start = device * bias_width
    with_bias = (
        lax.dynamic_slice_in_dim(partial_mods, bias_start, bias_width, 1) + modulation_bias[None, :]
    )
    partial_mods = lax.dynamic_update_slice_in_dim(partial_mods, with_bias, bias_start, 1)
    mods_width = partial_mods.shape[1]
    gain_rows, gain_width = norm_gains.shape
    own_gains = lax.dynamic_update_slice_in_dim(
        jnp.zeros((gain_rows, WIDTH), F32), norm_gains.astype(F32), device * gain_width, 1
    ).reshape(1, -1)

    def message(item):
        return jnp.concatenate([lax.dynamic_slice_in_dim(partial_mods, item, 1, 0), own_gains], axis=1)

    head_vector = tree(
        [message(dp)] + [swap(message(dp ^ k), "dp", n_dp, k) for k in range(1, n_dp)]
    )
    head_vector = sum_over(sum_over(head_vector, "core", n_core), "z", n_z)
    mods = head_vector[:, :mods_width]
    gains = head_vector[0, mods_width:].reshape(gain_rows, WIDTH)
    shift_a, scale_a, gate_a, shift_f, scale_f, gate_f = [
        jnp.broadcast_to(mods[:, i * WIDTH : (i + 1) * WIDTH], (slots, WIDTH)) for i in range(6)
    ]

    joint_full, mixer_full, gate_up_full, down_full = (
        lax.all_gather(joint_weight, everyone, axis=0, tiled=True),
        lax.all_gather(mixer_weight, everyone, axis=0, tiled=True),
        lax.all_gather(gate_up_weight, everyone, axis=0, tiled=True),
        lax.all_gather(down_weight, everyone, axis=0, tiled=True),
    )

    flat_text = caption.reshape(-1, caption.shape[2])
    text_raw = lax.psum_scatter(
        product(flat_text, text_weight).astype(BF), everyone, scatter_dimension=0, tiled=True
    ).astype(F32)
    text_rows = text_raw.shape[0]
    text_keys, text_key_pull = jax.vjp(norm_rows, text_raw[:, :WIDTH], gains[6])

    def to_groups(parts):
        count = parts[0].shape[0]
        spread = []
        for part in parts:
            part = jnp.pad(part, ((0, 0), (0, spare * HEAD_DIM)))
            spread.append(part.reshape(count, n_seq, wide).transpose(1, 0, 2))
        return jnp.concatenate(spread, axis=2)

    def from_groups(grouped, which):
        part = grouped[:, :, which * wide : (which + 1) * wide].transpose(1, 0, 2)
        return part.reshape(part.shape[0], n_seq * wide)[:, :WIDTH]

    def exchange(v):
        return lax.all_to_all(v, seq, 0, 0, tiled=True)

    text_own = exchange(
        to_groups([text_keys.astype(BF), text_raw[:, WIDTH:].astype(BF)])
    ).reshape(n_seq * text_rows, 2 * wide)

    pad = ((0, slots - rows), (0, 0))
    xfloat = jnp.pad(tokens[0], pad).astype(F32)
    upstream = jnp.pad(cotangent[0], pad).astype(F32)
    normed_in, normed_pull = jax.vjp(modulate, xfloat, gains[0], scale_a, shift_a)
    normed_low = normed_in.astype(BF)
    joint = product(normed_low, joint_full)
    lane = jnp.arange(LANES)
    freq = jnp.exp((lane % (HEAD_DIM // 2)).astype(F32) * (-jnp.log(10000.0) / (HEAD_DIM // 2)))
    angle = (seq_index * rows + jnp.arange(slots)).astype(F32)[:, None] * freq[None, :]
    cosine = jnp.cos(angle)
    sine = jnp.sin(angle) * jnp.where(lane % HEAD_DIM < HEAD_DIM // 2, -1.0, 1.0)[None, :]
    rope_gains = gains[4:6]
    qkv = exchange(group_heads(joint, rope_gains, cosine, sine, heads, n_seq)).reshape(
        n_seq * slots, 3 * wide
    )
    place = jnp.arange(n_seq * slots)
    within = place % slots
    shape_row = image_shape[dp]
    valid = shape_row[0] * (shape_row[1] + 1)
    live = (within < rows) & ((place // slots) * rows + within < valid)
    bias = jnp.where(live, 0.0, NEG).astype(BF)[:, None]
    text_bias = jnp.where(jnp.arange(TEXT) < caption_len[dp], 0.0, NEG).astype(BF)[:, None]
    tanh_gates = jnp.tanh(head_gates)
    first_head = seq_index * heads
    own_gates = lax.dynamic_slice_in_dim(jnp.pad(tanh_gates, (0, spare)), first_head, heads, 0)
    gate_row = jnp.repeat(own_gates, HEAD_DIM)[None, :]
    attend_args = (qkv, text_own, bias, text_bias, gate_row)
    mixed_own, own_out, cross_out, lse = attend_forward(*attend_args, heads, 2 * slots)
    mixed = from_groups(exchange(mixed_own.reshape(n_seq, slots, wide)), 0)
    proj = product(mixed, mixer_full)
    branch_a, branch_a_pull = jax.vjp(branch_out, proj, gains[1], gate_a)
    hstate = xfloat + branch_a
    ffn_in, ffn_in_pull = jax.vjp(modulate, hstate, gains[2], scale_f, shift_f)
    ffn_low = ffn_in.astype(BF)
    gate_up = product(ffn_low, gate_up_full)
    hidden, swiglu_pull = jax.vjp(swiglu, gate_up)
    hidden_low = hidden.astype(BF)
    ffn = product(hidden_low, down_full)
    branch_f, branch_f_pull = jax.vjp(branch_out, ffn, gains[3], gate_f)
    output = (hstate + branch_f).astype(BF)[None, :rows]

    def weight_grad(left, right):
        half = right.shape[1] // n_core
        both_left = jnp.concatenate([left, swap(left, "core", n_core, 1)], axis=0)
        mine = lax.dynamic_slice_in_dim(right, core * half, half, 1)
        other = lax.dynamic_slice_in_dim(right, (1 - core) * half, half, 1)
        both_right = jnp.concatenate([mine, swap(other, "core", n_core, 1)], axis=0)
        part = contract(both_left, both_right, 0, 0).astype(BF)
        part = lax.psum_scatter(part, ("dp", "z"), scatter_dimension=0, tiled=True)
        count = part.shape[0] // n_core
        kept = lax.dynamic_slice_in_dim(part, core * count, count, 0)
        sent = lax.dynamic_slice_in_dim(part, (1 - core) * count, count, 0)
        received = swap(sent, "core", n_core, 1)
        first = jnp.where(core == 0, kept, received)
        second = jnp.where(core == 0, received, kept)
        return jnp.concatenate([first, second], axis=1).astype(F32)

    ffn_grad, gain3_grad, gate_f_grad = branch_f_pull(upstream)
    ffn_grad_low = ffn_grad.astype(BF)
    down_out = weight_grad(hidden_low, ffn_grad_low)
    (gate_up_grad_rows,) = swiglu_pull(contract(ffn_grad_low, down_full, 1, 1))
    gate_up_low = gate_up_grad_rows.astype(BF)
    gate_up_out = weight_grad(ffn_low, gate_up_low)
    state_part, gain2_grad, scale_f_grad, shift_f_grad = ffn_in_pull(
        contract(gate_up_low, gate_up_full, 1, 1)
    )
    state_grad = upstream + state_part
    proj_grad, gain1_grad, gate_a_grad = branch_a_pull(state_grad)
    proj_low = proj_grad.astype(BF)
    mixer_out = weight_grad(mixed, proj_low)
    mixed_grad = contract(proj_low, mixer_full, 1, 1).astype(BF)
    up_own = exchange(to_groups([mixed_grad])).reshape(n_seq * slots, wide)
    dq, dkv, dtext, dgate = attend_backward(
        *attend_args, up_own, own_out, cross_out, lse, heads, 2 * slots
    )
    grouped = exchange(jnp.concatenate([dq, dkv], axis=1).reshape(n_seq, slots, 3 * wide))
    joint_low, rope_gain_grads = ungroup_heads(grouped, joint, rope_gains, cosine, sine, heads)
    joint_out = weight_grad(normed_low, joint_low)
    input_part, gain0_grad, scale_a_grad, shift_a_grad = normed_pull(
        contract(joint_low, joint_full, 1, 1)
    )
    tokens_grad = (state_grad + input_part).astype(BF)[None, :rows]
    text_back = exchange(dtext.reshape(n_seq, text_rows, 2 * wide))
    text_key_grad, gain6_grad = text_key_pull(from_groups(text_back, 0).astype(F32))
    text_grad_rows = jnp.concatenate([text_key_grad.astype(BF), from_groups(text_back, 1)], axis=1)
    text_grad_all = lax.all_gather(text_grad_rows, everyone, axis=0, tiled=True)
    text_grad = contract(flat_text, text_grad_all, 0, 0)

    gates_own = jnp.sum(dgate.reshape(heads, HEAD_DIM), axis=1) * (1.0 - own_gates * own_gates)
    gates_all = lax.dynamic_update_slice_in_dim(
        jnp.zeros((HEADS + spare,), F32), gates_own, first_head, 0
    )
    pieces = [
        jnp.sum(value, axis=0)
        for value in (shift_a_grad, scale_a_grad, gate_a_grad, shift_f_grad, scale_f_grad, gate_f_grad)
    ]
    shared = [gain0_grad, gain1_grad, gain2_grad, gain3_grad, rope_gain_grads[0], rope_gain_grads[1], gain6_grad]
    tail = jnp.concatenate(pieces + shared + [gates_all])
    tail = sum_over(sum_over(tail, "core", n_core), "z", n_z)
    tails = [tail] + [swap(tail, "dp", n_dp, k) for k in range(1, n_dp)]
    total = tree([t[mods_width:] for t in tails])
    gates_grad = total[gain_rows * WIDTH : gain_rows * WIDTH + HEADS]
    gains_grad = lax.dynamic_slice_in_dim(
        total[: gain_rows * WIDTH].reshape(gain_rows, WIDTH), device * gain_width, gain_width, 1
    )
    mods_low = jnp.stack([t[:mods_width].astype(BF) for t in tails])
    cond_rows = jnp.concatenate(
        [lax.dynamic_slice_in_dim(soft_cond, dp ^ k, 1, 0) for k in range(n_dp)], axis=0
    )
    modulation_grad = contract(cond_rows, mods_low, 0, 0)
    bias_grad = lax.dynamic_slice_in_dim(
        jnp.sum(mods_low.astype(F32), axis=0), bias_start, bias_width, 0
    )
    return (
        output,
        tokens_grad,
        joint_out,
        mixer_out,
        gate_up_out,
        down_out,
        text_grad,
        modulation_grad,
        bias_grad,
        gains_grad,
        gates_grad,
    )


def solution(mesh):
    n_dp, n_seq = mesh.shape["dp"], mesh.shape["seq"]
    sizes = (n_dp, n_seq // 2, 2)
    split = Mesh(mesh.devices.reshape(sizes), ("dp", "z", "core"))
    seq, everyone = ("z", "core"), ("dp", "z", "core")
    token_spec, row_spec, column_spec = P("dp", seq, None), P(everyone, None), P(None, everyone)
    in_specs = (
        token_spec, column_spec, P(None, None, everyone), P(), P(), token_spec,
        row_spec, row_spec, row_spec, row_spec, row_spec, row_spec, P(everyone), column_spec, P(),
    )
    out_specs = (
        token_spec, token_spec, row_spec, row_spec, row_spec, row_spec, row_spec, row_spec,
        P(everyone), column_spec, P(),
    )
    return jax.shard_map(
        functools.partial(local, sizes), mesh=split, in_specs=in_specs, out_specs=out_specs, check_vma=False
    )
```

time: 3020 us -> 1430 us (0.47)
  waiting for transfers between devices: 1680 us -> 986 us
  matrix products: 602 us -> 127 us
  local copies, waits for them, and re-layouts: 336 us -> 39.1 us
  blocking collectives: 233 us -> 50.2 us
  Pallas kernels: 0 us -> 116 us
  other arithmetic: 113 us -> 48.3 us
  starting transfers between devices: 1.98 us -> 37.8 us
    reduce_scatter x6 -> x5, waiting for transfers between devices: 1210 us -> 467 us  [the longest x4 354 us: weight_grad(): part = lax.psum_scatter(part, ('dp', 'z'), scatter_dimension=0, tiled=True)]
    dot_general x94 -> x16, matrix products: 602 us -> 127 us  [the longest x10 84.9 us: contract(): lax.dot_general(left, right, (((left_dim,), (right_dim,)), ((), ())), pre...]
    unnamed x1 -> x0, blocking collectives: 147 us -> none
    all_to_all x0 -> x4, waiting for transfers between devices: none -> 137 us  [exchange(): return lax.all_to_all(v, seq, 0, 0, tiled=True)]
    psum x1 -> x0, waiting for transfers between devices: 122 us -> none  [local(): all_mods = lax.psum(partial_mods, ('dp', 'seq'))]
    pallas_call x0 -> x4, Pallas kernels: none -> 116 us  [the longest x1 70.3 us: attend_backward(): pl.pallas_call(functools.partial(attend_backward_kernel, heads), grid=(sl...]
    dynamic_slice x67 -> x15, local copies, waits for them, and re-layouts: 119 us -> 11.2 us  [the longest x4 5.17 us: weight_grad(): mine = lax.dynamic_slice_in_dim(right, core * half, half, 1)]
    convert_element_type x8 -> x2, local copies, waits for them, and re-layouts: 74.5 us -> 0.27 us  [local(): from_groups(text_back, 0).astype(F32)]
  transfers between devices with their start and end apart: 18 -> 40, of which waited for: 12 -> 29; matrix products, arithmetic and copies ran while one was open for 30% -> 14% of each run, Pallas kernels for 0% -> 8%
where the time goes in v1:
time: 1430 us; the launch traced here: 1420 us
  waiting for transfers between devices  986 us (69%)
  matrix products  127 us (9%)
  Pallas kernels  116 us (8%)
  blocking collectives  50.2 us (4%)
  other arithmetic  48.3 us (3%)
  local copies, waits for them, and re-layouts  39.1 us (3%)
  starting transfers between devices  37.8 us (3%)
  between operations  16.9 us (1%)
    reduce_scatter x4, waiting for transfers between devices, weight_grad(): part = lax.psum_scatter(part, ('dp', 'z'), scatter_dimension=0, tiled=True)  354 us
    all_to_all x4, waiting for transfers between devices, exchange(): return lax.all_to_all(v, seq, 0, 0, tiled=True)  137 us
    all_gather x1, waiting for transfers between devices, local(): lax.all_gather(gate_up_weight, everyone, axis=0, tiled=True)  127 us
    reduce_scatter x1, waiting for transfers between devices, local(): lax.psum_scatter(product(flat_text, text_weight).astype(BF), everyone, sc...  113 us
    dot_general x10, matrix products, contract(): lax.dot_general(left, right, (((left_dim,), (right_dim,)), ((), ())), pre...  84.9 us
    all_gather x1, waiting for transfers between devices, local(): lax.all_gather(down_weight, everyone, axis=0, tiled=True)  78.5 us
    all_gather x1, waiting for transfers between devices, local(): lax.all_gather(joint_weight, everyone, axis=0, tiled=True)  77.5 us
    pallas_call x1, Pallas kernels, attend_backward(): pl.pallas_call(functools.partial(attend_backward_kernel, heads), grid=(sl...  70.3 us
  transfers between devices with their start and end apart: 40, of which 29 were waited for; matrix products, arithmetic and copies ran while one was open for 14% of the time, Pallas kernels for 8%

profile of v1, /device:TPU:0, one launch (start us, length us, event | category | flops | bytes accessed | tf_op | source)
XLA Modules:
  0.0 1421.3 jit_solution(17165614516347621885)
XLA Ops:
  8.3 5.3 convolution_convert_fusion.3
  33.7 5.1 collective-permute-done.4
  44.7 77.5 %all-gather.6.cloned.1.call-done = bf16[1536,4608]{1,0:T(8,128)(2,1)} async-done(((bf16[48,4608]{1,0:T(8,128)(2,1)}), bf16[1536,4608]{1,0:T(8,128)(2,1)}) %all-gather.6.cloned.1.call-update) | async-done | bytes 14155792 | tf_op jit(solution)/shard_map/all_gather | solution.py:418
  122.2 11.3 fusion.90.joint_ref
  133.5 6.3 group_heads.1
  139.8 4.6 all-to-all-start
  149.5 112.9 %reduce-scatter.6.cloned.1.call-done = bf16[32,3072]{1,0:T(8,128)(2,1)} async-done(((bf16[1024,3072]{1,0:T(8,128)(2,1)}), bf16[32,3072]{1,0:T(8,128)(2,1)}) %reduce-scatter.6.cloned.1.call-update) | async-done | bytes 196624 | tf_op jit(solution)/shard_map/reduce_scatter | solution.py:425
  274.7 5.0 all-to-all-done.1
  280.5 33.1 %attend_forward.1 = (bf16[2432,192]{1,0:T(8,128)(2,1)}, f32[2432,192]{1,0:T(8,128)}, f32[2432,192]{1,0:T(8,128)}, f32[2432,6]{1,0:T(8,128)}) custom-call(bf16[2432,576]{1,0:T(8,128)(2,1)} %bitcast.1.qkv_ref, bf16[256,384]{1,0:T(8,128)(2,1)} %bitcast.76, bf16[2432,1]{1,0:T(8,128)(2,1)} %select_convert_fusion.bias_ref, ...), custom_call_target="tpu_custom_call" | custom-call | flops 20082327552 | bytes 8404992 | tf_op jit(solution)/shard_map/attend_forward/pallas_call | solution.py:181
  319.8 37.0 %all-to-all-done.2 = bf16[8,304,192]{1,2,0:T(8,128)(2,1)S(1)} async-done(((bf16[8,304,192]{1,2,0:T(8,128)(2,1)}), bf16[8,304,192]{1,2,0:T(8,128)(2,1)S(1)}, u32[]{:S(2)}, u32[]{:S(2)}) %all-to-all-start.2) | async-done | bytes 933920 | tf_op jit(solution)/shard_map/all_to_all | solution.py:444
  367.0 127.1 %all-gather.10.cloned.1.call-done = bf16[1536,8192]{1,0:T(8,128)(2,1)} async-done(((bf16[48,8192]{1,0:T(8,128)(2,1)}), bf16[1536,8192]{1,0:T(8,128)(2,1)}) %all-gather.10.cloned.1.call-update) | async-done | bytes 25165840 | tf_op jit(solution)/shard_map/all_gather | solution.py:420
  494.0 12.8 fusion.91
  513.1 78.5 %all-gather.12.cloned.1.call-done = bf16[4096,1536]{1,0:T(8,128)(2,1)} async-done(((bf16[128,1536]{1,0:T(8,128)(2,1)}), bf16[4096,1536]{1,0:T(8,128)(2,1)}) %all-gather.12.cloned.1.call-update) | async-done | bytes 12582928 | tf_op jit(solution)/shard_map/all_gather | solution.py:421
  591.6 8.0 multiply_reduce_fusion.9
  603.1 13.1 fusion.52
  616.3 6.8 add_convert_fusion
  623.1 15.9 %multiply_reduce_fusion = (f32[1536]{0:T(1024)S(1)}, f32[304]{0:T(512)S(1)}, f32[1536]{0:T(1024)S(1)}, f32[1536]{0:T(1024)S(1)}, f32[304,1536]{1,0:T(8,128)}) fusion(f32[304,1536]{1,0:T(8,128)} %copy-done.2, f32[1536]{0:T(1024)S(1)} %get-tuple-element.94, f32[304]{0:T(512)S(1)} %fusion.69, f32[1536]{0:T(1024)S(1)} %get-tuple-element.95, ...), kind=kOutput, calls=%fused_computation.49 | convolution fusion | flops 7655541760 | bytes 33915264 | tf_op jit(solution)/shard_map/dot_general | solution.py:46
  646.7 4.9 convolution_convert_fusion.4
  657.1 9.1 convolution_convert_fusion.2
  673.6 38.4 %all_to_all.30 = bf16[8,304,192]{1,2,0:T(8,128)(2,1)S(1)} all-to-all(bf16[8,304,192]{1,2,0:T(8,128)(2,1)S(1)} %copy.52), channel_id=1, replica_groups=mesh['dp'=4,'z'=4,'core'=2] {'z','core'}, dimensions={0} | all-to-all | bytes 1867776 | tf_op jit(solution)/shard_map/all_to_all | solution.py:444
  713.6 70.3 %attend_backward.1 = (bf16[2432,192]{1,0:T(8,128)(2,1)}, bf16[2432,384]{1,0:T(8,128)(2,1)}, bf16[256,384]{1,0:T(8,128)(2,1)}, f32[1,192]{1,0:T(1,128)}) custom-call(bf16[2432,576]{1,0:T(8,128)(2,1)} %bitcast.1.qkv_ref, bf16[256,384]{1,0:T(8,128)(2,1)} %bitcast.77, bf16[2432,1]{1,0:T(8,128)(2,1)} %select_convert_fusion.bias_ref, ...), custom_call_target="tpu_custom_call" | custom-call | flops 50205818880 | bytes 12140544 | tf_op jit(solution)/shard_map/attend_backward/pallas_call | solution.py:208
  783.9 11.8 all_to_all.31
  806.2 95.4 %all-to-all-done.4.grad_ref = bf16[8,304,576]{2,1,0:T(8,128)(2,1)} async-done(((bf16[8,304,576]{2,1,0:T(8,128)(2,1)}), bf16[8,304,576]{2,1,0:T(8,128)(2,1)}, u32[]{:S(2)}, u32[]{:S(2)}) %all-to-all-start.4) | async-done | bytes 2801696 | tf_op jit(solution)/shard_map/all_to_all | solution.py:444
  901.6 6.6 ungroup_heads.1
  914.8 7.7 convolution_convert_fusion.1
  926.2 5.5 collective-permute-done.13
  931.8 12.7 convolution_convert_fusion
  955.2 11.5 multiply_reduce_fusion.2
  991.1 55.5 %all-gather.14.cloned.1.call-done = bf16[1024,3072]{1,0:T(8,128)(2,1)} async-done(((bf16[32,3072]{1,0:T(8,128)(2,1)}), bf16[1024,3072]{1,0:T(8,128)(2,1)}) %all-gather.14.cloned.1.call-update) | async-done | bytes 6291472 | tf_op jit(solution)/shard_map/all_gather | solution.py:535
  1046.5 4.6 convolution_bitcast_fusion
  1052.9 148.8 %reduce-scatter.8.cloned.1.call-done = bf16[96,2304]{1,0:T(8,128)(2,1)} async-done(((bf16[1536,2304]{1,0:T(8,128)(2,1)}), bf16[96,2304]{1,0:T(8,128)(2,1)}) %reduce-scatter.8.cloned.1.call-update) | async-done | bytes 442384 | tf_op jit(solution)/shard_map/reduce_scatter | solution.py:498
  1205.2 204.8 %reduce-scatter.12.cloned.1.call-done = bf16[96,4096]{1,0:T(8,128)(2,1)} async-done(((bf16[1536,4096]{1,0:T(8,128)(2,1)}), bf16[96,4096]{1,0:T(8,128)(2,1)}) %reduce-scatter.12.cloned.1.call-update) | async-done | bytes 786448 | tf_op jit(solution)/shard_map/reduce_scatter | solution.py:498
  (318 shorter events, 156.4 us)
Async XLA Ops:
  7.2 115.0 %all-gather.6.cloned.1.call-start = ((), (), s32[]{:S(2)}) async-start(), calls=%async_computation.11 | async-start | bytes 14598144 | tf_op jit(solution)/shard_map/all_gather | solution.py:418
  7.9 254.5 %reduce-scatter.6.cloned.1.call-start = ((), (), s32[]{:S(2)}) async-start(), calls=%async_computation.12 | async-start | bytes 6488064 | tf_op jit(solution)/shard_map/reduce_scatter | solution.py:425
  13.7 344.5 %all-gather.8.cloned.1.call-start = ((), (), s32[]{:S(2)}) async-start(), calls=%async_computation.13 | async-start | bytes 4866048 | tf_op jit(solution)/shard_map/all_gather | solution.py:419
  14.4 479.6 %all-gather.10.cloned.1.call-start = ((), (), s32[]{:S(2)}) async-start(), calls=%async_computation.14 | async-start | bytes 25952256 | tf_op jit(solution)/shard_map/all_gather | solution.py:420
  15.0 576.6 %all-gather.12.cloned.1.call-start = ((), (), s32[]{:S(2)}) async-start(), calls=%async_computation.15 | async-start | bytes 12976128 | tf_op jit(solution)/shard_map/all_gather | solution.py:421
  16.3 5.6 collective-permute-start
  19.3 5.6 collective-permute-start.1
  20.8 5.5 collective-permute-start.2
  28.3 10.5 collective-permute-start.4
  30.9 10.2 collective-permute-start.5
  33.7 9.6 collective-permute-start.6
  139.8 126.7 %all-to-all-start = ((bf16[8,304,576]{2,1,0:T(8,128)(2,1)}), bf16[8,304,576]{2,1,0:T(8,128)(2,1)}, u32[]{:S(2)}, u32[]{:S(2)}) async-start(bf16[8,304,576]{2,1,0:T(8,128)(2,1)} %group_heads.1), calls=%async_computation | async-start | bytes 6225920 | tf_op jit(solution)/shard_map/all_to_all | solution.py:444
  266.5 13.2 all-to-all-start.1
  316.0 40.8 %all-to-all-start.2 = ((bf16[8,304,192]{1,2,0:T(8,128)(2,1)}), bf16[8,304,192]{1,2,0:T(8,128)(2,1)S(1)}, u32[]{:S(2)}, u32[]{:S(2)}) async-start(bf16[8,304,192]{1,2,0:T(8,128)(2,1)} %copy.50), calls=%async_computation.3 | async-start | bytes 2359296 | tf_op jit(solution)/shard_map/all_to_all | solution.py:444
  319.6 632.5 %reduce-scatter.10.cloned.1.call-start = ((), (), s32[]{:S(2)}) async-start(), calls=%async_computation.17 | async-start | bytes 2506752 | tf_op jit(solution)/shard_map/reduce_scatter | solution.py:498
  358.2 286.9 %collective-permute-start.10 = (bf16[304,1536]{1,0:T(8,128)(2,1)}, bf16[304,1536]{1,0:T(8,128)(2,1)}, u32[]{:S(2)}, u32[]{:S(2)}) collective-permute-start(bf16[304,1536]{1,0:T(8,128)(2,1)} %copy.57), channel_id=1, source_target_pairs={{0,1},{1,0},{2,3},{3,2},{4,5},{5,4},{6,7},{7,6},{8,9},{9,8},{10,11... | collective-permute-start | bytes 2801672 | tf_op jit(solution)/shard_map/ppermute | solution.py:380
  651.6 338.4 %reduce-scatter.14.cloned.1.call-start = ((), (), s32[]{:S(2)}) async-start(), calls=%async_computation.19 | async-start | bytes 6684672 | tf_op jit(solution)/shard_map/reduce_scatter | solution.py:498
  651.7 5.5 collective-permute-start.16
  666.2 380.3 %all-gather.14.cloned.1.call-start = ((), (), s32[]{:S(2)}) async-start(), calls=%async_computation.20 | async-start | bytes 6488064 | tf_op jit(solution)/shard_map/all_gather | solution.py:535
  801.7 99.9 %all-to-all-start.4 = ((bf16[8,304,576]{2,1,0:T(8,128)(2,1)}), bf16[8,304,576]{2,1,0:T(8,128)(2,1)}, u32[]{:S(2)}, u32[]{:S(2)}) async-start(bf16[8,304,576]{2,1,0:T(8,128)(2,1)} %bitcast.65), calls=%async_computation.5 | async-start | bytes 6225920 | tf_op jit(solution)/shard_map/all_to_all | solution.py:444
  806.2 395.5 %reduce-scatter.8.cloned.1.call-start = ((), (), s32[]{:S(2)}) async-start(), calls=%async_computation.16 | async-start | bytes 7520256 | tf_op jit(solution)/shard_map/reduce_scatter | solution.py:498
  910.2 4.6 collective-permute-start.8
  922.6 487.4 %reduce-scatter.12.cloned.1.call-start = ((), (), s32[]{:S(2)}) async-start(), calls=%async_computation.18 | async-start | bytes 13369344 | tf_op jit(solution)/shard_map/reduce_scatter | solution.py:498
  925.7 6.1 collective-permute-start.14
  925.8 6.0 collective-permute-start.13
  968.3 6.4 collective-permute-start.20
  968.4 9.9 collective-permute-start.21
  970.6 7.7 collective-permute-start.22
  978.3 5.3 collective-permute-start.23
  979.8 5.1 collective-permute-start.24
  981.1 5.3 collective-permute-start.25
  991.0 61.8 %collective-permute-start.18 = (bf16[128,768]{1,0:T(8,128)(2,1)S(1)}, bf16[128,768]{1,0:T(8,128)(2,1)S(1)}, u32[]{:S(2)}, u32[]{:S(2)}) collective-permute-start(bf16[128,768]{1,0:T(8,128)(2,1)S(1)} %constant_dynamic-slice_fusion.5), channel_id=1, source_target_pairs={{0,1},{1,0},{2,3},{3,2},{4,5},{5,4},{6,7},{7,6},{8,9},{9,8},{10,11... | collective-permute-start | bytes 589832 | tf_op jit(solution)/shard_map/ppermute | solution.py:380
  (63 other events, 1659.7 us)
Sparse Core Ops, SparseCore 0:
  11.0 111.0 all-gather.5
  127.8 134.6 reduce-scatter.5
  265.9 68.3 all-gather.7
  337.6 156.3 all-gather.9
  497.3 94.2 all-gather.11
  651.8 131.3 reduce-scatter.9
  788.4 185.1 reduce-scatter.13
  977.2 69.2 all-gather.13
  1051.9 149.7 reduce-scatter.7
  1207.2 202.7 reduce-scatter.11

commit v2 on v1

v2 whole, which is shorter than its diff:
```python
import functools

import jax
import jax.numpy as jnp
from jax import lax
from jax.experimental import pallas as pl
from jax.experimental.pallas import tpu as pltpu
from jax.sharding import Mesh
from jax.sharding import PartitionSpec as P

HEADS = 24
HEAD_DIM = 64
TEXT = 256
WIDTH = HEADS * HEAD_DIM
EPS = 1e-06
NEG = -1e30
SCALE = float(HEAD_DIM) ** (-0.5)
LANES = 128
BF = jnp.bfloat16
F32 = jnp.float32
VMEM_BYTES = 56 << 20


def norm_rows(v, gain):
    return v * lax.rsqrt(jnp.mean(v * v, axis=-1, keepdims=True) + EPS) * gain


def modulate(v, gain, scale, shift):
    return norm_rows(v, gain) * (1.0 + scale) + shift


def branch_out(v, gain, gate):
    return gate * norm_rows(v, gain)


def swiglu(gate_up):
    half = gate_up.shape[-1] // 2
    return jax.nn.silu(gate_up[:, :half]) * gate_up[:, half:]


def product(left, right):
    return jnp.dot(left, right, preferred_element_type=F32)


def contract(left, right, left_dim, right_dim):
    return lax.dot_general(
        left, right, (((left_dim,), (right_dim,)), ((), ())), preferred_element_type=F32
    )


def split3(v):
    high = v.astype(BF)
    rest = v - high.astype(F32)
    mid = rest.astype(BF)
    return [high, mid, (rest - mid.astype(F32)).astype(BF)]


def extend(block, columns):
    rows = block.shape[0]
    fill = HEAD_DIM - len(columns)
    return jnp.concatenate([block] + list(columns) + [jnp.zeros((rows, fill), BF)], axis=1)


def unfold(v, start, period):
    return jnp.concatenate(
        [v[:, start : start + HEAD_DIM], v[:, period + start : period + start + HEAD_DIM]], axis=0
    )


def fold(parts):
    rows = parts[0].shape[0] // 2
    return jnp.concatenate([p[:rows] for p in parts] + [p[rows:] for p in parts], axis=1)


def spread_keys(index, qkv_ref, text_ref, bias_ref, text_bias_ref, outs, key_ones, value_ones):
    wide = text_ref.shape[1] // 2
    at = index * HEAD_DIM
    sources = (
        (unfold(qkv_ref, HEAD_DIM, 3 * HEAD_DIM), unfold(qkv_ref, 2 * HEAD_DIM, 3 * HEAD_DIM), bias_ref),
        (text_ref[:, at : at + HEAD_DIM], text_ref[:, wide + at : wide + at + HEAD_DIM], text_bias_ref),
    )
    for i, (keys, values, bias) in enumerate(sources):
        one = jnp.ones((keys.shape[0], 1), BF)
        outs[2 * i][...] = extend(keys, [bias[...]] + [one] * key_ones)
        outs[2 * i + 1][...] = extend(values, [one] * value_ones)


def attend_forward_kernel(
    index, qkv_ref, text_ref, bias_ref, text_bias_ref, gate_ref, q_ref,
    mixed_ref, own_ref, cross_ref, lse_ref, *spread
):
    @pl.when(pl.program_id(0) == 0)
    def _():
        spread_keys(index, qkv_ref, text_ref, bias_ref, text_bias_ref, spread, 0, 1)

    query = unfold(q_ref, 0, 3 * HEAD_DIM) * SCALE
    query = extend(query, [jnp.ones((query.shape[0], 1), BF)])

    def soft(keys, values):
        scores = contract(query, keys[...], 1, 1)
        high = jnp.max(scores, axis=1, keepdims=True)
        total = contract(jnp.exp(scores - high).astype(BF), values[...], 1, 0)
        mass = total[:, HEAD_DIM : HEAD_DIM + 1]
        return total[:, :HEAD_DIM] / mass, high + jnp.log(mass)

    own, own_lse = soft(spread[0], spread[1])
    cross, cross_lse = soft(spread[2], spread[3])
    own_ref[...] = fold([own])
    cross_ref[...] = fold([cross])
    mixed_ref[...] = fold([own + gate_ref[...] * cross]).astype(BF)
    lse_ref[...] = fold([own_lse, cross_lse])


def attend_backward_kernel(
    index, qkv_ref, text_ref, bias_ref, text_bias_ref, gate_ref, q_ref, up_ref, own_ref, cross_ref, lse_ref,
    grad_ref, dtext_ref, dgate_ref, *scratch
):
    spread, sums = scratch[:4], scratch[4:]
    step = pl.program_id(0)

    @pl.when(step == 0)
    def _():
        spread_keys(index, qkv_ref, text_ref, bias_ref, text_bias_ref, spread, 3, 3)
        for ref in sums + (dgate_ref,):
            ref[...] = jnp.zeros_like(ref)

    query = unfold(q_ref, 0, 3 * HEAD_DIM)
    one = jnp.ones((query.shape[0], 1), BF)
    up = unfold(up_ref, 0, HEAD_DIM)
    cross = unfold(cross_ref, 0, HEAD_DIM)
    up_float = up.astype(F32)
    up_cross = (gate_ref[...] * up_float).astype(BF)
    dgate_ref[...] += jnp.sum(up_float * cross, axis=0, keepdims=True)
    half = lse_ref.shape[0]
    lse = jnp.concatenate([lse_ref[:, 0:2], lse_ref[:, 2:4]], axis=0)

    def one_soft(upstream, row, spread_lse, keys, values, key_sum, value_sum):
        center = jnp.sum(row, axis=1, keepdims=True)
        left = extend(query * SCALE, [one] + [-part for part in split3(spread_lse)])
        weights = jnp.exp(contract(left, keys[...], 1, 1))
        left = extend(upstream, [-part for part in split3(center)])
        score_grad = (weights * contract(left, values[...], 1, 1)).astype(BF)
        weights = weights.astype(BF)
        key_sum[...] += contract(score_grad, query, 0, 0)
        value_sum[...] += contract(weights, upstream, 0, 0)
        return contract(score_grad, keys[...], 1, 0)[:, :HEAD_DIM]

    dq = one_soft(
        up, up_float * unfold(own_ref, 0, HEAD_DIM), lse[:, 0:1], spread[0], spread[1], sums[0], sums[1]
    )
    dq += one_soft(
        up_cross, up_cross.astype(F32) * cross, lse[:, 1:2], spread[2], spread[3], sums[2], sums[3]
    )
    dq = (dq * SCALE).astype(BF)
    here = pl.ds(pl.multiple_of(step * half, half), half)
    grad_ref[here, 0:HEAD_DIM] = dq[:half]
    grad_ref[here, 3 * HEAD_DIM : 4 * HEAD_DIM] = dq[half:]

    @pl.when(step == pl.num_programs(0) - 1)
    def _():
        slots = grad_ref.shape[0]
        both = jnp.concatenate([sums[0][...] * SCALE, sums[1][...]], axis=1).astype(BF)
        grad_ref[:, HEAD_DIM : 3 * HEAD_DIM] = both[:slots]
        grad_ref[:, 4 * HEAD_DIM :] = both[slots:]
        dtext_ref[...] = jnp.concatenate([sums[2][...] * SCALE, sums[3][...]], axis=1).astype(BF)


def whole_block(shape):
    return pl.BlockSpec(shape, lambda i: (0,) * len(shape), pipeline_mode=pl.Buffered(1))


def row_block(rows, columns):
    return pl.BlockSpec((rows, columns), lambda i: (i, 0))


def params():
    return pltpu.CompilerParams(vmem_limit_bytes=VMEM_BYTES)


def cost(flops, size, exps=0):
    return pl.CostEstimate(flops=int(flops), bytes_accessed=int(size), transcendentals=int(exps))


def attend_forward(qkv, text, bias, text_bias, gate, index, rows):
    half, words, head = qkv.shape[0], text.shape[0], HEAD_DIM
    slots = 2 * half
    pairs = slots * (slots + words)
    return pl.pallas_call(
        functools.partial(attend_forward_kernel, index),
        grid=(half // rows,),
        in_specs=[
            whole_block((half, 6 * head)), whole_block(text.shape), whole_block((slots, 1)),
            whole_block((words, 1)), whole_block((1, head)), row_block(rows, 6 * head),
        ],
        out_specs=[row_block(rows, 2 * head)] * 3 + [row_block(rows, 4)],
        out_shape=[
            jax.ShapeDtypeStruct((half, 2 * head), BF),
            jax.ShapeDtypeStruct((half, 2 * head), F32),
            jax.ShapeDtypeStruct((half, 2 * head), F32),
            jax.ShapeDtypeStruct((half, 4), F32),
        ],
        scratch_shapes=[pltpu.VMEM((n, 2 * head), BF) for n in (slots, slots, words, words)],
        compiler_params=params(),
        cost_estimate=cost(pairs * head * 16, slots * head * 18, pairs),
        name="attend_forward",
    )(qkv, text, bias, text_bias, gate, qkv)


def attend_backward(qkv, text, bias, text_bias, gate, up, own, cross, lse, index, rows):
    half, words, head = qkv.shape[0], text.shape[0], HEAD_DIM
    slots = 2 * half
    pairs = slots * (slots + words)
    return pl.pallas_call(
        functools.partial(attend_backward_kernel, index),
        grid=(half // rows,),
        in_specs=[
            whole_block((half, 6 * head)), whole_block(text.shape), whole_block((slots, 1)),
            whole_block((words, 1)), whole_block((1, head)), row_block(rows, 6 * head),
            row_block(rows, 2 * head), row_block(rows, 2 * head), row_block(rows, 2 * head), row_block(rows, 4),
        ],
        out_specs=[whole_block((half, 6 * head)), whole_block((words, 2 * head)), whole_block((1, head))],
        out_shape=[
            jax.ShapeDtypeStruct((half, 6 * head), BF),
            jax.ShapeDtypeStruct((words, 2 * head), BF),
            jax.ShapeDtypeStruct((1, head), F32),
        ],
        scratch_shapes=[pltpu.VMEM((n, 2 * head), BF) for n in (slots, slots, words, words)]
        + [pltpu.VMEM((n, head), F32) for n in (slots, slots, words, words)],
        compiler_params=params(),
        cost_estimate=cost(pairs * head * 40, slots * head * 26, pairs),
        name="attend_backward",
    )(qkv, text, bias, text_bias, gate, qkv, up, own, cross, lse)


def swap_halves(v):
    lane = lax.broadcasted_iota(jnp.int32, v.shape, 1)
    half = HEAD_DIM // 2
    return jnp.where(
        lane % HEAD_DIM < half, pltpu.roll(v, LANES - half, 1), pltpu.roll(v, half, 1)
    )


def tiles_of(v):
    return [v[:, t : t + LANES] for t in range(0, v.shape[1], LANES)]


def split_heads(parts, out_refs):
    heads, groups = len(out_refs), out_refs[0].shape[0]
    rows = parts[0].shape[0]
    for g in range(groups):
        for i in range(heads):
            at = (g * heads + i) * HEAD_DIM
            if at < WIDTH:
                out_refs[i][g] = fold([part[:, at : at + HEAD_DIM] for part in parts])
            else:
                out_refs[i][g] = jnp.zeros(out_refs[i].shape[1:], out_refs[i].dtype)


def join_heads(refs, which, count):
    groups, columns = refs[0].shape[0], []
    for g in range(groups):
        for i, ref in enumerate(refs):
            if (g * len(refs) + i) * HEAD_DIM < WIDTH:
                columns.append(unfold(ref.at[g], which * HEAD_DIM, count * HEAD_DIM))
    return jnp.concatenate(columns, axis=1)


def group_kernel(joint_ref, gains_ref, cos_ref, sin_ref, *out_refs):
    cosine, sine = cos_ref[...], sin_ref[...]
    parts = []
    for which in range(2):
        raw = joint_ref[:, which * WIDTH : (which + 1) * WIDTH]
        root = lax.rsqrt(jnp.mean(raw * raw, axis=1, keepdims=True) + EPS)
        scaled = raw * root * gains_ref[which : which + 1, :]
        turned = [tile * cosine + swap_halves(tile) * sine for tile in tiles_of(scaled)]
        parts.append(jnp.concatenate(turned, axis=1).astype(BF))
    parts.append(joint_ref[:, 2 * WIDTH :].astype(BF))
    split_heads(parts, out_refs)


def ungroup_kernel(heads, *refs):
    grad_refs = refs[:heads]
    joint_ref, gains_ref, cos_ref, sin_ref, out_ref, dgain_ref = refs[heads:]
    cosine, sine = cos_ref[...], sin_ref[...]
    for which in range(2):
        cut = slice(which * WIDTH, (which + 1) * WIDTH)
        grad = join_heads(grad_refs, which, 3).astype(F32)
        turned = [tile * cosine - swap_halves(tile) * sine for tile in tiles_of(grad)]
        grad = jnp.concatenate(turned, axis=1)
        raw = joint_ref[:, cut]
        root = lax.rsqrt(jnp.mean(raw * raw, axis=1, keepdims=True) + EPS)
        unit = raw * root
        dgain_ref[which : which + 1, :] = jnp.sum(grad * unit, axis=0, keepdims=True)
        grad = grad * gains_ref[which : which + 1, :]
        grad = root * (grad - unit * jnp.mean(grad * unit, axis=1, keepdims=True))
        out_ref[:, cut] = grad.astype(BF)
    out_ref[:, 2 * WIDTH :] = join_heads(grad_refs, 2, 3)


def split_kernel(value_ref, *out_refs):
    split_heads([value_ref[...]], out_refs)


def join_kernel(*refs):
    refs[-1][...] = join_heads(refs[:-1], 0, 1)


def pack_kernel(*refs):
    out_ref = refs[-1]
    rows = [ref[...] for ref in refs[:-1]]
    rows.append(jnp.zeros((out_ref.shape[0] - len(rows), out_ref.shape[1]), F32))
    out_ref[...] = jnp.concatenate(rows, axis=0)


def simple_call(kernel, out_shape, name, *args):
    size = sum(a.size * a.dtype.itemsize for a in args)
    shapes = out_shape if isinstance(out_shape, list) else [out_shape]
    return pl.pallas_call(
        kernel,
        in_specs=[pl.BlockSpec(memory_space=pltpu.VMEM)] * len(args),
        out_specs=jax.tree.map(lambda _: pl.BlockSpec(memory_space=pltpu.VMEM), out_shape),
        out_shape=out_shape,
        compiler_params=params(),
        cost_estimate=cost(size * 8, size + sum(o.size * o.dtype.itemsize for o in shapes)),
        name=name,
    )(*args)


def local(
    sizes,
    tokens,
    condition,
    caption,
    caption_len,
    image_shape,
    cotangent,
    joint_weight,
    mixer_weight,
    gate_up_weight,
    down_weight,
    text_weight,
    modulation_weight,
    modulation_bias,
    norm_gains,
    head_gates,
):
    n_dp, n_z, n_core = sizes
    everyone = ("dp", "z", "core")
    seq = ("z", "core")
    n_seq = n_z * n_core
    heads = -(-HEADS // n_seq)
    wide = heads * HEAD_DIM
    spare = n_seq * heads - HEADS
    rows = tokens.shape[1]
    slots = -(-rows // 16) * 16
    dp = lax.axis_index("dp")
    core = lax.axis_index("core")
    z_index = lax.axis_index("z")
    seq_index = lax.axis_index(seq)
    device = lax.axis_index(everyone)

    def swap(v, axis, n, k):
        return lax.ppermute(v, axis, [(i, i ^ k) for i in range(n)])

    def tree(parts):
        while len(parts) > 1:
            parts = [parts[i] + parts[i + 1] for i in range(0, len(parts), 2)]
        return parts[0]

    def sum_over(v, axis, n):
        return tree([v] + [swap(v, axis, n, k) for k in range(1, n)])

    soft_cond = jax.nn.silu(condition).astype(BF)
    partial_mods = product(soft_cond, modulation_weight)
    bias_width = modulation_bias.shape[0]
    bias_start = device * bias_width
    with_bias = (
        lax.dynamic_slice_in_dim(partial_mods, bias_start, bias_width, 1) + modulation_bias[None, :]
    )
    partial_mods = lax.dynamic_update_slice_in_dim(partial_mods, with_bias, bias_start, 1)
    mods_width = partial_mods.shape[1]
    gain_rows, gain_width = norm_gains.shape
    own_gains = lax.dynamic_update_slice_in_dim(
        jnp.zeros((gain_rows, WIDTH), F32), norm_gains.astype(F32), device * gain_width, 1
    ).reshape(1, -1)

    def after(v, *others):
        return lax.optimization_barrier((v,) + others)[0]

    def shift_z(v, k):
        return lax.ppermute(v, "z", [(i, (i + k) % n_z) for i in range(n_z)])

    def place(full, part, index):
        return lax.dynamic_update_slice(full, part[None], (index,) + (0,) * part.ndim)


    def gather_line(shard):
        parts = [shift_z(shard, k) for k in range(1, n_z)]

        def arrive(*before):
            line = place(jnp.zeros((n_z,) + shard.shape, shard.dtype), shard, z_index)
            for k, part in enumerate(parts, 1):
                line = place(line, after(part, *before), (z_index - k) % n_z)
            return line.reshape(-1, shard.shape[1])

        return arrive

    def gather_dp(line):
        return lax.all_gather(line, "dp", axis=0, tiled=True)

    def gather_all(shard):
        if n_dp != 4:
            full = lax.all_gather(shard, everyone, axis=0, tiled=True)
            return lambda *before: lambda *before: full
        chunk, columns = shard.shape
        line_arrive = gather_line(shard)

        def first(*before):
            line = line_arrive(*before)
            empty = jnp.zeros((n_dp, n_z, n_core, chunk, columns), shard.dtype)
            line, empty = lax.optimization_barrier((line, empty))
            near = [swap(line, "dp", n_dp, k) for k in (1, 2)]

            def second(*before):
                half = line.shape[0] // 2
                by_x, by_y = [after(v, *before) for v in near]
                far = (swap(by_y[:half], "dp", n_dp, 1), swap(by_x[half:], "dp", n_dp, 2))
                full = empty
                parts = [(line, dp, 0), (by_x, dp ^ 1, 0), (by_y, dp ^ 2, 0)]
                parts += [(far[0], dp ^ 3, 0), (far[1], dp ^ 3, n_z // 2)]
                for part, index, start in parts:
                    for held, of_core in ((part, core), (swap(part, "core", n_core, 1), 1 - core)):
                        held = held.reshape(1, -1, 1, chunk, columns)
                        full = lax.dynamic_update_slice(full, held, (index, start, of_core, 0, 0))
                return full.reshape(-1, columns)

            second.line = line
            return second

        return first

    def reduce_dp(part):
        return lax.psum_scatter(part, "dp", scatter_dimension=0, tiled=True)

    def reduce_line(part):
        line = part.reshape(n_z, -1, part.shape[1])

        def at(index):
            return lax.dynamic_index_in_dim(line, index, 0, keepdims=False)

        others = [shift_z(at((z_index + k) % n_z), k) for k in range(1, n_z)]

        def arrive(*before):
            parts = [at(z_index)] + [after(other, *before) for other in others]
            return tree([v.astype(F32) for v in parts])

        return arrive

    def by_core(mine, other, axis):
        first = jnp.where(core == 0, mine, other)
        second = jnp.where(core == 0, other, mine)
        return jnp.concatenate([first, second], axis=axis)

    def column_split(left, right):
        half = right.shape[1] // n_core
        mine = lax.dynamic_slice_in_dim(right, core * half, half, 1)
        other = lax.dynamic_slice_in_dim(right, (1 - core) * half, half, 1)
        both_right = jnp.concatenate([mine, swap(other, "core", n_core, 1)], axis=0)
        return both_cores(left), both_right

    def both_cores(v):
        return jnp.concatenate([v, swap(v, "core", n_core, 1)], axis=0)

    def sum_cores(v, *before):
        return v[:slots] + after(swap(v[slots:], "core", n_core, 1), *before)

    def own_rows(part):
        return by_core(*trade(part.astype(BF)), 1).astype(F32)

    def core_columns(shard):
        half = shard.shape[1] // n_core
        mine = lax.dynamic_slice_in_dim(shard, core * half, half, 1)
        other = lax.dynamic_slice_in_dim(shard, (1 - core) * half, half, 1)
        return by_core(mine, swap(other, "core", n_core, 1), 0)

    def grad_of(left, right):
        return contract(left, right, 0, 0).astype(BF)

    def trade(part):
        count = part.shape[0] // n_core
        kept = lax.dynamic_slice_in_dim(part, core * count, count, 0)
        sent = lax.dynamic_slice_in_dim(part, (1 - core) * count, count, 0)
        return kept, swap(sent, "core", n_core, 1)

    flat_text = caption.reshape(-1, caption.shape[2])
    text_left, text_right = column_split(flat_text.T, text_weight)
    def halve(v):
        count = n_dp
        while count > 1:
            count //= 2
            bit = (dp // count) % 2
            kept = lax.dynamic_slice_in_dim(v, bit * count, count, 0)
            sent = lax.dynamic_slice_in_dim(v, (1 - bit) * count, count, 0)
            v = kept + swap(sent, "dp", n_dp, count)
        return v

    def double(v, axis, n):
        k = 1
        while k < n:
            v = v + swap(v, axis, n, k)
            k *= 2
        return v

    head_rows = jnp.concatenate(
        [partial_mods, jnp.broadcast_to(own_gains, (n_dp, own_gains.shape[1]))], axis=1
    )
    head_vector = double(double(halve(after(head_rows, text_right)), "core", n_core), "z", n_z)
    mods = head_vector[:, :mods_width]
    gains = head_vector[0, mods_width:].reshape(gain_rows, WIDTH)
    shift_a, scale_a, gate_a, shift_f, scale_f, gate_f = [
        mods[:, i * WIDTH : (i + 1) * WIDTH] for i in range(6)
    ]
    gain = [gains[i : i + 1] for i in range(gain_rows)]

    own_units = down_weight.shape[0]
    unit_blocks = n_dp * n_z
    shard_rows = gate_up_weight.shape[0]
    by_units = gate_up_weight.reshape(shard_rows, 2 * unit_blocks, n_core, own_units)


    def units_of(which):
        return lax.dynamic_index_in_dim(by_units, which, 2, keepdims=False).reshape(shard_rows, -1)

    gate_up_shard = by_core(units_of(core), swap(after(units_of(1 - core), mods), "core", n_core, 1), 0)
    text_part = grad_of(text_left, text_right)
    text_sum = lax.psum_scatter(text_part, ("dp", "z"), scatter_dimension=0, tiled=True)
    joint_near = gather_all(joint_weight)(text_part)
    joint_line = getattr(joint_near, "line", text_part)
    first_shard = jnp.concatenate([gate_up_shard, core_columns(after(mixer_weight, mods))], axis=1)
    first_line = gather_line(after(first_shard, joint_line))

    pad = ((0, slots - rows), (0, 0))
    xfloat = jnp.pad(tokens[0], pad).astype(F32)
    upstream = jnp.pad(cotangent[0], pad).astype(F32)
    normed_in, normed_pull = jax.vjp(modulate, xfloat, gain[0], scale_a, shift_a)
    normed_low = normed_in.astype(BF)
    joint_full = joint_near(normed_low)
    joint = product(normed_low, joint_full)
    def to_groups(parts):
        count = parts[0].shape[0]
        spread = []
        for part in parts:
            part = jnp.pad(part, ((0, 0), (0, spare * HEAD_DIM)))
            spread.append(part.reshape(count, n_seq, wide).transpose(1, 0, 2))
        return jnp.concatenate(spread, axis=2)

    def from_groups(part):
        part = part.transpose(1, 0, 2)
        return part.reshape(part.shape[0], n_seq * wide)[:, :WIDTH]

    def exchange(v):
        return lax.all_to_all(v, seq, 0, 0, tiled=True)

    lane = jnp.arange(LANES)
    freq = jnp.exp((lane % (HEAD_DIM // 2)).astype(F32) * (-jnp.log(10000.0) / (HEAD_DIM // 2)))
    angle = (seq_index * rows + jnp.arange(slots)).astype(F32)[:, None] * freq[None, :]
    cosine = jnp.cos(angle)
    sine = jnp.sin(angle) * jnp.where(lane % HEAD_DIM < HEAD_DIM // 2, -1.0, 1.0)[None, :]
    rope_gains = gains[4:6]
    half_slots = slots // 2

    def head_arrays(columns):
        return [jax.ShapeDtypeStruct((n_seq, half_slots, columns * HEAD_DIM), BF)] * heads

    def exchange_heads(arrays):
        return [exchange(v).reshape(n_seq * half_slots, -1) for v in arrays]

    def exchange_back(arrays):
        return [exchange(v.reshape(n_seq, half_slots, -1)) for v in arrays]

    sent = simple_call(group_kernel, head_arrays(6), "group_heads", joint, rope_gains, cosine, sine)
    first_line = first_line(sent[0])
    split_at = gate_up_shard.shape[1]
    mixer_half = gather_dp(first_line[:, split_at:])
    gate_up_half = gather_dp(first_line[:, :split_at])
    down_line = gather_line(after(down_weight, first_line))
    text_raw = own_rows(after(text_sum, sent[0]))
    text_rows = text_raw.shape[0]
    text_keys, text_key_pull = jax.vjp(norm_rows, text_raw[:, :WIDTH], gain[6])
    text_own = exchange(
        to_groups([text_keys.astype(BF), text_raw[:, WIDTH:].astype(BF)])
    ).reshape(n_seq * text_rows, 2 * wide)

    qkv = exchange_heads(sent)
    mixer_full = by_core(mixer_half, swap(mixer_half, "core", n_core, 1), 1)
    down_half = gather_dp(down_line(qkv[0]))
    slot = jnp.arange(n_seq * slots)
    side, line = slot // (n_seq * half_slots), slot % (n_seq * half_slots)
    within = side * half_slots + line % half_slots
    shape_row = image_shape[dp]
    valid = shape_row[0] * (shape_row[1] + 1)
    live = (within < rows) & ((line // half_slots) * rows + within < valid)
    bias = jnp.where(live, 0.0, NEG).astype(BF)[:, None]
    text_bias = jnp.where(jnp.arange(TEXT) < caption_len[dp], 0.0, NEG).astype(BF)[:, None]
    tanh_gates = jnp.tanh(head_gates)
    first_head = seq_index * heads
    own_gates = lax.dynamic_slice_in_dim(jnp.pad(tanh_gates, (0, spare)), first_head, heads, 0)
    gate_rows = [jnp.broadcast_to(own_gates[i : i + 1, None], (1, HEAD_DIM)) for i in range(heads)]
    attended = [
        attend_forward(qkv[i], text_own, bias, text_bias, gate_rows[i], i, 2 * half_slots)
        for i in range(heads)
    ]
    token_shape = jax.ShapeDtypeStruct((slots, WIDTH), BF)
    mixed = simple_call(
        join_kernel, token_shape, "join_heads", *exchange_back([v[0] for v in attended])
    )
    proj = product(mixed, mixer_full)
    branch_a, branch_a_pull = jax.vjp(branch_out, proj, gain[1], gate_a)
    hstate = xfloat + branch_a
    ffn_in, ffn_in_pull = jax.vjp(modulate, hstate, gain[2], scale_f, shift_f)

    ffn_both = both_cores(ffn_in.astype(BF))
    gate_up = product(ffn_both, gate_up_half)
    hidden, swiglu_pull = jax.vjp(swiglu, gate_up)
    hidden_low = hidden.astype(BF)
    ffn = sum_cores(product(hidden_low, down_half))
    branch_f, branch_f_pull = jax.vjp(branch_out, ffn, gain[3], gate_f)
    output = (hstate + branch_f).astype(BF)[None, :rows]

    ffn_grad, gain3_grad, gate_f_grad = branch_f_pull(upstream)
    ffn_grad_both = both_cores(ffn_grad.astype(BF))
    (gate_up_grad_rows,) = swiglu_pull(contract(ffn_grad_both, down_half, 1, 1))
    gate_up_low = gate_up_grad_rows.astype(BF)
    down_part = grad_of(hidden_low, ffn_grad_both)
    gate_up_part = grad_of(ffn_both, after(gate_up_low, down_part))
    down_part = reduce_dp(down_part)
    state_part, gain2_grad, scale_f_grad, shift_f_grad = ffn_in_pull(
        sum_cores(contract(gate_up_low, gate_up_half, 1, 1), gate_up_part)
    )
    state_grad = upstream + state_part
    proj_grad, gain1_grad, gate_a_grad = branch_a_pull(state_grad)
    proj_low = proj_grad.astype(BF)
    mixed_grad = contract(proj_low, mixer_full, 1, 1).astype(BF)
    ups = exchange_heads(simple_call(split_kernel, head_arrays(2), "split_heads", mixed_grad))
    mixer_part = grad_of(*column_split(mixed, after(proj_low, mixed_grad)))
    ups[0] = after(ups[0], mixer_part)
    gate_up_part = reduce_dp(after(gate_up_part, mixer_part))
    mixer_part = reduce_dp(mixer_part)
    ups[-1] = after(ups[-1], down_part)
    grads, dtexts, dgates = zip(*[
        attend_backward(
            qkv[i], text_own, bias, text_bias, gate_rows[i], ups[i], *attended[i][1:], i, 2 * half_slots
        )
        for i in range(heads)
    ])
    grouped = exchange_back(grads)
    down_line = reduce_line(after(down_part, grads[0]))
    mixer_line = reduce_line(after(mixer_part, grads[-1]))
    joint_low, rope_gain_grads = simple_call(
        functools.partial(ungroup_kernel, heads),
        [jax.ShapeDtypeStruct((slots, 3 * WIDTH), BF), jax.ShapeDtypeStruct((2, WIDTH), F32)],
        "ungroup_heads", *grouped, joint, rope_gains, cosine, sine,
    )
    joint_left, joint_right = column_split(normed_low, joint_low)
    piece = joint_right.shape[1] // 2
    joint_parts = [grad_of(joint_left, joint_right[:, p * piece : (p + 1) * piece]) for p in range(2)]
    joint_lines = [
        reduce_line(reduce_dp(after(part, gate_up_part, mixer_part))) for part in joint_parts
    ]
    later_low = after(joint_low, *joint_parts)
    input_part, gain0_grad, scale_a_grad, shift_a_grad = normed_pull(
        contract(later_low, joint_full, 1, 1)
    )
    gate_up_line = reduce_line(after(gate_up_part, later_low))
    down_out = down_line(later_low)
    mixer_out = own_rows(mixer_line(later_low))
    joint_out = own_rows(jnp.concatenate([arrive(input_part) for arrive in joint_lines], axis=1))
    kept, received = [
        v.reshape(shard_rows, 2 * unit_blocks, 1, own_units)
        for v in trade(gate_up_line(input_part).astype(BF))
    ]
    gate_up_out = by_core(kept, received, 2).reshape(shard_rows, -1).astype(F32)
    tokens_grad = (state_grad + input_part).astype(BF)[None, :rows]
    dtext = jnp.concatenate([v[:, :HEAD_DIM] for v in dtexts] + [v[:, HEAD_DIM:] for v in dtexts], axis=1)
    text_back = exchange(dtext.reshape(n_seq, text_rows, 2 * wide))
    text_key_grad, gain6_grad = text_key_pull(from_groups(text_back[:, :, :wide]).astype(F32))
    text_grad_rows = jnp.concatenate(
        [text_key_grad.astype(BF), from_groups(text_back[:, :, wide:])], axis=1
    )
    text_grad_all = lax.all_gather(after(text_grad_rows, *joint_parts), everyone, axis=0, tiled=True)
    text_grad = contract(flat_text, text_grad_all, 0, 0)

    gates_own = jnp.concatenate([jnp.sum(v, axis=1) for v in dgates]) * (1.0 - own_gates * own_gates)
    gates_all = lax.dynamic_update_slice_in_dim(jnp.zeros((WIDTH,), F32), gates_own, first_head, 0)[None, :]
    pieces = [shift_a_grad, scale_a_grad, gate_a_grad, shift_f_grad, scale_f_grad, gate_f_grad]
    shared = [
        gain0_grad, gain1_grad, gain2_grad, gain3_grad, rope_gain_grads[0:1], rope_gain_grads[1:2], gain6_grad,
    ]
    tail = pieces + shared + [gates_all]
    tail = simple_call(
        pack_kernel, jax.ShapeDtypeStruct((-(-len(tail) // 8) * 8, WIDTH), F32), "pack_rows", *tail
    )
    tail = sum_over(sum_over(tail, "core", n_core), "z", n_z)
    tails = [tail] + [swap(tail, "dp", n_dp, k) for k in range(1, n_dp)]
    count = len(pieces)
    total = tree([t[count:] for t in tails])
    gates_grad = total[gain_rows, :HEADS]
    gains_grad = lax.dynamic_slice_in_dim(total[:gain_rows], device * gain_width, gain_width, 1)
    mods_low = jnp.stack([t[:count].astype(BF).reshape(-1) for t in tails])
    cond_rows = jnp.concatenate(
        [lax.dynamic_slice_in_dim(soft_cond, dp ^ k, 1, 0) for k in range(n_dp)], axis=0
    )
    modulation_grad = contract(cond_rows, mods_low, 0, 0)
    bias_grad = lax.dynamic_slice_in_dim(
        jnp.sum(mods_low.astype(F32), axis=0), bias_start, bias_width, 0
    )
    return (
        output,
        tokens_grad,
        joint_out,
        mixer_out,
        gate_up_out,
        down_out,
        text_grad,
        modulation_grad,
        bias_grad,
        gains_grad,
        gates_grad,
    )


def solution(mesh):
    n_dp, n_seq = mesh.shape["dp"], mesh.shape["seq"]
    sizes = (n_dp, n_seq // 2, 2)
    split = Mesh(mesh.devices.reshape(sizes), ("dp", "z", "core"))
    seq, everyone = ("z", "core"), ("dp", "z", "core")
    token_spec, row_spec, column_spec = P("dp", seq, None), P(everyone, None), P(None, everyone)
    in_specs = (
        token_spec, column_spec, P(None, None, everyone), P(), P(), token_spec,
        row_spec, row_spec, row_spec, row_spec, row_spec, row_spec, P(everyone), column_spec, P(),
    )
    out_specs = (
        token_spec, token_spec, row_spec, row_spec, row_spec, row_spec, row_spec, row_spec,
        P(everyone), column_spec, P(),
    )
    return jax.shard_map(
        functools.partial(local, sizes), mesh=split, in_specs=in_specs, out_specs=out_specs, check_vma=False
    )
```

time: 1430 us -> 946 us (0.66)
  waiting for transfers between devices: 986 us -> 327 us
  starting transfers between devices: 37.8 us -> 126 us
  local copies, waits for them, and re-layouts: 39.1 us -> 104 us
  Pallas kernels: 116 us -> 143 us
  blocking collectives: 50.2 us -> 31.7 us
    reduce_scatter x5 -> x6, waiting for transfers between devices: 467 us -> 0.11 us  [the longest x5 0.09 us: reduce_dp(): return lax.psum_scatter(part, 'dp', scatter_dimension=0, tiled=True)]
    all_gather x5 -> x4, waiting for transfers between devices: 338 us -> 5.01 us  [the longest x3 5.01 us: gather_dp(): return lax.all_gather(line, 'dp', axis=0, tiled=True)]
    ppermute x0 -> x24, waiting for transfers between devices: none -> 144 us  [shift_z(): return lax.ppermute(v, 'z', [(i, (i + k) % n_z) for i in range(n_z)])]
    ppermute x0 -> x24, starting transfers between devices: none -> 40.4 us  [shift_z(): return lax.ppermute(v, 'z', [(i, (i + k) % n_z) for i in range(n_z)])]
    all_to_all x4 -> x12, starting transfers between devices: 16.7 us -> 51.4 us  [exchange(): return lax.all_to_all(v, seq, 0, 0, tiled=True)]
    all_to_all x4 -> x12, waiting for transfers between devices: 137 us -> 105 us  [exchange(): return lax.all_to_all(v, seq, 0, 0, tiled=True)]
    ppermute x26 -> x38, waiting for transfers between devices: 41.2 us -> 71.9 us  [swap(): return lax.ppermute(v, axis, [(i, i ^ k) for i in range(n)])]
    dynamic_update_slice x0 -> x23, local copies, waits for them, and re-layouts: none -> 29 us  [the longest x10 16.6 us: second(): full = lax.dynamic_update_slice(full, held, (index, start, of_core, 0, 0))]
  transfers between devices with their start and end apart: 40 -> 84, of which waited for: 29 -> 35; matrix products, arithmetic and copies ran while one was open for 14% -> 27% of each run, Pallas kernels for 8% -> 15%
where the time goes in v2:
time: 946 us; the launch traced here: 935 us
  waiting for transfers between devices  327 us (35%)
  Pallas kernels  143 us (15%)
  starting transfers between devices  126 us (13%)
  matrix products  124 us (13%)
  local copies, waits for them, and re-layouts  104 us (11%)
  other arithmetic  60.2 us (6%)
  blocking collectives  31.7 us (3%)
  between operations  18.6 us (2%)
    ppermute x24, waiting for transfers between devices, shift_z(): return lax.ppermute(v, 'z', [(i, (i + k) % n_z) for i in range(n_z)])  144 us
    all_to_all x12, waiting for transfers between devices, exchange(): return lax.all_to_all(v, seq, 0, 0, tiled=True)  105 us
    dot_general x12, matrix products, contract(): lax.dot_general(left, right, (((left_dim,), (right_dim,)), ((), ())), pre...  90.1 us
    ppermute x38, waiting for transfers between devices, swap(): return lax.ppermute(v, axis, [(i, i ^ k) for i in range(n)])  71.9 us
    pallas_call x3, Pallas kernels, attend_backward(): pl.pallas_call(functools.partial(attend_backward_kernel, index), grid=(ha...  71.7 us
    all_to_all x12, starting transfers between devices, exchange(): return lax.all_to_all(v, seq, 0, 0, tiled=True)  51.4 us
    pallas_call x3, Pallas kernels, attend_forward(): pl.pallas_call(functools.partial(attend_forward_kernel, index), grid=(hal...  47.5 us
    ppermute x24, starting transfers between devices, shift_z(): return lax.ppermute(v, 'z', [(i, (i + k) % n_z) for i in range(n_z)])  40.4 us
  transfers between devices with their start and end apart: 84, of which 35 were waited for; matrix products, arithmetic and copies ran while one was open for 27% of the time, Pallas kernels for 15%

profile of v2, /device:TPU:0, one launch (start us, length us, event | category | flops | bytes accessed | tf_op | source)
XLA Modules:
  0.0 935.2 jit_solution(9163013255896408293)
XLA Ops:
  44.4 10.3 %collective-permute-start.5 = (f32[1,19968]{1,0:T(1,128)S(1)}, f32[1,19968]{1,0:T(1,128)S(1)}, u32[]{:S(2)}, u32[]{:S(2)}) collective-permute-start(f32[1,19968]{1,0:T(1,128)S(1)} %add.562), channel_id=1, source_target_pairs={{0,4},{2,6},{4,0},{6,2},{1,5},{3,7},{5,1},{7,3},{8,12},{10,14},{12... | collective-permute-start | bytes 239624 | tf_op jit(solution)/shard_map/ppermute | solution.py:363
  81.2 23.6 %collective-permute-done.11 = bf16[192,4608]{1,0:T(8,128)(2,1)} collective-permute-done((bf16[192,4608]{1,0:T(8,128)(2,1)}, bf16[192,4608]{1,0:T(8,128)(2,1)}, u32[]{:S(2)}, u32[]{:S(2)}) %collective-permute-start.11) | collective-permute-done | bytes 1769504 | tf_op jit(solution)/shard_map/ppermute | solution.py:363
  118.6 10.9 %collective-permute-done.15 = bf16[96,4608]{1,0:T(8,128)(2,1)S(1)} collective-permute-done((bf16[96,4608]{1,0:T(8,128)(2,1)S(1)}, bf16[96,4608]{1,0:T(8,128)(2,1)S(1)}, u32[]{:S(2)}, u32[]{:S(2)}) %collective-permute-start.15) | collective-permute-done | bytes 884768 | tf_op jit(solution)/shard_map/ppermute | solution.py:363
  143.2 12.2 %fusion.127.joint_ref.refs_3_ = f32[304,4608]{1,0:T(8,128)} fusion(bf16[304,1536]{1,0:T(8,128)(2,1)} %fusion.20, bf16[1536,4608]{1,0:T(8,128)(2,1)} %bitcast.195), kind=kOutput, calls=%fused_computation.322 | convolution fusion | flops 4303355904 | bytes 20692992 | tf_op jit(solution)/shard_map/dot_general | solution.py:42
  155.4 7.6 group_heads.1
  188.8 42.5 %all-to-all-done = bf16[8,152,384]{2,1,0:T(8,128)(2,1)} async-done(((bf16[8,152,384]{2,1,0:T(8,128)(2,1)}), bf16[8,152,384]{2,1,0:T(8,128)(2,1)}, u32[]{:S(2)}, u32[]{:S(2)}) %all-to-all-start) | async-done | bytes 933920 | tf_op jit(solution)/shard_map/all_to_all | solution.py:562
  247.0 21.1 %all-to-all-done.3 = bf16[8,152,384]{2,1,0:T(8,128)(2,1)} async-done(((bf16[8,152,384]{2,1,0:T(8,128)(2,1)}), bf16[8,152,384]{2,1,0:T(8,128)(2,1)}, u32[]{:S(2)}, u32[]{:S(2)}) %all-to-all-start.3) | async-done | bytes 933920 | tf_op jit(solution)/shard_map/all_to_all | solution.py:562
  272.8 7.0 all-to-all-done.1
  293.1 15.8 %attend_forward.3 = (bf16[1216,128]{1,0:T(8,128)(2,1)}, f32[1216,128]{1,0:T(8,128)}, f32[1216,128]{1,0:T(8,128)}, f32[1216,4]{1,0:T(8,128)}) custom-call(bf16[1216,384]{1,0:T(8,128)(2,1)} %bitcast.20.qkv_ref.q_ref, bf16[256,384]{1,0:T(8,128)(2,1)} %bitcast.241, bf16[2432,1]{1,0:T(8,128)(2,1)} %select_convert_fusion.bias_ref, ...), custom_call_target="tpu_custom_call" | custom-call | flops 6694109184 | bytes 2801664 | tf_op jit(solution)/shard_map/attend_forward/pallas_call | solution.py:188
  315.1 15.9 %attend_forward.4 = (bf16[1216,128]{1,0:T(8,128)(2,1)}, f32[1216,128]{1,0:T(8,128)}, f32[1216,128]{1,0:T(8,128)}, f32[1216,4]{1,0:T(8,128)}) custom-call(bf16[1216,384]{1,0:T(8,128)(2,1)} %bitcast.28.qkv_ref.q_ref, bf16[256,384]{1,0:T(8,128)(2,1)} %bitcast.242, bf16[2432,1]{1,0:T(8,128)(2,1)} %select_convert_fusion.bias_ref, ...), custom_call_target="tpu_custom_call" | custom-call | flops 6694109184 | bytes 2801664 | tf_op jit(solution)/shard_map/attend_forward/pallas_call | solution.py:188
  337.4 15.8 %attend_forward.5 = (bf16[1216,128]{1,0:T(8,128)(2,1)}, f32[1216,128]{1,0:T(8,128)}, f32[1216,128]{1,0:T(8,128)}, f32[1216,4]{1,0:T(8,128)}) custom-call(bf16[1216,384]{1,0:T(8,128)(2,1)} %bitcast.215, bf16[256,384]{1,0:T(8,128)(2,1)} %bitcast.243, bf16[2432,1]{1,0:T(8,128)(2,1)} %select_convert_fusion.bias_ref, ...), custom_call_target="tpu_custom_call" | custom-call | flops 6694109184 | bytes 2801664 | tf_op jit(solution)/shard_map/attend_forward/pallas_call | solution.py:188
  353.3 16.2 %all_to_all.70.refs_2_ = bf16[8,152,128]{2,1,0:T(8,128)(2,1)} all-to-all(bf16[8,152,128]{2,1,0:T(8,128)(2,1)} %bitcast.240), channel_id=1, replica_groups=mesh['dp'=4,'z'=4,'core'=2] {'z','core'}, dimensions={0} | all-to-all | bytes 622592 | tf_op jit(solution)/shard_map/all_to_all | solution.py:562
  383.3 11.4 %fusion.56 = f32[608,4096]{1,0:T(8,128)S(1)} fusion(bf16[1536,4096]{1,0:T(8,128)(2,1)} %all-gather.7.cloned.1.call-done, bf16[304,1536]{1,0:T(8,128)(2,1)} %collective-permute-done.26, bf16[304,1536]{1,0:T(8,128)(2,1)} %copy-done.28), kind=kOutput, calls=%fused_computation.111 | convolution fusion | flops 7654146048 | bytes 24412160 | tf_op jit(solution)/shard_map/dot_general | solution.py:42
  424.3 7.5 convolution_convert_fusion.3
  431.8 15.5 %fusion.63 = (f32[608,2048]{1,0:T(8,128)}, f32[608,2048]{1,0:T(8,128)}) fusion(f32[608,4096]{1,0:T(8,128)} %copy-done.9, bf16[2048,1536]{1,0:T(8,128)(2,1)} %all-gather.9.cloned.1.call-done, bf16[304,1536]{1,0:T(8,128)(2,1)} %copy-done.71, bf16[304,1536]{1,0:T(8,128)(2,1)} %copy-done.30), kind=kOutput, calls=%fused_computation.131 | convolution fusion | flops 3843883008 | bytes 28082176 | tf_op jit(solution)/shard_map/dot_general | solution.py:46
  447.3 7.0 add_convert_fusion
  454.3 13.3 %fusion.129 = f32[608,1536]{1,0:T(8,128)S(1)} fusion(bf16[608,4096]{1,0:T(8,128)(2,1)} %add_convert_fusion, bf16[1536,4096]{1,0:T(8,128)(2,1)} %all-gather.7.cloned.1.call-done), kind=kOutput, calls=%fused_computation.324 | convolution fusion | flops 7650410496 | bytes 21299200 | tf_op jit(solution)/shard_map/dot_general | solution.py:46
  471.5 13.6 %convolution_convert_fusion = bf16[1536,4096]{1,0:T(8,128)(2,1)} fusion(bf16[608,4096]{1,0:T(8,128)(2,1)S(1)} %copy-done.12, bf16[304,1536]{1,0:T(8,128)(2,1)} %collective-permute-done.26, bf16[304,1536]{1,0:T(8,128)(2,1)S(1)} %copy-done.29), kind=kOutput, calls=%fused_computation | convolution fusion | flops 7660437504 | bytes 19431424 | tf_op jit(solution)/shard_map/dot_general | solution.py:46
  505.2 15.5 %all_to_all.71 = bf16[8,152,128]{2,1,0:T(8,128)(2,1)} all-to-all(bf16[8,152,128]{2,1,0:T(8,128)(2,1)} %get-tuple-element.114), channel_id=1, replica_groups=mesh['dp'=4,'z'=4,'core'=2] {'z','core'}, dimensions={0} | all-to-all | bytes 622592 | tf_op jit(solution)/shard_map/all_to_all | solution.py:562
  524.2 10.7 %all-to-all-done.9 = bf16[8,152,128]{2,1,0:T(8,128)(2,1)S(1)} async-done(((bf16[8,152,128]{2,1,0:T(8,128)(2,1)}), bf16[8,152,128]{2,1,0:T(8,128)(2,1)S(1)}, u32[]{:S(2)}, u32[]{:S(2)}) %all-to-all-start.9) | async-done | bytes 311328 | tf_op jit(solution)/shard_map/all_to_all | solution.py:562
  538.5 23.7 %attend_backward.3 = (bf16[1216,384]{1,0:T(8,128)(2,1)}, bf16[256,128]{1,0:T(8,128)(2,1)}, f32[1,64]{1,0:T(1,128)}) custom-call(bf16[1216,384]{1,0:T(8,128)(2,1)} %bitcast.20.qkv_ref.q_ref, bf16[256,384]{1,0:T(8,128)(2,1)} %bitcast.244, bf16[2432,1]{1,0:T(8,128)(2,1)} %select_convert_fusion.bias_ref, bf16[256,1]{1,0:T(8,128)(2,1)} %select_convert_fusion.1.text_bias_ref, ...), custom_call_target="tpu_custom_call" | custom-call | flops 16735272960 | bytes 4046848 | tf_op jit(solution)/shard_map/attend_backward/pallas_call | solution.py:213
  567.5 24.0 %attend_backward.4 = (bf16[1216,384]{1,0:T(8,128)(2,1)}, bf16[256,128]{1,0:T(8,128)(2,1)}, f32[1,64]{1,0:T(1,128)}) custom-call(bf16[1216,384]{1,0:T(8,128)(2,1)} %bitcast.28.qkv_ref.q_ref, bf16[256,384]{1,0:T(8,128)(2,1)} %bitcast.245, bf16[2432,1]{1,0:T(8,128)(2,1)} %select_convert_fusion.bias_ref, bf16[256,1]{1,0:T(8,128)(2,1)} %select_convert_fusion.1.text_bias_ref, ...), custom_call_target="tpu_custom_call" | custom-call | flops 16735272960 | bytes 4046848 | tf_op jit(solution)/shard_map/attend_backward/pallas_call | solution.py:213
  596.9 24.0 %attend_backward.5 = (bf16[1216,384]{1,0:T(8,128)(2,1)}, bf16[256,128]{1,0:T(8,128)(2,1)}, f32[1,64]{1,0:T(1,128)}) custom-call(bf16[1216,384]{1,0:T(8,128)(2,1)} %bitcast.217, bf16[256,384]{1,0:T(8,128)(2,1)} %bitcast.246, bf16[2432,1]{1,0:T(8,128)(2,1)} %select_convert_fusion.bias_ref, bf16[256,1]{1,0:T(8,128)(2,1)} %select_convert_fusion.1.text_bias_ref, ...), custom_call_target="tpu_custom_call" | custom-call | flops 16735272960 | bytes 4046848 | tf_op jit(solution)/shard_map/attend_backward/pallas_call | solution.py:213
  627.3 23.1 %all-to-all-done.12.refs_2_ = bf16[8,152,384]{2,1,0:T(8,128)(2,1)} async-done(((bf16[8,152,384]{2,1,0:T(8,128)(2,1)}), bf16[8,152,384]{2,1,0:T(8,128)(2,1)}, u32[]{:S(2)}, u32[]{:S(2)}) %all-to-all-start.12) | async-done | bytes 933920 | tf_op jit(solution)/shard_map/all_to_all | solution.py:562
  654.3 8.9 ungroup_heads.1
  671.8 6.9 convolution_convert_fusion.1
  722.1 35.8 %collective-permute-done.53 = bf16[128,1536]{1,0:T(8,128)(2,1)S(1)} collective-permute-done((bf16[128,1536]{1,0:T(8,128)(2,1)S(1)}, bf16[128,1536]{1,0:T(8,128)(2,1)S(1)}, u32[]{:S(2)}, u32[]{:S(2)}) %collective-permute-start.53) | collective-permute-done | bytes 393248 | tf_op jit(solution)/shard_map/ppermute | solution.py:391
  758.0 9.2 fusion.22
  817.5 9.0 collective-permute-done.50
  826.4 50.2 %collective-permute-done.49 = bf16[96,4096]{1,0:T(8,128)(2,1)} collective-permute-done((bf16[96,4096]{1,0:T(8,128)(2,1)}, bf16[96,4096]{1,0:T(8,128)(2,1)}, u32[]{:S(2)}, u32[]{:S(2)}) %collective-permute-start.49) | collective-permute-done | bytes 786464 | tf_op jit(solution)/shard_map/ppermute | solution.py:391
  889.3 13.4 %collective-permute-done.38 = bf16[96,1152]{1,0:T(8,128)(2,1)S(1)} collective-permute-done((bf16[96,1152]{1,0:T(8,128)(2,1)S(1)}, bf16[96,1152]{1,0:T(8,128)(2,1)S(1)}, u32[]{:S(2)}, u32[]{:S(2)}) %collective-permute-start.38) | collective-permute-done | bytes 221216 | tf_op jit(solution)/shard_map/ppermute | solution.py:391
  902.7 17.3 %collective-permute-done.41 = bf16[96,1152]{1,0:T(8,128)(2,1)S(1)} collective-permute-done((bf16[96,1152]{1,0:T(8,128)(2,1)S(1)}, bf16[96,1152]{1,0:T(8,128)(2,1)S(1)}, u32[]{:S(2)}, u32[]{:S(2)}) %collective-permute-start.41) | collective-permute-done | bytes 221216 | tf_op jit(solution)/shard_map/ppermute | solution.py:391
  (511 shorter events, 377.6 us)
Async XLA Ops:
  8.0 232.9 %reduce-scatter.7.cloned.1.call-start = ((), (), s32[]{:S(2)}) async-start(), calls=%async_computation.20 | async-start | bytes 3342336 | tf_op jit(solution)/shard_map/reduce_scatter | solution.py:536
  8.1 46.6 %collective-permute-start.6 = (bf16[48,4608]{1,0:T(8,128)(2,1)}, bf16[48,4608]{1,0:T(8,128)(2,1)}, u32[]{:S(2)}, u32[]{:S(2)}) collective-permute-start(bf16[48,4608]{1,0:T(8,128)(2,1)} %param.21), channel_id=1, source_target_pairs={{0,2},{2,4},{4,6},{6,0},{1,3},{3,5},{5,7},{7,1},{8,10},{10,12},{12... | collective-permute-start | bytes 1327112 | tf_op jit(solution)/shard_map/ppermute | solution.py:391
  11.2 43.5 %collective-permute-start.8 = (bf16[48,4608]{1,0:T(8,128)(2,1)}, bf16[48,4608]{1,0:T(8,128)(2,1)}, u32[]{:S(2)}, u32[]{:S(2)}) collective-permute-start(bf16[48,4608]{1,0:T(8,128)(2,1)} %param.21), channel_id=1, source_target_pairs={{0,4},{2,6},{4,0},{6,2},{1,5},{3,7},{5,1},{7,3},{8,12},{10,14},{12... | collective-permute-start | bytes 1327112 | tf_op jit(solution)/shard_map/ppermute | solution.py:391
  13.8 40.9 %collective-permute-start.9 = (bf16[48,4608]{1,0:T(8,128)(2,1)}, bf16[48,4608]{1,0:T(8,128)(2,1)}, u32[]{:S(2)}, u32[]{:S(2)}) collective-permute-start(bf16[48,4608]{1,0:T(8,128)(2,1)} %param.21), channel_id=1, source_target_pairs={{0,6},{2,0},{4,2},{6,4},{1,7},{3,1},{5,3},{7,5},{8,14},{10,8},{12,... | collective-permute-start | bytes 1327112 | tf_op jit(solution)/shard_map/ppermute | solution.py:391
  40.6 251.0 %all-gather.5.cloned.1.call-start = ((), (), s32[]{:S(2)}) async-start(), calls=%async_computation.21 | async-start | bytes 2949120 | tf_op jit(solution)/shard_map/all_gather | solution.py:409
  60.1 47.2 %collective-permute-start.10 = (bf16[192,4608]{1,0:T(8,128)(2,1)}, bf16[192,4608]{1,0:T(8,128)(2,1)}, u32[]{:S(2)}, u32[]{:S(2)}) collective-permute-start(bf16[192,4608]{1,0:T(8,128)(2,1)} %bitcast.8), channel_id=1, source_target_pairs={{0,1},{1,0},{2,3},{3,2},{4,5},{5,4},{6,7},{7,6},{8,9},{9,8},{10,11... | collective-permute-start | bytes 5308424 | tf_op jit(solution)/shard_map/ppermute | solution.py:363
  60.1 44.7 %collective-permute-start.11 = (bf16[192,4608]{1,0:T(8,128)(2,1)}, bf16[192,4608]{1,0:T(8,128)(2,1)}, u32[]{:S(2)}, u32[]{:S(2)}) collective-permute-start(bf16[192,4608]{1,0:T(8,128)(2,1)} %bitcast.8), channel_id=1, source_target_pairs={{0,8},{8,0},{16,24},{24,16},{1,9},{9,1},{17,25},{25,17},{2,10},{10... | collective-permute-start | bytes 5308424 | tf_op jit(solution)/shard_map/ppermute | solution.py:363
  62.1 43.9 %collective-permute-start.13 = (bf16[192,4608]{1,0:T(8,128)(2,1)}, bf16[192,4608]{1,0:T(8,128)(2,1)S(1)}, u32[]{:S(2)}, u32[]{:S(2)}) collective-permute-start(bf16[192,4608]{1,0:T(8,128)(2,1)} %bitcast.8), channel_id=1, source_target_pairs={{0,16},{8,24},{16,0},{24,8},{1,17},{9,25},{17,1},{25,9},{2,18},{10... | collective-permute-start | bytes 5308424 | tf_op jit(solution)/shard_map/ppermute | solution.py:363
  78.3 84.8 %collective-permute-start.22 = (bf16[96,4864]{1,0:T(8,128)(2,1)S(1)}, bf16[96,4864]{1,0:T(8,128)(2,1)}, u32[]{:S(2)}, u32[]{:S(2)}) collective-permute-start(bf16[96,4864]{1,0:T(8,128)(2,1)S(1)} %maximum_maximum_fusion), channel_id=1, source_target_pairs={{0,2},{2,4},{4,6},{6,0},{1,3},{3,5},{5,7},{7,1},{8,10},{10,12},{12... | collective-permute-start | bytes 2801672 | tf_op jit(solution)/shard_map/ppermute | solution.py:391
  81.2 81.8 %collective-permute-start.23 = (bf16[96,4864]{1,0:T(8,128)(2,1)S(1)}, bf16[96,4864]{1,0:T(8,128)(2,1)}, u32[]{:S(2)}, u32[]{:S(2)}) collective-permute-start(bf16[96,4864]{1,0:T(8,128)(2,1)S(1)} %maximum_maximum_fusion), channel_id=1, source_target_pairs={{0,4},{2,6},{4,0},{6,2},{1,5},{3,7},{5,1},{7,3},{8,12},{10,14},{12... | collective-permute-start | bytes 2801672 | tf_op jit(solution)/shard_map/ppermute | solution.py:391
  129.4 37.9 %collective-permute-start.24 = (bf16[96,4864]{1,0:T(8,128)(2,1)S(1)}, bf16[96,4864]{1,0:T(8,128)(2,1)}, u32[]{:S(2)}, u32[]{:S(2)}) collective-permute-start(bf16[96,4864]{1,0:T(8,128)(2,1)S(1)} %maximum_maximum_fusion), channel_id=1, source_target_pairs={{0,6},{2,0},{4,2},{6,4},{1,7},{3,1},{5,3},{7,5},{8,14},{10,8},{12,... | collective-permute-start | bytes 2801672 | tf_op jit(solution)/shard_map/ppermute | solution.py:391
  173.9 209.4 %all-gather.7.cloned.1.call-start = ((), (), s32[]{:S(2)}) async-start(), calls=%async_computation.22 | async-start | bytes 15728640 | tf_op jit(solution)/shard_map/all_gather | solution.py:409
  178.2 53.1 %all-to-all-start = ((bf16[8,152,384]{2,1,0:T(8,128)(2,1)}), bf16[8,152,384]{2,1,0:T(8,128)(2,1)}, u32[]{:S(2)}, u32[]{:S(2)}) async-start(bf16[8,152,384]{2,1,0:T(8,128)(2,1)} %get-tuple-element.95), calls=%async_computation | async-start | bytes 1867776 | tf_op jit(solution)/shard_map/all_to_all | solution.py:562
  182.6 53.0 %collective-permute-start.27 = (bf16[128,1536]{1,0:T(8,128)(2,1)S(1)}, bf16[128,1536]{1,0:T(8,128)(2,1)}, u32[]{:S(2)}, u32[]{:S(2)}) collective-permute-start(bf16[128,1536]{1,0:T(8,128)(2,1)S(1)} %copy-done.37), channel_id=1, source_target_pairs={{0,2},{2,4},{4,6},{6,0},{1,3},{3,5},{5,7},{7,1},{8,10},{10,12},{12... | collective-permute-start | bytes 1179656 | tf_op jit(solution)/shard_map/ppermute | solution.py:391
  184.5 55.4 %collective-permute-start.28 = (bf16[128,1536]{1,0:T(8,128)(2,1)S(1)}, bf16[128,1536]{1,0:T(8,128)(2,1)}, u32[]{:S(2)}, u32[]{:S(2)}) collective-permute-start(bf16[128,1536]{1,0:T(8,128)(2,1)S(1)} %copy-done.37), channel_id=1, source_target_pairs={{0,4},{2,6},{4,0},{6,2},{1,5},{3,7},{5,1},{7,3},{8,12},{10,14},{12... | collective-permute-start | bytes 1179656 | tf_op jit(solution)/shard_map/ppermute | solution.py:391
  186.8 56.1 %collective-permute-start.29 = (bf16[128,1536]{1,0:T(8,128)(2,1)S(1)}, bf16[128,1536]{1,0:T(8,128)(2,1)S(1)}, u32[]{:S(2)}, u32[]{:S(2)}) collective-permute-start(bf16[128,1536]{1,0:T(8,128)(2,1)S(1)} %copy-done.37), channel_id=1, source_target_pairs={{0,6},{2,0},{4,2},{6,4},{1,7},{3,1},{5,3},{7,5},{8,14},{10,8},{12,... | collective-permute-start | bytes 1179656 | tf_op jit(solution)/shard_map/ppermute | solution.py:391
  231.3 36.8 %all-to-all-start.3 = ((bf16[8,152,384]{2,1,0:T(8,128)(2,1)}), bf16[8,152,384]{2,1,0:T(8,128)(2,1)}, u32[]{:S(2)}, u32[]{:S(2)}) async-start(bf16[8,152,384]{2,1,0:T(8,128)(2,1)} %get-tuple-element.98), calls=%async_computation.4 | async-start | bytes 1867776 | tf_op jit(solution)/shard_map/all_to_all | solution.py:562
  271.5 134.5 %all-gather.9.cloned.1.call-start = ((), (), s32[]{:S(2)}) async-start(), calls=%async_computation.23 | async-start | bytes 7864320 | tf_op jit(solution)/shard_map/all_gather | solution.py:409
  291.6 80.9 %collective-permute-start.25 = (bf16[1536,768]{1,0:T(8,128)(2,1)}, bf16[1536,768]{1,0:T(8,128)(2,1)}, u32[]{:S(2)}, u32[]{:S(2)}) collective-permute-start(bf16[1536,768]{1,0:T(8,128)(2,1)} %all-gather.5.cloned.1.call-done), channel_id=1, source_target_pairs={{0,1},{1,0},{2,3},{3,2},{4,5},{5,4},{6,7},{7,6},{8,9},{9,8},{10,11... | collective-permute-start | bytes 7077896 | tf_op jit(solution)/shard_map/ppermute | solution.py:363
  336.0 260.8 %reduce-scatter.9.cloned.1.call-start = ((), (), s32[]{:S(2)}) async-start(), calls=%async_computation.24 | async-start | bytes 7864320 | tf_op jit(solution)/shard_map/reduce_scatter | solution.py:443
  431.8 253.8 %reduce-scatter.13.cloned.1.call-start = ((), (), s32[]{:S(2)}) async-start(), calls=%async_computation.26 | async-start | bytes 2949120 | tf_op jit(solution)/shard_map/reduce_scatter | solution.py:443
  502.0 183.6 %reduce-scatter.11.cloned.1.call-start = ((), (), s32[]{:S(2)}) async-start(), calls=%async_computation.25 | async-start | bytes 15728640 | tf_op jit(solution)/shard_map/reduce_scatter | solution.py:443
  653.8 157.5 %all-gather.11.cloned.1.call-start = ((), (), s32[]{:S(2)}) async-start(), calls=%async_computation.29 | async-start | bytes 6488064 | tf_op jit(solution)/shard_map/all_gather | solution.py:690
  685.5 193.1 %reduce-scatter.15.cloned.1.call-start = ((), (), s32[]{:S(2)}) async-start(), calls=%async_computation.27 | async-start | bytes 4423680 | tf_op jit(solution)/shard_map/reduce_scatter | solution.py:443
  686.1 197.3 %reduce-scatter.17.cloned.1.call-start = ((), (), s32[]{:S(2)}) async-start(), calls=%async_computation.28 | async-start | bytes 4423680 | tf_op jit(solution)/shard_map/reduce_scatter | solution.py:443
  705.5 52.4 %collective-permute-start.53 = (bf16[128,1536]{1,0:T(8,128)(2,1)S(1)}, bf16[128,1536]{1,0:T(8,128)(2,1)S(1)}, u32[]{:S(2)}, u32[]{:S(2)}) collective-permute-start(bf16[128,1536]{1,0:T(8,128)(2,1)S(1)} %get-tuple-element.236), channel_id=1, source_target_pairs={{0,4},{2,6},{4,0},{6,2},{1,5},{3,7},{5,1},{7,3},{8,12},{10,14},{12... | collective-permute-start | bytes 1179656 | tf_op jit(solution)/shard_map/ppermute | solution.py:391
  710.0 47.9 %collective-permute-start.52 = (bf16[128,1536]{1,0:T(8,128)(2,1)S(1)}, bf16[128,1536]{1,0:T(8,128)(2,1)S(1)}, u32[]{:S(2)}, u32[]{:S(2)}) collective-permute-start(bf16[128,1536]{1,0:T(8,128)(2,1)S(1)} %get-tuple-element.234), channel_id=1, source_target_pairs={{0,2},{2,4},{4,6},{6,0},{1,3},{3,5},{5,7},{7,1},{8,10},{10,12},{12... | collective-permute-start | bytes 1179656 | tf_op jit(solution)/shard_map/ppermute | solution.py:391
  717.3 61.4 %collective-permute-start.47 = (bf16[48,768]{1,0:T(8,128)(2,1)S(1)}, bf16[48,768]{1,0:T(8,128)(2,1)S(1)}, u32[]{:S(2)}, u32[]{:S(2)}) collective-permute-start(bf16[48,768]{1,0:T(8,128)(2,1)S(1)} %constant_dynamic-slice_fusion.6), channel_id=1, source_target_pairs={{0,1},{1,0},{2,3},{3,2},{4,5},{5,4},{6,7},{7,6},{8,9},{9,8},{10,11... | collective-permute-start | bytes 221192 | tf_op jit(solution)/shard_map/ppermute | solution.py:363
  808.1 68.5 %collective-permute-start.49 = (bf16[96,4096]{1,0:T(8,128)(2,1)}, bf16[96,4096]{1,0:T(8,128)(2,1)}, u32[]{:S(2)}, u32[]{:S(2)}) collective-permute-start(bf16[96,4096]{1,0:T(8,128)(2,1)} %get-tuple-element.231), channel_id=1, source_target_pairs={{0,4},{2,6},{4,0},{6,2},{1,5},{3,7},{5,1},{7,3},{8,12},{10,14},{12... | collective-permute-start | bytes 2359304 | tf_op jit(solution)/shard_map/ppermute | solution.py:391
  808.8 67.8 %collective-permute-start.48 = (bf16[96,4096]{1,0:T(8,128)(2,1)}, bf16[96,4096]{1,0:T(8,128)(2,1)}, u32[]{:S(2)}, u32[]{:S(2)}) collective-permute-start(bf16[96,4096]{1,0:T(8,128)(2,1)} %get-tuple-element.229), channel_id=1, source_target_pairs={{0,2},{2,4},{4,6},{6,0},{1,3},{3,5},{5,7},{7,1},{8,10},{10,12},{12... | collective-permute-start | bytes 2359304 | tf_op jit(solution)/shard_map/ppermute | solution.py:391
  886.5 33.4 %collective-permute-start.41 = (bf16[96,1152]{1,0:T(8,128)(2,1)S(1)}, bf16[96,1152]{1,0:T(8,128)(2,1)S(1)}, u32[]{:S(2)}, u32[]{:S(2)}) collective-permute-start(bf16[96,1152]{1,0:T(8,128)(2,1)S(1)} %get-tuple-element.243), channel_id=1, source_target_pairs={{0,4},{2,6},{4,0},{6,2},{1,5},{3,7},{5,1},{7,3},{8,12},{10,14},{12... | collective-permute-start | bytes 663560 | tf_op jit(solution)/shard_map/ppermute | solution.py:391
  886.5 33.4 %collective-permute-start.40 = (bf16[96,1152]{1,0:T(8,128)(2,1)S(1)}, bf16[96,1152]{1,0:T(8,128)(2,1)S(1)}, u32[]{:S(2)}, u32[]{:S(2)}) collective-permute-start(bf16[96,1152]{1,0:T(8,128)(2,1)S(1)} %get-tuple-element.241), channel_id=1, source_target_pairs={{0,2},{2,4},{4,6},{6,0},{1,3},{3,5},{5,7},{7,1},{8,10},{10,12},{12... | collective-permute-start | bytes 663560 | tf_op jit(solution)/shard_map/ppermute | solution.py:391
  (129 other events, 2131.8 us)
Sparse Core Ops, SparseCore 0:
  40.7 190.8 reduce-scatter.6
  685.6 94.9 all-gather.10
Sparse Core Ops, SparseCore 1:
  174.0 35.6 all-gather.4
  211.4 122.3 all-gather.6
  336.0 70.0 all-gather.8
  431.9 70.0 reduce-scatter.8
  505.0 37.2 reduce-scatter.12
  545.4 120.5 reduce-scatter.10
  689.1 47.9 reduce-scatter.14
  772.4 51.2 reduce-scatter.16

commit v3 on v2

--- a/solution.py
+++ b/solution.py
@@ -405,6 +405,58 @@
 
         return arrive
 
+    class Gather:
+        def __init__(self, shard):
+            self.stack, self.offsets, self.next = shard[None], [0], n_z // 2
+            self.send()
+
+        def send(self):
+            self.pending = swap(self.stack, "z", n_z, self.next) if self.next else None
+
+        def step(self, *before):
+            other = after(self.pending, *before)
+            self.offsets = self.offsets + [offset ^ self.next for offset in self.offsets]
+            self.stack = jnp.concatenate([self.stack, other], axis=0)
+            self.next //= 2
+            self.send()
+            return self.stack
+
+        def finish(self, *before):
+            while self.next > 1:
+                self.step(*before)
+            count = len(self.offsets)
+            last = after(self.pending, *before)
+            line = jnp.zeros((n_z,) + last.shape[1:], last.dtype)
+            for i, offset in enumerate(self.offsets):
+                line = place(line, self.stack[i], z_index ^ offset)
+                line = place(line, last[i], z_index ^ offset ^ self.next)
+            return line.reshape(-1, last.shape[2])
+
+    class Reduce:
+        def __init__(self, part):
+            self.line, self.next = part.reshape(n_z, -1, part.shape[1]), 1
+            self.send()
+
+        def send(self):
+            if self.next < n_z:
+                bit = (z_index // self.next) % 2
+                pairs = self.line.reshape((-1, 2) + self.line.shape[1:])
+                self.kept = lax.dynamic_index_in_dim(pairs, bit, 1, keepdims=False)
+                sent = lax.dynamic_index_in_dim(pairs, 1 - bit, 1, keepdims=False)
+                self.pending = swap(sent, "z", n_z, self.next)
+
+        def step(self, *before):
+            other = after(self.pending, *before)
+            self.line = (self.kept.astype(F32) + other.astype(F32)).astype(BF)
+            self.next *= 2
+            self.send()
+            return self.line
+
+        def finish(self, *before):
+            while self.next < n_z:
+                self.step(*before)
+            return self.line[0]
+
     def gather_dp(line):
         return lax.all_gather(line, "dp", axis=0, tiled=True)
 
@@ -442,20 +494,6 @@
     def reduce_dp(part):
         return lax.psum_scatter(part, "dp", scatter_dimension=0, tiled=True)
 
-    def reduce_line(part):
-        line = part.reshape(n_z, -1, part.shape[1])
-
-        def at(index):
-            return lax.dynamic_index_in_dim(line, index, 0, keepdims=False)
-
-        others = [shift_z(at((z_index + k) % n_z), k) for k in range(1, n_z)]
-
-        def arrive(*before):
-            parts = [at(z_index)] + [after(other, *before) for other in others]
-            return tree([v.astype(F32) for v in parts])
-
-        return arrive
-
     def by_core(mine, other, axis):
         first = jnp.where(core == 0, mine, other)
         second = jnp.where(core == 0, other, mine)
@@ -535,16 +573,17 @@
     text_part = grad_of(text_left, text_right)
     text_sum = lax.psum_scatter(text_part, ("dp", "z"), scatter_dimension=0, tiled=True)
     joint_near = gather_all(joint_weight)(text_part)
-    joint_line = getattr(joint_near, "line", text_part)
+    joint_early = getattr(joint_near, "line", text_part)
     first_shard = jnp.concatenate([gate_up_shard, core_columns(after(mixer_weight, mods))], axis=1)
-    first_line = gather_line(after(first_shard, joint_line))
+    first_line = Gather(after(first_shard, joint_early))
+    first_early = first_line.step()
 
     pad = ((0, slots - rows), (0, 0))
     xfloat = jnp.pad(tokens[0], pad).astype(F32)
     upstream = jnp.pad(cotangent[0], pad).astype(F32)
     normed_in, normed_pull = jax.vjp(modulate, xfloat, gain[0], scale_a, shift_a)
     normed_low = normed_in.astype(BF)
-    joint_full = joint_near(normed_low)
+    joint_full = joint_near(normed_low, first_early)
     joint = product(normed_low, joint_full)
     def to_groups(parts):
         count = parts[0].shape[0]
@@ -579,11 +618,13 @@
         return [exchange(v.reshape(n_seq, half_slots, -1)) for v in arrays]
 
     sent = simple_call(group_kernel, head_arrays(6), "group_heads", joint, rope_gains, cosine, sine)
-    first_line = first_line(sent[0])
+    sent = list(sent)
+    first_line = first_line.finish(joint)
+    sent[0] = after(sent[0], first_line)
     split_at = gate_up_shard.shape[1]
     mixer_half = gather_dp(first_line[:, split_at:])
     gate_up_half = gather_dp(first_line[:, :split_at])
-    down_line = gather_line(after(down_weight, first_line))
+    down_line = Gather(after(down_weight, first_line))
     text_raw = own_rows(after(text_sum, sent[0]))
     text_rows = text_raw.shape[0]
     text_keys, text_key_pull = jax.vjp(norm_rows, text_raw[:, :WIDTH], gain[6])
@@ -591,9 +632,10 @@
         to_groups([text_keys.astype(BF), text_raw[:, WIDTH:].astype(BF)])
     ).reshape(n_seq * text_rows, 2 * wide)
 
+    sent[1] = after(sent[1], text_own)
     qkv = exchange_heads(sent)
     mixer_full = by_core(mixer_half, swap(mixer_half, "core", n_core, 1), 1)
-    down_half = gather_dp(down_line(qkv[0]))
+    down_half = gather_dp(down_line.finish(qkv[0]))
     slot = jnp.arange(n_seq * slots)
     side, line = slot // (n_seq * half_slots), slot % (n_seq * half_slots)
     within = side * half_slots + line % half_slots
@@ -653,9 +695,13 @@
         )
         for i in range(heads)
     ])
+    grads = list(grads)
+    down_sum = Reduce(down_part)
+    grads[0] = after(grads[0], down_sum.step())
+    down_out = down_sum.finish()
+    grads[-2] = after(grads[-2], down_out)
+    down_out = down_out.astype(F32)
     grouped = exchange_back(grads)
-    down_line = reduce_line(after(down_part, grads[0]))
-    mixer_line = reduce_line(after(mixer_part, grads[-1]))
     joint_low, rope_gain_grads = simple_call(
         functools.partial(ungroup_kernel, heads),
         [jax.ShapeDtypeStruct((slots, 3 * WIDTH), BF), jax.ShapeDtypeStruct((2, WIDTH), F32)],
@@ -664,22 +710,12 @@
     joint_left, joint_right = column_split(normed_low, joint_low)
     piece = joint_right.shape[1] // 2
     joint_parts = [grad_of(joint_left, joint_right[:, p * piece : (p + 1) * piece]) for p in range(2)]
-    joint_lines = [
-        reduce_line(reduce_dp(after(part, gate_up_part, mixer_part))) for part in joint_parts
-    ]
-    later_low = after(joint_low, *joint_parts)
+    joint_parts = [reduce_dp(after(part, gate_up_part, mixer_part)) for part in joint_parts]
+    gate_up_sum = Reduce(gate_up_part)
+    later_low = after(joint_low, gate_up_sum.step(joint_low))
     input_part, gain0_grad, scale_a_grad, shift_a_grad = normed_pull(
         contract(later_low, joint_full, 1, 1)
     )
-    gate_up_line = reduce_line(after(gate_up_part, later_low))
-    down_out = down_line(later_low)
-    mixer_out = own_rows(mixer_line(later_low))
-    joint_out = own_rows(jnp.concatenate([arrive(input_part) for arrive in joint_lines], axis=1))
-    kept, received = [
-        v.reshape(shard_rows, 2 * unit_blocks, 1, own_units)
-        for v in trade(gate_up_line(input_part).astype(BF))
-    ]
-    gate_up_out = by_core(kept, received, 2).reshape(shard_rows, -1).astype(F32)
     tokens_grad = (state_grad + input_part).astype(BF)[None, :rows]
     dtext = jnp.concatenate([v[:, :HEAD_DIM] for v in dtexts] + [v[:, HEAD_DIM:] for v in dtexts], axis=1)
     text_back = exchange(dtext.reshape(n_seq, text_rows, 2 * wide))
@@ -687,8 +723,8 @@
     text_grad_rows = jnp.concatenate(
         [text_key_grad.astype(BF), from_groups(text_back[:, :, wide:])], axis=1
     )
-    text_grad_all = lax.all_gather(after(text_grad_rows, *joint_parts), everyone, axis=0, tiled=True)
-    text_grad = contract(flat_text, text_grad_all, 0, 0)
+    text_grad_all = lax.all_gather(after(text_grad_rows, joint_low), everyone, axis=0, tiled=True)
+    text_grad = contract(flat_text, after(text_grad_all, joint_parts[1]), 0, 0)
 
     gates_own = jnp.concatenate([jnp.sum(v, axis=1) for v in dgates]) * (1.0 - own_gates * own_gates)
     gates_all = lax.dynamic_update_slice_in_dim(jnp.zeros((WIDTH,), F32), gates_own, first_head, 0)[None, :]
@@ -700,8 +736,19 @@
     tail = simple_call(
         pack_kernel, jax.ShapeDtypeStruct((-(-len(tail) // 8) * 8, WIDTH), F32), "pack_rows", *tail
     )
-    tail = sum_over(sum_over(tail, "core", n_core), "z", n_z)
-    tails = [tail] + [swap(tail, "dp", n_dp, k) for k in range(1, n_dp)]
+    gate_up_sum = gate_up_sum.finish(tail)
+    joint_sums = [Reduce(after(part, tail)) for part in joint_parts]
+    tails = [after(double(double(tail, "core", n_core), "z", n_z), gate_up_sum, joint_sums[0].step())]
+    kept, received = [
+        v.reshape(shard_rows, 2 * unit_blocks, 1, own_units)
+        for v in trade(gate_up_sum)
+    ]
+    gate_up_out = by_core(kept, received, 2).reshape(shard_rows, -1).astype(F32)
+    joint_sums = [part.finish(tails[0]) for part in joint_sums]
+    joint_out = own_rows(jnp.concatenate(joint_sums, axis=1))
+    mixer_out = own_rows(Reduce(after(mixer_part, tails[0])).finish())
+    while len(tails) < n_dp:
+        tails += list(swap(jnp.stack(tails), "dp", n_dp, len(tails)))
     count = len(pieces)
     total = tree([t[count:] for t in tails])
     gates_grad = total[gain_rows, :HEADS]

time: 946 us -> 895 us (0.946)
  starting transfers between devices: 126 us -> 92.2 us
  blocking collectives: 31.7 us -> 42.4 us
    ppermute x38 -> x50, waiting for transfers between devices: 71.9 us -> 249 us  [swap(): return lax.ppermute(v, axis, [(i, i ^ k) for i in range(n)])]
    ppermute x24 -> x3, waiting for transfers between devices: 144 us -> 0.01 us  [shift_z(): return lax.ppermute(v, 'z', [(i, (i + k) % n_z) for i in range(n_z)])]
    all_to_all x12 -> x11, waiting for transfers between devices: 105 us -> 61.6 us  [exchange(): return lax.all_to_all(v, seq, 0, 0, tiled=True)]
    ppermute x24 -> x3, starting transfers between devices: 40.4 us -> 7.26 us  [shift_z(): return lax.ppermute(v, 'z', [(i, (i + k) % n_z) for i in range(n_z)])]
    all_to_all x2 -> x3, blocking collectives: 31.7 us -> 42.4 us  [exchange(): return lax.all_to_all(v, seq, 0, 0, tiled=True)]
    all_to_all x12 -> x11, starting transfers between devices: 51.4 us -> 45.2 us  [exchange(): return lax.all_to_all(v, seq, 0, 0, tiled=True)]
    ppermute x38 -> x50, starting transfers between devices: 33 us -> 39 us  [swap(): return lax.ppermute(v, axis, [(i, i ^ k) for i in range(n)])]
  transfers between devices with their start and end apart: 84 -> 74, of which waited for: 35 -> 36; matrix products, arithmetic and copies ran while one was open for 27% -> 27% of each run, Pallas kernels for 15% -> 16%
where the time goes in v3:
time: 895 us; the launch traced here: 885 us
  waiting for transfers between devices  319 us (36%)
  Pallas kernels  143 us (16%)
  matrix products  120 us (13%)
  local copies, waits for them, and re-layouts  94.8 us (11%)
  starting transfers between devices  92.2 us (10%)
  other arithmetic  54.7 us (6%)
  blocking collectives  42.4 us (5%)
  between operations  19 us (2%)
    ppermute x50, waiting for transfers between devices, swap(): return lax.ppermute(v, axis, [(i, i ^ k) for i in range(n)])  249 us
    dot_general x12, matrix products, contract(): lax.dot_general(left, right, (((left_dim,), (right_dim,)), ((), ())), pre...  91.3 us
    pallas_call x3, Pallas kernels, attend_backward(): pl.pallas_call(functools.partial(attend_backward_kernel, index), grid=(ha...  71.8 us
    all_to_all x11, waiting for transfers between devices, exchange(): return lax.all_to_all(v, seq, 0, 0, tiled=True)  61.6 us
    pallas_call x3, Pallas kernels, attend_forward(): pl.pallas_call(functools.partial(attend_forward_kernel, index), grid=(hal...  47.6 us
    all_to_all x11, starting transfers between devices, exchange(): return lax.all_to_all(v, seq, 0, 0, tiled=True)  45.2 us
    all_to_all x3, blocking collectives, exchange(): return lax.all_to_all(v, seq, 0, 0, tiled=True)  42.4 us
    ppermute x50, starting transfers between devices, swap(): return lax.ppermute(v, axis, [(i, i ^ k) for i in range(n)])  39 us
  transfers between devices with their start and end apart: 74, of which 36 were waited for; matrix products, arithmetic and copies ran while one was open for 27% of the time, Pallas kernels for 16%

profile of v3, /device:TPU:0, one launch (start us, length us, event | category | flops | bytes accessed | tf_op | source)
XLA Modules:
  0.0 884.9 jit_solution(184425481571832120)
XLA Ops:
  39.1 17.9 %collective-permute-done.4 = f32[1,19968]{1,0:T(1,128)S(1)} collective-permute-done((f32[1,19968]{1,0:T(1,128)S(1)}, f32[1,19968]{1,0:T(1,128)S(1)}, u32[]{:S(2)}, u32[]{:S(2)}) %collective-permute-start.4) | collective-permute-done | bytes 79904 | tf_op jit(solution)/shard_map/ppermute | solution.py:363
  80.4 40.7 %collective-permute-done.14 = bf16[1,96,4864]{2,1,0:T(8,128)(2,1)S(1)} collective-permute-done((bf16[1,96,4864]{2,1,0:T(8,128)(2,1)S(1)}, bf16[1,96,4864]{2,1,0:T(8,128)(2,1)S(1)}, u32[]{:S(2)}, u32[]{:S(2)}) %collective-permute-start.14) | collective-permute-done | bytes 933920 | tf_op jit(solution)/shard_map/ppermute | solution.py:363
  130.0 19.8 %collective-permute-done.18 = bf16[96,4608]{1,0:T(8,128)(2,1)S(1)} collective-permute-done((bf16[96,4608]{1,0:T(8,128)(2,1)S(1)}, bf16[96,4608]{1,0:T(8,128)(2,1)S(1)}, u32[]{:S(2)}, u32[]{:S(2)}) %collective-permute-start.18) | collective-permute-done | bytes 884768 | tf_op jit(solution)/shard_map/ppermute | solution.py:363
  160.4 9.3 %collective-permute-done.22 = bf16[2,96,4864]{2,1,0:T(8,128)(2,1)S(1)} collective-permute-done((bf16[2,96,4864]{2,1,0:T(8,128)(2,1)S(1)}, bf16[2,96,4864]{2,1,0:T(8,128)(2,1)S(1)}, u32[]{:S(2)}, u32[]{:S(2)}) %collective-permute-start.22) | collective-permute-done | bytes 1867808 | tf_op jit(solution)/shard_map/ppermute | solution.py:363
  178.9 7.8 group_heads.1
  202.6 31.0 %collective-permute-done.26 = bf16[1,128,1536]{2,1,0:T(8,128)(2,1)S(1)} collective-permute-done((bf16[1,128,1536]{2,1,0:T(8,128)(2,1)S(1)}, bf16[1,128,1536]{2,1,0:T(8,128)(2,1)S(1)}, u32[]{:S(2)}, u32[]{:S(2)}) %collective-permute-start.26) | collective-permute-done | bytes 393248 | tf_op jit(solution)/shard_map/ppermute | solution.py:363
  243.3 15.3 %collective-permute-done.27 = bf16[2,128,1536]{2,1,0:T(8,128)(2,1)} collective-permute-done((bf16[2,128,1536]{2,1,0:T(8,128)(2,1)}, bf16[2,128,1536]{2,1,0:T(8,128)(2,1)}, u32[]{:S(2)}, u32[]{:S(2)}) %collective-permute-start.27) | collective-permute-done | bytes 786464 | tf_op jit(solution)/shard_map/ppermute | solution.py:363
  268.2 15.8 %attend_forward.3 = (bf16[1216,128]{1,0:T(8,128)(2,1)}, f32[1216,128]{1,0:T(8,128)}, f32[1216,128]{1,0:T(8,128)}, f32[1216,4]{1,0:T(8,128)}) custom-call(bf16[1216,384]{1,0:T(8,128)(2,1)} %bitcast.222, bf16[256,384]{1,0:T(8,128)(2,1)} %bitcast.25.text_ref, bf16[2432,1]{1,0:T(8,128)(2,1)} %select_convert_fusion.bias_ref, ...), custom_call_target="tpu_custom_call" | custom-call | flops 6694109184 | bytes 2801664 | tf_op jit(solution)/shard_map/attend_forward/pallas_call | solution.py:188
  291.0 10.7 %all-to-all-done.2.refs_0_ = bf16[8,152,128]{2,1,0:T(8,128)(2,1)S(1)} async-done(((bf16[8,152,128]{2,1,0:T(8,128)(2,1)}), bf16[8,152,128]{2,1,0:T(8,128)(2,1)S(1)}, u32[]{:S(2)}, u32[]{:S(2)}) %all-to-all-start.2) | async-done | bytes 311328 | tf_op jit(solution)/shard_map/all_to_all | solution.py:601
  306.9 15.8 %attend_forward.5 = (bf16[1216,128]{1,0:T(8,128)(2,1)}, f32[1216,128]{1,0:T(8,128)}, f32[1216,128]{1,0:T(8,128)}, f32[1216,4]{1,0:T(8,128)}) custom-call(bf16[1216,384]{1,0:T(8,128)(2,1)} %bitcast.33.qkv_ref.q_ref, bf16[256,384]{1,0:T(8,128)(2,1)} %bitcast.25.text_ref, bf16[2432,1]{1,0:T(8,128)(2,1)} %select_convert_fusion.bias_ref, ...), custom_call_target="tpu_custom_call" | custom-call | flops 6694109184 | bytes 2801664 | tf_op jit(solution)/shard_map/attend_forward/pallas_call | solution.py:188
  334.2 15.9 %attend_forward.4 = (bf16[1216,128]{1,0:T(8,128)(2,1)}, f32[1216,128]{1,0:T(8,128)}, f32[1216,128]{1,0:T(8,128)}, f32[1216,4]{1,0:T(8,128)}) custom-call(bf16[1216,384]{1,0:T(8,128)(2,1)} %bitcast.226, bf16[256,384]{1,0:T(8,128)(2,1)} %bitcast.25.text_ref, bf16[2432,1]{1,0:T(8,128)(2,1)} %select_convert_fusion.bias_ref, ...), custom_call_target="tpu_custom_call" | custom-call | flops 6694109184 | bytes 2801664 | tf_op jit(solution)/shard_map/attend_forward/pallas_call | solution.py:188
  350.1 16.2 %all_to_all.70.refs_1_ = bf16[8,152,128]{2,1,0:T(8,128)(2,1)} all-to-all(bf16[8,152,128]{2,1,0:T(8,128)(2,1)} %bitcast.252), channel_id=1, replica_groups=mesh['dp'=4,'z'=4,'core'=2] {'z','core'}, dimensions={0} | all-to-all | bytes 622592 | tf_op jit(solution)/shard_map/all_to_all | solution.py:601
  380.5 11.5 %fusion.48 = f32[608,4096]{1,0:T(8,128)S(1)} fusion(bf16[1536,4096]{1,0:T(8,128)(2,1)} %all-gather.7.cloned.1.call-done, bf16[304,1536]{1,0:T(8,128)(2,1)} %collective-permute-done.25, bf16[304,1536]{1,0:T(8,128)(2,1)} %copy-done.37), kind=kOutput, calls=%fused_computation.111 | convolution fusion | flops 7654146048 | bytes 24412160 | tf_op jit(solution)/shard_map/dot_general | solution.py:42
  398.3 7.0 all-gather.9.cloned.1.call-done
  423.5 7.4 convolution_convert_fusion.3
  431.0 15.4 %fusion.57 = (f32[608,2048]{1,0:T(8,128)}, f32[608,2048]{1,0:T(8,128)}) fusion(f32[608,4096]{1,0:T(8,128)} %copy-done.11, bf16[2048,1536]{1,0:T(8,128)(2,1)} %all-gather.9.cloned.1.call-done, bf16[304,1536]{1,0:T(8,128)(2,1)} %copy-done.80, bf16[304,1536]{1,0:T(8,128)(2,1)} %copy-done.39), kind=kOutput, calls=%fused_computation.133 | convolution fusion | flops 3843883008 | bytes 28082176 | tf_op jit(solution)/shard_map/dot_general | solution.py:46
  453.4 13.4 %fusion.122 = f32[608,1536]{1,0:T(8,128)S(1)} fusion(bf16[608,4096]{1,0:T(8,128)(2,1)} %add_convert_fusion, bf16[1536,4096]{1,0:T(8,128)(2,1)} %all-gather.7.cloned.1.call-done), kind=kOutput, calls=%fused_computation.324 | convolution fusion | flops 7650410496 | bytes 21299200 | tf_op jit(solution)/shard_map/dot_general | solution.py:46
  470.5 13.6 %convolution_convert_fusion = bf16[1536,4096]{1,0:T(8,128)(2,1)} fusion(bf16[608,4096]{1,0:T(8,128)(2,1)S(1)} %copy-done.17, bf16[304,1536]{1,0:T(8,128)(2,1)} %collective-permute-done.25, bf16[304,1536]{1,0:T(8,128)(2,1)S(1)} %copy-done.38), kind=kOutput, calls=%fused_computation | convolution fusion | flops 7660437504 | bytes 19431424 | tf_op jit(solution)/shard_map/dot_general | solution.py:46
  504.2 15.5 %all_to_all.71 = bf16[8,152,128]{2,1,0:T(8,128)(2,1)} all-to-all(bf16[8,152,128]{2,1,0:T(8,128)(2,1)} %get-tuple-element.106), channel_id=1, replica_groups=mesh['dp'=4,'z'=4,'core'=2] {'z','core'}, dimensions={0} | all-to-all | bytes 622592 | tf_op jit(solution)/shard_map/all_to_all | solution.py:601
  526.6 7.5 all-to-all-done.11
  538.2 23.7 %attend_backward.5 = (bf16[1216,384]{1,0:T(8,128)(2,1)}, bf16[256,128]{1,0:T(8,128)(2,1)}, f32[1,64]{1,0:T(1,128)}) custom-call(bf16[1216,384]{1,0:T(8,128)(2,1)} %bitcast.33.qkv_ref.q_ref, bf16[256,384]{1,0:T(8,128)(2,1)} %bitcast.25.text_ref, bf16[2432,1]{1,0:T(8,128)(2,1)} %select_convert_fusion.bias_ref, ...), custom_call_target="tpu_custom_call" | custom-call | flops 16735272960 | bytes 4046848 | tf_op jit(solution)/shard_map/attend_backward/pallas_call | solution.py:213
  566.9 24.1 %attend_backward.3 = (bf16[1216,384]{1,0:T(8,128)(2,1)}, bf16[256,128]{1,0:T(8,128)(2,1)}, f32[1,64]{1,0:T(1,128)}) custom-call(bf16[1216,384]{1,0:T(8,128)(2,1)} %bitcast.224, bf16[256,384]{1,0:T(8,128)(2,1)} %bitcast.25.text_ref, bf16[2432,1]{1,0:T(8,128)(2,1)} %select_convert_fusion.bias_ref, bf16[256,1]{1,0:T(8,128)(2,1)} %select_convert_fusion.1.text_bias_ref, ...), custom_call_target="tpu_custom_call" | custom-call | flops 16735272960 | bytes 4046848 | tf_op jit(solution)/shard_map/attend_backward/pallas_call | solution.py:213
  600.2 24.0 %attend_backward.4 = (bf16[1216,384]{1,0:T(8,128)(2,1)}, bf16[256,128]{1,0:T(8,128)(2,1)}, f32[1,64]{1,0:T(1,128)}) custom-call(bf16[1216,384]{1,0:T(8,128)(2,1)} %bitcast.228, bf16[256,384]{1,0:T(8,128)(2,1)} %bitcast.25.text_ref, bf16[2432,1]{1,0:T(8,128)(2,1)} %select_convert_fusion.bias_ref, bf16[256,1]{1,0:T(8,128)(2,1)} %select_convert_fusion.1.text_bias_ref, ...), custom_call_target="tpu_custom_call" | custom-call | flops 16735272960 | bytes 4046848 | tf_op jit(solution)/shard_map/attend_backward/pallas_call | solution.py:213
  625.6 8.3 all-to-all-done.8.refs_0_
  638.7 24.2 %all-to-all-done.10.refs_1_ = bf16[8,152,384]{2,1,0:T(8,128)(2,1)} async-done(((bf16[8,152,384]{2,1,0:T(8,128)(2,1)}), bf16[8,152,384]{2,1,0:T(8,128)(2,1)}, u32[]{:S(2)}, u32[]{:S(2)}) %all-to-all-start.10) | async-done | bytes 933920 | tf_op jit(solution)/shard_map/all_to_all | solution.py:601
  662.9 9.1 %ungroup_heads.1 = (bf16[304,4608]{1,0:T(8,128)(2,1)}, f32[2,1536]{1,0:T(2,128)}) custom-call(bf16[8,152,384]{2,1,0:T(8,128)(2,1)} %all-to-all-done.8.refs_0_, bf16[8,152,384]{2,1,0:T(8,128)(2,1)} %all-to-all-done.10.refs_1_, bf16[8,152,384]{2,1,0:T(8,128)(2,1)} %all-to-all-done.12.refs_2_, f32[304,4608]{1,0:T(8,128)} %fusion.120.joint_ref.refs_3_, ...), custom_call_target="tpu_custom_call" | custom-call | flops 69828608 | bytes 11542528 | tf_op jit(solution)/shard_map/ungroup_heads/pallas_call | solution.py:318
  693.3 10.7 %all_to_all.72 = bf16[8,32,384]{2,1,0:T(8,128)(2,1)S(1)} all-to-all(bf16[8,32,384]{2,1,0:T(8,128)(2,1)S(1)} %bitcast.241), channel_id=1, replica_groups=mesh['dp'=4,'z'=4,'core'=2] {'z','core'}, dimensions={0} | all-to-all | bytes 393216 | tf_op jit(solution)/shard_map/all_to_all | solution.py:601
  720.1 36.4 %collective-permute-done.35 = bf16[2,96,4096]{2,1,0:T(8,128)(2,1)} collective-permute-done((bf16[2,96,4096]{2,1,0:T(8,128)(2,1)}, bf16[2,96,4096]{2,1,0:T(8,128)(2,1)}, u32[]{:S(2)}, u32[]{:S(2)}) %collective-permute-start.35) | collective-permute-done | bytes 1572896 | tf_op jit(solution)/shard_map/ppermute | solution.py:363
  760.3 12.4 %multiply_reduce_fusion.2 = (f32[1536]{0:T(1024)S(1)}, f32[1536]{0:T(1024)S(1)}, f32[1536]{0:T(1024)S(1)}, f32[304]{0:T(512)S(1)}, f32[304,1536]{1,0:T(8,128)}) fusion(f32[1536]{0:T(1024)S(1)} %copy-done.58, f32[304]{0:T(512)S(1)} %copy-done.67, bf16[294,1536]{1,0:T(8,128)(2,1)S(1)} %bitcast.198, f32[1536]{0:T(1024)S(1)} %copy-done.60, ...), kind=kOutput, calls=%fused_computation.58 | convolution fusion | flops 4308954112 | bytes 19761536 | tf_op jit(solution)/shard_map/dot_general | solution.py:46
  782.4 16.3 %collective-permute-done.41 = f32[16,1536]{1,0:T(8,128)S(1)} collective-permute-done((f32[16,1536]{1,0:T(8,128)S(1)}, f32[16,1536]{1,0:T(8,128)S(1)}, u32[]{:S(2)}, u32[]{:S(2)}) %collective-permute-start.41) | collective-permute-done | bytes 98336 | tf_op jit(solution)/shard_map/ppermute | solution.py:363
  802.3 15.2 %collective-permute-done.49 = bf16[1,96,4096]{2,1,0:T(8,128)(2,1)S(1)} collective-permute-done((bf16[1,96,4096]{2,1,0:T(8,128)(2,1)S(1)}, bf16[1,96,4096]{2,1,0:T(8,128)(2,1)S(1)}, u32[]{:S(2)}, u32[]{:S(2)}) %collective-permute-start.49) | collective-permute-done | bytes 786464 | tf_op jit(solution)/shard_map/ppermute | solution.py:363
  841.0 11.2 %collective-permute-done.43 = bf16[2,96,1152]{2,1,0:T(8,128)(2,1)S(1)} collective-permute-done((bf16[2,96,1152]{2,1,0:T(8,128)(2,1)}, bf16[2,96,1152]{2,1,0:T(8,128)(2,1)S(1)}, u32[]{:S(2)}, u32[]{:S(2)}) %collective-permute-start.43) | collective-permute-done | bytes 442400 | tf_op jit(solution)/shard_map/ppermute | solution.py:363
  (524 shorter events, 342.9 us)
Async XLA Ops:
  8.0 225.6 %reduce-scatter.7.cloned.1.call-start = ((), (), s32[]{:S(2)}) async-start(), calls=%async_computation.20 | async-start | bytes 3342336 | tf_op jit(solution)/shard_map/reduce_scatter | solution.py:574
  8.1 49.1 %collective-permute-start.6 = (bf16[48,4608]{1,0:T(8,128)(2,1)}, bf16[48,4608]{1,0:T(8,128)(2,1)}, u32[]{:S(2)}, u32[]{:S(2)}) collective-permute-start(bf16[48,4608]{1,0:T(8,128)(2,1)} %param.21), channel_id=1, source_target_pairs={{0,2},{2,4},{4,6},{6,0},{1,3},{3,5},{5,7},{7,1},{8,10},{10,12},{12... | collective-permute-start | bytes 1327112 | tf_op jit(solution)/shard_map/ppermute | solution.py:391
  11.2 46.0 %collective-permute-start.8 = (bf16[48,4608]{1,0:T(8,128)(2,1)}, bf16[48,4608]{1,0:T(8,128)(2,1)}, u32[]{:S(2)}, u32[]{:S(2)}) collective-permute-start(bf16[48,4608]{1,0:T(8,128)(2,1)} %param.21), channel_id=1, source_target_pairs={{0,4},{2,6},{4,0},{6,2},{1,5},{3,7},{5,1},{7,3},{8,12},{10,14},{12... | collective-permute-start | bytes 1327112 | tf_op jit(solution)/shard_map/ppermute | solution.py:391
  32.9 28.0 %collective-permute-start.9 = (bf16[48,4608]{1,0:T(8,128)(2,1)}, bf16[48,4608]{1,0:T(8,128)(2,1)S(1)}, u32[]{:S(2)}, u32[]{:S(2)}) collective-permute-start(bf16[48,4608]{1,0:T(8,128)(2,1)} %param.21), channel_id=1, source_target_pairs={{0,6},{2,0},{4,2},{6,4},{1,7},{3,1},{5,3},{7,5},{8,14},{10,8},{12,... | collective-permute-start | bytes 1327112 | tf_op jit(solution)/shard_map/ppermute | solution.py:391
  38.9 266.4 %all-gather.5.cloned.1.call-start = ((), (), s32[]{:S(2)}) async-start(), calls=%async_computation.21 | async-start | bytes 2949120 | tf_op jit(solution)/shard_map/all_gather | solution.py:461
  66.4 59.5 %collective-permute-start.10 = (bf16[192,4608]{1,0:T(8,128)(2,1)}, bf16[192,4608]{1,0:T(8,128)(2,1)}, u32[]{:S(2)}, u32[]{:S(2)}) collective-permute-start(bf16[192,4608]{1,0:T(8,128)(2,1)} %bitcast.8), channel_id=1, source_target_pairs={{0,1},{1,0},{2,3},{3,2},{4,5},{5,4},{6,7},{7,6},{8,9},{9,8},{10,11... | collective-permute-start | bytes 5308424 | tf_op jit(solution)/shard_map/ppermute | solution.py:363
  66.5 54.9 %collective-permute-start.11 = (bf16[192,4608]{1,0:T(8,128)(2,1)}, bf16[192,4608]{1,0:T(8,128)(2,1)}, u32[]{:S(2)}, u32[]{:S(2)}) collective-permute-start(bf16[192,4608]{1,0:T(8,128)(2,1)} %bitcast.8), channel_id=1, source_target_pairs={{0,8},{8,0},{16,24},{24,16},{1,9},{9,1},{17,25},{25,17},{2,10},{10... | collective-permute-start | bytes 5308424 | tf_op jit(solution)/shard_map/ppermute | solution.py:363
  68.0 53.9 %collective-permute-start.16 = (bf16[192,4608]{1,0:T(8,128)(2,1)}, bf16[192,4608]{1,0:T(8,128)(2,1)}, u32[]{:S(2)}, u32[]{:S(2)}) collective-permute-start(bf16[192,4608]{1,0:T(8,128)(2,1)} %bitcast.8), channel_id=1, source_target_pairs={{0,16},{8,24},{16,0},{24,8},{1,17},{9,25},{17,1},{25,9},{2,18},{10... | collective-permute-start | bytes 5308424 | tf_op jit(solution)/shard_map/ppermute | solution.py:363
  70.2 50.9 %collective-permute-start.14 = (bf16[1,96,4864]{2,1,0:T(8,128)(2,1)S(1)}, bf16[1,96,4864]{2,1,0:T(8,128)(2,1)S(1)}, u32[]{:S(2)}, u32[]{:S(2)}) collective-permute-start(bf16[1,96,4864]{2,1,0:T(8,128)(2,1)S(1)} %bitcast.201), channel_id=1, source_target_pairs={{0,4},{2,6},{4,0},{6,2},{1,5},{3,7},{5,1},{7,3},{8,12},{10,14},{12... | collective-permute-start | bytes 2801672 | tf_op jit(solution)/shard_map/ppermute | solution.py:363
  121.3 28.9 %collective-permute-start.15 = (bf16[192,4608]{1,0:T(8,128)(2,1)}, bf16[192,4608]{1,0:T(8,128)(2,1)S(1)}, u32[]{:S(2)}, u32[]{:S(2)}) collective-permute-start(bf16[192,4608]{1,0:T(8,128)(2,1)} %collective-permute-done.11), channel_id=1, source_target_pairs={{0,1},{1,0},{2,3},{3,2},{4,5},{5,4},{6,7},{7,6},{8,9},{9,8},{10,11... | collective-permute-start | bytes 5308424 | tf_op jit(solution)/shard_map/ppermute | solution.py:363
  121.9 47.8 %collective-permute-start.22 = (bf16[2,96,4864]{2,1,0:T(8,128)(2,1)S(1)}, bf16[2,96,4864]{2,1,0:T(8,128)(2,1)S(1)}, u32[]{:S(2)}, u32[]{:S(2)}) collective-permute-start(bf16[2,96,4864]{2,1,0:T(8,128)(2,1)S(1)} %pad_maximum_fusion.5), channel_id=1, source_target_pairs={{0,2},{2,0},{4,6},{6,4},{1,3},{3,1},{5,7},{7,5},{8,10},{10,8},{12,... | collective-permute-start | bytes 5603336 | tf_op jit(solution)/shard_map/ppermute | solution.py:363
  121.9 30.2 %collective-permute-start.17 = (bf16[192,4608]{1,0:T(8,128)(2,1)}, bf16[192,4608]{1,0:T(8,128)(2,1)S(1)}, u32[]{:S(2)}, u32[]{:S(2)}) collective-permute-start(bf16[192,4608]{1,0:T(8,128)(2,1)} %collective-permute-done.16), channel_id=1, source_target_pairs={{0,1},{1,0},{2,3},{3,2},{4,5},{5,4},{6,7},{7,6},{8,9},{9,8},{10,11... | collective-permute-start | bytes 5308424 | tf_op jit(solution)/shard_map/ppermute | solution.py:363
  172.7 207.8 %all-gather.7.cloned.1.call-start = ((), (), s32[]{:S(2)}) async-start(), calls=%async_computation.22 | async-start | bytes 15728640 | tf_op jit(solution)/shard_map/all_gather | solution.py:461
  186.7 46.9 %all-to-all-start = ((bf16[8,152,384]{2,1,0:T(8,128)(2,1)}), bf16[8,152,384]{2,1,0:T(8,128)(2,1)S(1)}, u32[]{:S(2)}, u32[]{:S(2)}) async-start(bf16[8,152,384]{2,1,0:T(8,128)(2,1)} %get-tuple-element.93), calls=%async_computation | async-start | bytes 1867776 | tf_op jit(solution)/shard_map/all_to_all | solution.py:601
  196.0 37.6 %collective-permute-start.26 = (bf16[1,128,1536]{2,1,0:T(8,128)(2,1)S(1)}, bf16[1,128,1536]{2,1,0:T(8,128)(2,1)S(1)}, u32[]{:S(2)}, u32[]{:S(2)}) collective-permute-start(bf16[1,128,1536]{2,1,0:T(8,128)(2,1)S(1)} %bitcast.213), channel_id=1, source_target_pairs={{0,4},{2,6},{4,0},{6,2},{1,5},{3,7},{5,1},{7,3},{8,12},{10,14},{12... | collective-permute-start | bytes 1179656 | tf_op jit(solution)/shard_map/ppermute | solution.py:363
  259.2 28.4 %all-to-all-start.5 = ((bf16[8,152,384]{2,1,0:T(8,128)(2,1)}), bf16[8,152,384]{2,1,0:T(8,128)(2,1)}, u32[]{:S(2)}, u32[]{:S(2)}) async-start(bf16[8,152,384]{2,1,0:T(8,128)(2,1)} %get-tuple-element.99), calls=%async_computation.6 | async-start | bytes 1867776 | tf_op jit(solution)/shard_map/all_to_all | solution.py:601
  263.4 141.9 %all-gather.9.cloned.1.call-start = ((), (), s32[]{:S(2)}) async-start(), calls=%async_computation.23 | async-start | bytes 7864320 | tf_op jit(solution)/shard_map/all_gather | solution.py:461
  305.3 63.6 %collective-permute-start.24 = (bf16[1536,768]{1,0:T(8,128)(2,1)}, bf16[1536,768]{1,0:T(8,128)(2,1)}, u32[]{:S(2)}, u32[]{:S(2)}) collective-permute-start(bf16[1536,768]{1,0:T(8,128)(2,1)} %all-gather.5.cloned.1.call-done), channel_id=1, source_target_pairs={{0,1},{1,0},{2,3},{3,2},{4,5},{5,4},{6,7},{7,6},{8,9},{9,8},{10,11... | collective-permute-start | bytes 7077896 | tf_op jit(solution)/shard_map/ppermute | solution.py:363
  332.8 190.6 %reduce-scatter.9.cloned.1.call-start = ((), (), s32[]{:S(2)}) async-start(), calls=%async_computation.24 | async-start | bytes 7864320 | tf_op jit(solution)/shard_map/reduce_scatter | solution.py:495
  431.0 254.1 %reduce-scatter.13.cloned.1.call-start = ((), (), s32[]{:S(2)}) async-start(), calls=%async_computation.26 | async-start | bytes 2949120 | tf_op jit(solution)/shard_map/reduce_scatter | solution.py:495
  501.0 184.0 %reduce-scatter.11.cloned.1.call-start = ((), (), s32[]{:S(2)}) async-start(), calls=%async_computation.25 | async-start | bytes 15728640 | tf_op jit(solution)/shard_map/reduce_scatter | solution.py:495
  524.6 66.4 %collective-permute-start.33 = (bf16[2,128,1536]{2,1,0:T(8,128)(2,1)S(1)}, bf16[2,128,1536]{2,1,0:T(8,128)(2,1)}, u32[]{:S(2)}, u32[]{:S(2)}) collective-permute-start(bf16[2,128,1536]{2,1,0:T(8,128)(2,1)S(1)} %dynamic-slice_bitcast_fusion.1), channel_id=1, source_target_pairs={{0,2},{2,0},{4,6},{6,4},{1,3},{3,1},{5,7},{7,5},{8,10},{10,8},{12,... | collective-permute-start | bytes 2359304 | tf_op jit(solution)/shard_map/ppermute | solution.py:363
  534.1 27.7 %all-to-all-start.9 = ((bf16[8,152,128]{2,1,0:T(8,128)(2,1)}), bf16[8,152,128]{2,1,0:T(8,128)(2,1)}, u32[]{:S(2)}, u32[]{:S(2)}) async-start(bf16[8,152,128]{2,1,0:T(8,128)(2,1)} %get-tuple-element.114), calls=%async_computation.11 | async-start | bytes 622592 | tf_op jit(solution)/shard_map/all_to_all | solution.py:601
  561.8 33.9 %all-to-all-start.12 = ((bf16[8,152,384]{2,1,0:T(8,128)(2,1)}), bf16[8,152,384]{2,1,0:T(8,128)(2,1)}, u32[]{:S(2)}, u32[]{:S(2)}) async-start(bf16[8,152,384]{2,1,0:T(8,128)(2,1)} %bitcast.232), calls=%async_computation.14 | async-start | bytes 1867776 | tf_op jit(solution)/shard_map/all_to_all | solution.py:601
  593.1 31.5 %collective-permute-start.34 = (bf16[1,128,1536]{2,1,0:T(8,128)(2,1)}, bf16[1,128,1536]{2,1,0:T(8,128)(2,1)S(1)}, u32[]{:S(2)}, u32[]{:S(2)}) collective-permute-start(bf16[1,128,1536]{2,1,0:T(8,128)(2,1)} %constant_dynamic-slice_fusion.11), channel_id=1, source_target_pairs={{0,4},{2,6},{4,0},{6,2},{1,5},{3,7},{5,1},{7,3},{8,12},{10,14},{12... | collective-permute-start | bytes 1179656 | tf_op jit(solution)/shard_map/ppermute | solution.py:363
  595.8 38.1 %all-to-all-start.8 = ((bf16[8,152,384]{2,1,0:T(8,128)(2,1)}), bf16[8,152,384]{2,1,0:T(8,128)(2,1)}, u32[]{:S(2)}, u32[]{:S(2)}) async-start(bf16[8,152,384]{2,1,0:T(8,128)(2,1)} %bitcast.230), calls=%async_computation.10 | async-start | bytes 1867776 | tf_op jit(solution)/shard_map/all_to_all | solution.py:601
  633.9 29.0 %all-to-all-start.10 = ((bf16[8,152,384]{2,1,0:T(8,128)(2,1)}), bf16[8,152,384]{2,1,0:T(8,128)(2,1)}, u32[]{:S(2)}, u32[]{:S(2)}) async-start(bf16[8,152,384]{2,1,0:T(8,128)(2,1)} %bitcast.231), calls=%async_computation.12 | async-start | bytes 1867776 | tf_op jit(solution)/shard_map/all_to_all | solution.py:601
  638.6 185.1 %reduce-scatter.15.cloned.1.call-start = ((), (), s32[]{:S(2)}) async-start(), calls=%async_computation.27 | async-start | bytes 4423680 | tf_op jit(solution)/shard_map/reduce_scatter | solution.py:495
  685.0 140.5 %reduce-scatter.17.cloned.1.call-start = ((), (), s32[]{:S(2)}) async-start(), calls=%async_computation.28 | async-start | bytes 4423680 | tf_op jit(solution)/shard_map/reduce_scatter | solution.py:495
  692.0 137.4 %all-gather.11.cloned.1.call-start = ((), (), s32[]{:S(2)}) async-start(), calls=%async_computation.29 | async-start | bytes 6488064 | tf_op jit(solution)/shard_map/all_gather | solution.py:726
  708.5 48.0 %collective-permute-start.35 = (bf16[2,96,4096]{2,1,0:T(8,128)(2,1)}, bf16[2,96,4096]{2,1,0:T(8,128)(2,1)}, u32[]{:S(2)}, u32[]{:S(2)}) collective-permute-start(bf16[2,96,4096]{2,1,0:T(8,128)(2,1)} %dynamic-slice_bitcast_fusion), channel_id=1, source_target_pairs={{0,2},{2,0},{4,6},{6,4},{1,3},{3,1},{5,7},{7,5},{8,10},{10,8},{12,... | collective-permute-start | bytes 4718600 | tf_op jit(solution)/shard_map/ppermute | solution.py:363
  777.2 40.3 %collective-permute-start.49 = (bf16[1,96,4096]{2,1,0:T(8,128)(2,1)S(1)}, bf16[1,96,4096]{2,1,0:T(8,128)(2,1)S(1)}, u32[]{:S(2)}, u32[]{:S(2)}) collective-permute-start(bf16[1,96,4096]{2,1,0:T(8,128)(2,1)S(1)} %constant_dynamic-slice_fusion.5), channel_id=1, source_target_pairs={{0,4},{2,6},{4,0},{6,2},{1,5},{3,7},{5,1},{7,3},{8,12},{10,14},{12... | collective-permute-start | bytes 2359304 | tf_op jit(solution)/shard_map/ppermute | solution.py:363
  (128 other events, 2029.4 us)
Sparse Core Ops, SparseCore 0:
  39.0 161.2 reduce-scatter.6
  705.8 76.5 all-gather.10
Sparse Core Ops, SparseCore 1:
  172.8 36.1 all-gather.4
  210.6 122.3 all-gather.6
  335.3 70.0 all-gather.8
  431.0 70.0 reduce-scatter.8
  504.2 37.2 reduce-scatter.12
  544.5 120.5 reduce-scatter.10
  685.1 45.1 reduce-scatter.14
  733.2 49.5 reduce-scatter.16

commit v4 on v3

--- a/solution.py
+++ b/solution.py
@@ -303,6 +303,36 @@
 
 def join_kernel(*refs):
     refs[-1][...] = join_heads(refs[:-1], 0, 1)
+
+
+def swiglu_back_kernel(grad_ref, weight_ref, gate_ref, up_ref, out_ref):
+    size, half = gate_ref.shape[1], out_ref.shape[1] // 2
+    grad = contract(grad_ref[...], weight_ref[...], 1, 1)
+    gate = gate_ref[...]
+    sig = jax.nn.sigmoid(gate)
+    at = pl.multiple_of(pl.program_id(0) * size, size)
+    out_ref[:, pl.ds(at, size)] = (grad * up_ref[...] * (sig * (1.0 + gate * (1.0 - sig)))).astype(BF)
+    out_ref[:, pl.ds(half + at, size)] = (grad * (gate * sig)).astype(BF)
+
+
+def swiglu_back(grad, weight, gate_up):
+    rows, width = grad.shape
+    units = weight.shape[0]
+    size = 2 * LANES
+    count = units // size
+    return pl.pallas_call(
+        swiglu_back_kernel,
+        grid=(count,),
+        in_specs=[
+            whole_block((rows, width)), row_block(size, width),
+            pl.BlockSpec((rows, size), lambda i: (0, i)), pl.BlockSpec((rows, size), lambda i: (0, count + i)),
+        ],
+        out_specs=whole_block((rows, 2 * units)),
+        out_shape=jax.ShapeDtypeStruct((rows, 2 * units), BF),
+        compiler_params=params(),
+        cost_estimate=cost(2 * rows * width * units, rows * units * 12 + units * width * 2, rows * units),
+        name="swiglu_back",
+    )(grad, weight, gate_up, gate_up)
 
 
 def pack_kernel(*refs):
@@ -649,7 +679,7 @@
     own_gates = lax.dynamic_slice_in_dim(jnp.pad(tanh_gates, (0, spare)), first_head, heads, 0)
     gate_rows = [jnp.broadcast_to(own_gates[i : i + 1, None], (1, HEAD_DIM)) for i in range(heads)]
     attended = [
-        attend_forward(qkv[i], text_own, bias, text_bias, gate_rows[i], i, 2 * half_slots)
+        attend_forward(qkv[i], text_own, bias, text_bias, gate_rows[i], i, 4 * half_slots)
         for i in range(heads)
     ]
     token_shape = jax.ShapeDtypeStruct((slots, WIDTH), BF)
@@ -663,16 +693,14 @@
 
     ffn_both = both_cores(ffn_in.astype(BF))
     gate_up = product(ffn_both, gate_up_half)
-    hidden, swiglu_pull = jax.vjp(swiglu, gate_up)
-    hidden_low = hidden.astype(BF)
+    hidden_low = swiglu(gate_up).astype(BF)
     ffn = sum_cores(product(hidden_low, down_half))
     branch_f, branch_f_pull = jax.vjp(branch_out, ffn, gain[3], gate_f)
     output = (hstate + branch_f).astype(BF)[None, :rows]
 
     ffn_grad, gain3_grad, gate_f_grad = branch_f_pull(upstream)
     ffn_grad_both = both_cores(ffn_grad.astype(BF))
-    (gate_up_grad_rows,) = swiglu_pull(contract(ffn_grad_both, down_half, 1, 1))
-    gate_up_low = gate_up_grad_rows.astype(BF)
+    gate_up_low = swiglu_back(ffn_grad_both, down_half, gate_up)
     down_part = grad_of(hidden_low, ffn_grad_both)
     gate_up_part = grad_of(ffn_both, after(gate_up_low, down_part))
     down_part = reduce_dp(down_part)
@@ -691,7 +719,7 @@
     ups[-1] = after(ups[-1], down_part)
     grads, dtexts, dgates = zip(*[
         attend_backward(
-            qkv[i], text_own, bias, text_bias, gate_rows[i], ups[i], *attended[i][1:], i, 2 * half_slots
+            qkv[i], text_own, bias, text_bias, gate_rows[i], ups[i], *attended[i][1:], i, 4 * half_slots
         )
         for i in range(heads)
     ])

time: 895 us -> 889 us (level)
  matrix products: 120 us -> 104 us
  Pallas kernels: 143 us -> 152 us
    dot_general x12 -> x11, matrix products: 91.3 us -> 74.7 us  [contract(): lax.dot_general(left, right, (((left_dim,), (right_dim,)), ((), ())), pre...]
    pallas_call x0 -> x1, Pallas kernels: none -> 14.2 us  [swiglu_back(): pl.pallas_call(swiglu_back_kernel, grid=(count,), in_specs=[whole_block((...]
    unnamed x184 -> x180, local copies, waits for them, and re-layouts: 18.2 us -> 18.2 us
  transfers between devices with their start and end apart: 74 -> 74, of which waited for: 36 -> 37; matrix products, arithmetic and copies ran while one was open for 27% -> 24% of each run, Pallas kernels for 16% -> 17%
where the time goes in v4:
time: 889 us; the launch traced here: 879 us
  waiting for transfers between devices  324 us (36%)
  Pallas kernels  152 us (17%)
  matrix products  104 us (12%)
  local copies, waits for them, and re-layouts  94.6 us (11%)
  starting transfers between devices  93.1 us (10%)
  other arithmetic  49.4 us (6%)
  blocking collectives  42.9 us (5%)
  between operations  19 us (2%)
    ppermute x50, waiting for transfers between devices, swap(): return lax.ppermute(v, axis, [(i, i ^ k) for i in range(n)])  250 us
    dot_general x11, matrix products, contract(): lax.dot_general(left, right, (((left_dim,), (right_dim,)), ((), ())), pre...  74.7 us
    pallas_call x3, Pallas kernels, attend_backward(): pl.pallas_call(functools.partial(attend_backward_kernel, index), grid=(ha...  69.6 us
    all_to_all x11, waiting for transfers between devices, exchange(): return lax.all_to_all(v, seq, 0, 0, tiled=True)  63.7 us
    all_to_all x11, starting transfers between devices, exchange(): return lax.all_to_all(v, seq, 0, 0, tiled=True)  46.1 us
    pallas_call x3, Pallas kernels, attend_forward(): pl.pallas_call(functools.partial(attend_forward_kernel, index), grid=(hal...  45.2 us
    all_to_all x3, blocking collectives, exchange(): return lax.all_to_all(v, seq, 0, 0, tiled=True)  42.9 us
    ppermute x50, starting transfers between devices, swap(): return lax.ppermute(v, axis, [(i, i ^ k) for i in range(n)])  38.7 us
  transfers between devices with their start and end apart: 74, of which 37 were waited for; matrix products, arithmetic and copies ran while one was open for 24% of the time, Pallas kernels for 17%

profile of v4, /device:TPU:0, one launch (start us, length us, event | category | flops | bytes accessed | tf_op | source)
XLA Modules:
  0.0 878.8 jit_solution(400233589332422189)
XLA Ops:
  39.1 17.9 %collective-permute-done.4 = f32[1,19968]{1,0:T(1,128)S(1)} collective-permute-done((f32[1,19968]{1,0:T(1,128)S(1)}, f32[1,19968]{1,0:T(1,128)S(1)}, u32[]{:S(2)}, u32[]{:S(2)}) %collective-permute-start.4) | collective-permute-done | bytes 79904 | tf_op jit(solution)/shard_map/ppermute | solution.py:393
  80.4 40.7 %collective-permute-done.14 = bf16[1,96,4864]{2,1,0:T(8,128)(2,1)S(1)} collective-permute-done((bf16[1,96,4864]{2,1,0:T(8,128)(2,1)S(1)}, bf16[1,96,4864]{2,1,0:T(8,128)(2,1)S(1)}, u32[]{:S(2)}, u32[]{:S(2)}) %collective-permute-start.14) | collective-permute-done | bytes 933920 | tf_op jit(solution)/shard_map/ppermute | solution.py:393
  130.0 19.5 %collective-permute-done.18 = bf16[96,4608]{1,0:T(8,128)(2,1)S(1)} collective-permute-done((bf16[96,4608]{1,0:T(8,128)(2,1)S(1)}, bf16[96,4608]{1,0:T(8,128)(2,1)S(1)}, u32[]{:S(2)}, u32[]{:S(2)}) %collective-permute-start.18) | collective-permute-done | bytes 884768 | tf_op jit(solution)/shard_map/ppermute | solution.py:393
  160.0 11.0 %collective-permute-done.22 = bf16[2,96,4864]{2,1,0:T(8,128)(2,1)S(1)} collective-permute-done((bf16[2,96,4864]{2,1,0:T(8,128)(2,1)S(1)}, bf16[2,96,4864]{2,1,0:T(8,128)(2,1)S(1)}, u32[]{:S(2)}, u32[]{:S(2)}) %collective-permute-start.22) | collective-permute-done | bytes 1867808 | tf_op jit(solution)/shard_map/ppermute | solution.py:393
  180.1 7.8 group_heads.1
  203.9 29.8 %collective-permute-done.26 = bf16[1,128,1536]{2,1,0:T(8,128)(2,1)S(1)} collective-permute-done((bf16[1,128,1536]{2,1,0:T(8,128)(2,1)S(1)}, bf16[1,128,1536]{2,1,0:T(8,128)(2,1)S(1)}, u32[]{:S(2)}, u32[]{:S(2)}) %collective-permute-start.26) | collective-permute-done | bytes 393248 | tf_op jit(solution)/shard_map/ppermute | solution.py:393
  243.3 15.3 %collective-permute-done.27 = bf16[2,128,1536]{2,1,0:T(8,128)(2,1)} collective-permute-done((bf16[2,128,1536]{2,1,0:T(8,128)(2,1)}, bf16[2,128,1536]{2,1,0:T(8,128)(2,1)}, u32[]{:S(2)}, u32[]{:S(2)}) %collective-permute-start.27) | collective-permute-done | bytes 786464 | tf_op jit(solution)/shard_map/ppermute | solution.py:393
  268.2 15.0 %attend_forward.3 = (bf16[1216,128]{1,0:T(8,128)(2,1)}, f32[1216,128]{1,0:T(8,128)}, f32[1216,128]{1,0:T(8,128)}, f32[1216,4]{1,0:T(8,128)}) custom-call(bf16[1216,384]{1,0:T(8,128)(2,1)} %bitcast.221, bf16[256,384]{1,0:T(8,128)(2,1)} %bitcast.25.text_ref, bf16[2432,1]{1,0:T(8,128)(2,1)} %select_convert_fusion.bias_ref, ...), custom_call_target="tpu_custom_call" | custom-call | flops 6694109184 | bytes 2801664 | tf_op jit(solution)/shard_map/attend_forward/pallas_call | solution.py:188
  291.1 10.7 %all-to-all-done.2.refs_0_ = bf16[8,152,128]{2,1,0:T(8,128)(2,1)S(1)} async-done(((bf16[8,152,128]{2,1,0:T(8,128)(2,1)}), bf16[8,152,128]{2,1,0:T(8,128)(2,1)S(1)}, u32[]{:S(2)}, u32[]{:S(2)}) %all-to-all-start.2) | async-done | bytes 311328 | tf_op jit(solution)/shard_map/all_to_all | solution.py:631
  307.5 15.1 %attend_forward.5 = (bf16[1216,128]{1,0:T(8,128)(2,1)}, f32[1216,128]{1,0:T(8,128)}, f32[1216,128]{1,0:T(8,128)}, f32[1216,4]{1,0:T(8,128)}) custom-call(bf16[1216,384]{1,0:T(8,128)(2,1)} %bitcast.33.qkv_ref.q_ref, bf16[256,384]{1,0:T(8,128)(2,1)} %bitcast.25.text_ref, bf16[2432,1]{1,0:T(8,128)(2,1)} %select_convert_fusion.bias_ref, ...), custom_call_target="tpu_custom_call" | custom-call | flops 6694109184 | bytes 2801664 | tf_op jit(solution)/shard_map/attend_forward/pallas_call | solution.py:188
  322.6 7.3 all-to-all-done.3
  334.5 15.1 %attend_forward.4 = (bf16[1216,128]{1,0:T(8,128)(2,1)}, f32[1216,128]{1,0:T(8,128)}, f32[1216,128]{1,0:T(8,128)}, f32[1216,4]{1,0:T(8,128)}) custom-call(bf16[1216,384]{1,0:T(8,128)(2,1)} %bitcast.225, bf16[256,384]{1,0:T(8,128)(2,1)} %bitcast.25.text_ref, bf16[2432,1]{1,0:T(8,128)(2,1)} %select_convert_fusion.bias_ref, ...), custom_call_target="tpu_custom_call" | custom-call | flops 6694109184 | bytes 2801664 | tf_op jit(solution)/shard_map/attend_forward/pallas_call | solution.py:188
  349.6 16.3 %all_to_all.70.refs_1_ = bf16[8,152,128]{2,1,0:T(8,128)(2,1)} all-to-all(bf16[8,152,128]{2,1,0:T(8,128)(2,1)} %bitcast.251), channel_id=1, replica_groups=mesh['dp'=4,'z'=4,'core'=2] {'z','core'}, dimensions={0} | all-to-all | bytes 622592 | tf_op jit(solution)/shard_map/all_to_all | solution.py:631
  379.6 11.3 %fusion.45.gate_ref.up_ref = f32[608,4096]{1,0:T(8,128)S(1)} fusion(bf16[1536,4096]{1,0:T(8,128)(2,1)} %all-gather.7.cloned.1.call-done, bf16[304,1536]{1,0:T(8,128)(2,1)} %collective-permute-done.25, bf16[304,1536]{1,0:T(8,128)(2,1)} %copy-done.39), kind=kOutput, calls=%fused_computation.105 | convolution fusion | flops 7654146048 | bytes 24412160 | tf_op jit(solution)/shard_map/dot_general | solution.py:42
  397.4 9.2 %all-gather.9.cloned.1.call-done.weight_ref = bf16[2048,1536]{1,0:T(8,128)(2,1)} async-done(((bf16[512,1536]{1,0:T(8,128)(2,1)}), bf16[2048,1536]{1,0:T(8,128)(2,1)}) %all-gather.9.cloned.1.call-update) | async-done | bytes 6291472 | tf_op jit(solution)/shard_map/all_gather | solution.py:491
  434.3 14.2 %swiglu_back.1 = bf16[608,4096]{1,0:T(8,128)(2,1)} custom-call(bf16[608,1536]{1,0:T(8,128)(2,1)} %pad_maximum_fusion.7.grad_ref, bf16[2048,1536]{1,0:T(8,128)(2,1)} %all-gather.9.cloned.1.call-done.weight_ref, f32[608,4096]{1,0:T(8,128)} %copy-done.2, f32[608,4096]{1,0:T(8,128)} %copy-done.2), custom_call_target="tpu_custom_call" | custom-call | flops 3825205248 | bytes 21233664 | tf_op jit(solution)/shard_map/swiglu_back/pallas_call | solution.py:323
  448.5 13.0 %fusion.116 = f32[608,1536]{1,0:T(8,128)S(1)} fusion(bf16[608,4096]{1,0:T(8,128)(2,1)} %swiglu_back.1, bf16[1536,4096]{1,0:T(8,128)(2,1)} %all-gather.7.cloned.1.call-done), kind=kOutput, calls=%fused_computation.315 | convolution fusion | flops 7650410496 | bytes 21299200 | tf_op jit(solution)/shard_map/dot_general | solution.py:46
  465.3 13.5 %convolution_convert_fusion = bf16[1536,4096]{1,0:T(8,128)(2,1)} fusion(bf16[608,4096]{1,0:T(8,128)(2,1)S(1)} %copy-done.17, bf16[304,1536]{1,0:T(8,128)(2,1)} %collective-permute-done.25, bf16[304,1536]{1,0:T(8,128)(2,1)S(1)} %copy-done.40), kind=kOutput, calls=%fused_computation | convolution fusion | flops 7660437504 | bytes 19431424 | tf_op jit(solution)/shard_map/dot_general | solution.py:46
  499.0 15.7 %all_to_all.71 = bf16[8,152,128]{2,1,0:T(8,128)(2,1)} all-to-all(bf16[8,152,128]{2,1,0:T(8,128)(2,1)} %get-tuple-element.106), channel_id=1, replica_groups=mesh['dp'=4,'z'=4,'core'=2] {'z','core'}, dimensions={0} | all-to-all | bytes 622592 | tf_op jit(solution)/shard_map/all_to_all | solution.py:631
  521.3 7.6 all-to-all-done.11
  533.0 23.2 %attend_backward.5 = (bf16[1216,384]{1,0:T(8,128)(2,1)}, bf16[256,128]{1,0:T(8,128)(2,1)}, f32[1,64]{1,0:T(1,128)}) custom-call(bf16[1216,384]{1,0:T(8,128)(2,1)} %bitcast.33.qkv_ref.q_ref, bf16[256,384]{1,0:T(8,128)(2,1)} %bitcast.25.text_ref, bf16[2432,1]{1,0:T(8,128)(2,1)} %select_convert_fusion.bias_ref, ...), custom_call_target="tpu_custom_call" | custom-call | flops 16735272960 | bytes 4046848 | tf_op jit(solution)/shard_map/attend_backward/pallas_call | solution.py:213
  561.5 23.1 %attend_backward.3 = (bf16[1216,384]{1,0:T(8,128)(2,1)}, bf16[256,128]{1,0:T(8,128)(2,1)}, f32[1,64]{1,0:T(1,128)}) custom-call(bf16[1216,384]{1,0:T(8,128)(2,1)} %bitcast.223, bf16[256,384]{1,0:T(8,128)(2,1)} %bitcast.25.text_ref, bf16[2432,1]{1,0:T(8,128)(2,1)} %select_convert_fusion.bias_ref, bf16[256,1]{1,0:T(8,128)(2,1)} %select_convert_fusion.1.text_bias_ref, ...), custom_call_target="tpu_custom_call" | custom-call | flops 16735272960 | bytes 4046848 | tf_op jit(solution)/shard_map/attend_backward/pallas_call | solution.py:213
  594.4 23.3 %attend_backward.4 = (bf16[1216,384]{1,0:T(8,128)(2,1)}, bf16[256,128]{1,0:T(8,128)(2,1)}, f32[1,64]{1,0:T(1,128)}) custom-call(bf16[1216,384]{1,0:T(8,128)(2,1)} %bitcast.227, bf16[256,384]{1,0:T(8,128)(2,1)} %bitcast.25.text_ref, bf16[2432,1]{1,0:T(8,128)(2,1)} %select_convert_fusion.bias_ref, bf16[256,1]{1,0:T(8,128)(2,1)} %select_convert_fusion.1.text_bias_ref, ...), custom_call_target="tpu_custom_call" | custom-call | flops 16735272960 | bytes 4046848 | tf_op jit(solution)/shard_map/attend_backward/pallas_call | solution.py:213
  619.5 8.9 %all-to-all-done.8.refs_0_ = bf16[8,152,384]{2,1,0:T(8,128)(2,1)} async-done(((bf16[8,152,384]{2,1,0:T(8,128)(2,1)}), bf16[8,152,384]{2,1,0:T(8,128)(2,1)}, u32[]{:S(2)}, u32[]{:S(2)}) %all-to-all-start.8) | async-done | bytes 933920 | tf_op jit(solution)/shard_map/all_to_all | solution.py:631
  633.3 24.0 %all-to-all-done.10.refs_1_ = bf16[8,152,384]{2,1,0:T(8,128)(2,1)} async-done(((bf16[8,152,384]{2,1,0:T(8,128)(2,1)}), bf16[8,152,384]{2,1,0:T(8,128)(2,1)}, u32[]{:S(2)}, u32[]{:S(2)}) %all-to-all-start.10) | async-done | bytes 933920 | tf_op jit(solution)/shard_map/all_to_all | solution.py:631
  657.3 9.0 %ungroup_heads.1 = (bf16[304,4608]{1,0:T(8,128)(2,1)}, f32[2,1536]{1,0:T(2,128)}) custom-call(bf16[8,152,384]{2,1,0:T(8,128)(2,1)} %all-to-all-done.8.refs_0_, bf16[8,152,384]{2,1,0:T(8,128)(2,1)} %all-to-all-done.10.refs_1_, bf16[8,152,384]{2,1,0:T(8,128)(2,1)} %all-to-all-done.12.refs_2_, f32[304,4608]{1,0:T(8,128)} %fusion.114.joint_ref.refs_3_, ...), custom_call_target="tpu_custom_call" | custom-call | flops 69828608 | bytes 11542528 | tf_op jit(solution)/shard_map/ungroup_heads/pallas_call | solution.py:348
  687.2 11.0 %all_to_all.72 = bf16[8,32,384]{2,1,0:T(8,128)(2,1)S(1)} all-to-all(bf16[8,32,384]{2,1,0:T(8,128)(2,1)S(1)} %bitcast.240), channel_id=1, replica_groups=mesh['dp'=4,'z'=4,'core'=2] {'z','core'}, dimensions={0} | all-to-all | bytes 393216 | tf_op jit(solution)/shard_map/all_to_all | solution.py:631
  714.2 36.4 %collective-permute-done.35 = bf16[2,96,4096]{2,1,0:T(8,128)(2,1)} collective-permute-done((bf16[2,96,4096]{2,1,0:T(8,128)(2,1)}, bf16[2,96,4096]{2,1,0:T(8,128)(2,1)}, u32[]{:S(2)}, u32[]{:S(2)}) %collective-permute-start.35) | collective-permute-done | bytes 1572896 | tf_op jit(solution)/shard_map/ppermute | solution.py:393
  754.2 12.4 %multiply_reduce_fusion.2 = (f32[1536]{0:T(1024)S(1)}, f32[1536]{0:T(1024)S(1)}, f32[1536]{0:T(1024)S(1)}, f32[304]{0:T(512)S(1)}, f32[304,1536]{1,0:T(8,128)}) fusion(f32[1536]{0:T(1024)S(1)} %copy-done.59, f32[304]{0:T(512)S(1)} %copy-done.66, bf16[294,1536]{1,0:T(8,128)(2,1)S(1)} %bitcast.197, f32[1536]{0:T(1024)S(1)} %copy-done.61, ...), kind=kOutput, calls=%fused_computation.53 | convolution fusion | flops 4308954112 | bytes 19761536 | tf_op jit(solution)/shard_map/dot_general | solution.py:46
  776.7 16.4 %collective-permute-done.41 = f32[16,1536]{1,0:T(8,128)S(1)} collective-permute-done((f32[16,1536]{1,0:T(8,128)S(1)}, f32[16,1536]{1,0:T(8,128)S(1)}, u32[]{:S(2)}, u32[]{:S(2)}) %collective-permute-start.41) | collective-permute-done | bytes 98336 | tf_op jit(solution)/shard_map/ppermute | solution.py:393
  796.0 15.6 %collective-permute-done.49 = bf16[1,96,4096]{2,1,0:T(8,128)(2,1)S(1)} collective-permute-done((bf16[1,96,4096]{2,1,0:T(8,128)(2,1)S(1)}, bf16[1,96,4096]{2,1,0:T(8,128)(2,1)S(1)}, u32[]{:S(2)}, u32[]{:S(2)}) %collective-permute-start.49) | collective-permute-done | bytes 786464 | tf_op jit(solution)/shard_map/ppermute | solution.py:393
  835.4 11.0 %collective-permute-done.43 = bf16[2,96,1152]{2,1,0:T(8,128)(2,1)S(1)} collective-permute-done((bf16[2,96,1152]{2,1,0:T(8,128)(2,1)}, bf16[2,96,1152]{2,1,0:T(8,128)(2,1)S(1)}, u32[]{:S(2)}, u32[]{:S(2)}) %collective-permute-start.43) | collective-permute-done | bytes 442400 | tf_op jit(solution)/shard_map/ppermute | solution.py:393
  (520 shorter events, 339.6 us)
Async XLA Ops:
  8.0 225.7 %reduce-scatter.7.cloned.1.call-start = ((), (), s32[]{:S(2)}) async-start(), calls=%async_computation.20 | async-start | bytes 3342336 | tf_op jit(solution)/shard_map/reduce_scatter | solution.py:604
  8.1 49.1 %collective-permute-start.6 = (bf16[48,4608]{1,0:T(8,128)(2,1)}, bf16[48,4608]{1,0:T(8,128)(2,1)}, u32[]{:S(2)}, u32[]{:S(2)}) collective-permute-start(bf16[48,4608]{1,0:T(8,128)(2,1)} %param.21), channel_id=1, source_target_pairs={{0,2},{2,4},{4,6},{6,0},{1,3},{3,5},{5,7},{7,1},{8,10},{10,12},{12... | collective-permute-start | bytes 1327112 | tf_op jit(solution)/shard_map/ppermute | solution.py:421
  11.2 46.0 %collective-permute-start.8 = (bf16[48,4608]{1,0:T(8,128)(2,1)}, bf16[48,4608]{1,0:T(8,128)(2,1)}, u32[]{:S(2)}, u32[]{:S(2)}) collective-permute-start(bf16[48,4608]{1,0:T(8,128)(2,1)} %param.21), channel_id=1, source_target_pairs={{0,4},{2,6},{4,0},{6,2},{1,5},{3,7},{5,1},{7,3},{8,12},{10,14},{12... | collective-permute-start | bytes 1327112 | tf_op jit(solution)/shard_map/ppermute | solution.py:421
  32.8 27.9 %collective-permute-start.9 = (bf16[48,4608]{1,0:T(8,128)(2,1)}, bf16[48,4608]{1,0:T(8,128)(2,1)S(1)}, u32[]{:S(2)}, u32[]{:S(2)}) collective-permute-start(bf16[48,4608]{1,0:T(8,128)(2,1)} %param.21), channel_id=1, source_target_pairs={{0,6},{2,0},{4,2},{6,4},{1,7},{3,1},{5,3},{7,5},{8,14},{10,8},{12,... | collective-permute-start | bytes 1327112 | tf_op jit(solution)/shard_map/ppermute | solution.py:421
  38.8 267.0 %all-gather.5.cloned.1.call-start = ((), (), s32[]{:S(2)}) async-start(), calls=%async_computation.21 | async-start | bytes 2949120 | tf_op jit(solution)/shard_map/all_gather | solution.py:491
  66.4 59.3 %collective-permute-start.10 = (bf16[192,4608]{1,0:T(8,128)(2,1)}, bf16[192,4608]{1,0:T(8,128)(2,1)}, u32[]{:S(2)}, u32[]{:S(2)}) collective-permute-start(bf16[192,4608]{1,0:T(8,128)(2,1)} %bitcast.8), channel_id=1, source_target_pairs={{0,1},{1,0},{2,3},{3,2},{4,5},{5,4},{6,7},{7,6},{8,9},{9,8},{10,11... | collective-permute-start | bytes 5308424 | tf_op jit(solution)/shard_map/ppermute | solution.py:393
  66.4 54.9 %collective-permute-start.11 = (bf16[192,4608]{1,0:T(8,128)(2,1)}, bf16[192,4608]{1,0:T(8,128)(2,1)}, u32[]{:S(2)}, u32[]{:S(2)}) collective-permute-start(bf16[192,4608]{1,0:T(8,128)(2,1)} %bitcast.8), channel_id=1, source_target_pairs={{0,8},{8,0},{16,24},{24,16},{1,9},{9,1},{17,25},{25,17},{2,10},{10... | collective-permute-start | bytes 5308424 | tf_op jit(solution)/shard_map/ppermute | solution.py:393
  68.4 53.4 %collective-permute-start.16 = (bf16[192,4608]{1,0:T(8,128)(2,1)}, bf16[192,4608]{1,0:T(8,128)(2,1)}, u32[]{:S(2)}, u32[]{:S(2)}) collective-permute-start(bf16[192,4608]{1,0:T(8,128)(2,1)} %bitcast.8), channel_id=1, source_target_pairs={{0,16},{8,24},{16,0},{24,8},{1,17},{9,25},{17,1},{25,9},{2,18},{10... | collective-permute-start | bytes 5308424 | tf_op jit(solution)/shard_map/ppermute | solution.py:393
  70.2 50.9 %collective-permute-start.14 = (bf16[1,96,4864]{2,1,0:T(8,128)(2,1)S(1)}, bf16[1,96,4864]{2,1,0:T(8,128)(2,1)S(1)}, u32[]{:S(2)}, u32[]{:S(2)}) collective-permute-start(bf16[1,96,4864]{2,1,0:T(8,128)(2,1)S(1)} %bitcast.200), channel_id=1, source_target_pairs={{0,4},{2,6},{4,0},{6,2},{1,5},{3,7},{5,1},{7,3},{8,12},{10,14},{12... | collective-permute-start | bytes 2801672 | tf_op jit(solution)/shard_map/ppermute | solution.py:393
  121.3 28.7 %collective-permute-start.15 = (bf16[192,4608]{1,0:T(8,128)(2,1)}, bf16[192,4608]{1,0:T(8,128)(2,1)S(1)}, u32[]{:S(2)}, u32[]{:S(2)}) collective-permute-start(bf16[192,4608]{1,0:T(8,128)(2,1)} %collective-permute-done.11), channel_id=1, source_target_pairs={{0,1},{1,0},{2,3},{3,2},{4,5},{5,4},{6,7},{7,6},{8,9},{9,8},{10,11... | collective-permute-start | bytes 5308424 | tf_op jit(solution)/shard_map/ppermute | solution.py:393
  121.7 49.2 %collective-permute-start.22 = (bf16[2,96,4864]{2,1,0:T(8,128)(2,1)S(1)}, bf16[2,96,4864]{2,1,0:T(8,128)(2,1)S(1)}, u32[]{:S(2)}, u32[]{:S(2)}) collective-permute-start(bf16[2,96,4864]{2,1,0:T(8,128)(2,1)S(1)} %pad_maximum_fusion.5), channel_id=1, source_target_pairs={{0,2},{2,0},{4,6},{6,4},{1,3},{3,1},{5,7},{7,5},{8,10},{10,8},{12,... | collective-permute-start | bytes 5603336 | tf_op jit(solution)/shard_map/ppermute | solution.py:393
  121.8 30.0 %collective-permute-start.17 = (bf16[192,4608]{1,0:T(8,128)(2,1)}, bf16[192,4608]{1,0:T(8,128)(2,1)S(1)}, u32[]{:S(2)}, u32[]{:S(2)}) collective-permute-start(bf16[192,4608]{1,0:T(8,128)(2,1)} %collective-permute-done.16), channel_id=1, source_target_pairs={{0,1},{1,0},{2,3},{3,2},{4,5},{5,4},{6,7},{7,6},{8,9},{9,8},{10,11... | collective-permute-start | bytes 5308424 | tf_op jit(solution)/shard_map/ppermute | solution.py:393
  173.9 205.7 %all-gather.7.cloned.1.call-start = ((), (), s32[]{:S(2)}) async-start(), calls=%async_computation.22 | async-start | bytes 15728640 | tf_op jit(solution)/shard_map/all_gather | solution.py:491
  187.8 45.9 %all-to-all-start = ((bf16[8,152,384]{2,1,0:T(8,128)(2,1)}), bf16[8,152,384]{2,1,0:T(8,128)(2,1)S(1)}, u32[]{:S(2)}, u32[]{:S(2)}) async-start(bf16[8,152,384]{2,1,0:T(8,128)(2,1)} %get-tuple-element.93), calls=%async_computation | async-start | bytes 1867776 | tf_op jit(solution)/shard_map/all_to_all | solution.py:631
  197.3 36.5 %collective-permute-start.26 = (bf16[1,128,1536]{2,1,0:T(8,128)(2,1)S(1)}, bf16[1,128,1536]{2,1,0:T(8,128)(2,1)S(1)}, u32[]{:S(2)}, u32[]{:S(2)}) collective-permute-start(bf16[1,128,1536]{2,1,0:T(8,128)(2,1)S(1)} %bitcast.212), channel_id=1, source_target_pairs={{0,4},{2,6},{4,0},{6,2},{1,5},{3,7},{5,1},{7,3},{8,12},{10,14},{12... | collective-permute-start | bytes 1179656 | tf_op jit(solution)/shard_map/ppermute | solution.py:393
  259.3 28.4 %all-to-all-start.5 = ((bf16[8,152,384]{2,1,0:T(8,128)(2,1)}), bf16[8,152,384]{2,1,0:T(8,128)(2,1)}, u32[]{:S(2)}, u32[]{:S(2)}) async-start(bf16[8,152,384]{2,1,0:T(8,128)(2,1)} %get-tuple-element.99), calls=%async_computation.6 | async-start | bytes 1867776 | tf_op jit(solution)/shard_map/all_to_all | solution.py:631
  263.5 143.1 %all-gather.9.cloned.1.call-start = ((), (), s32[]{:S(2)}) async-start(), calls=%async_computation.23 | async-start | bytes 7864320 | tf_op jit(solution)/shard_map/all_gather | solution.py:491
  301.9 28.0 %all-to-all-start.3 = ((bf16[8,152,384]{2,1,0:T(8,128)(2,1)}), bf16[8,152,384]{2,1,0:T(8,128)(2,1)S(1)}, u32[]{:S(2)}, u32[]{:S(2)}) async-start(bf16[8,152,384]{2,1,0:T(8,128)(2,1)} %get-tuple-element.97), calls=%async_computation.4 | async-start | bytes 1867776 | tf_op jit(solution)/shard_map/all_to_all | solution.py:631
  305.9 62.8 %collective-permute-start.24 = (bf16[1536,768]{1,0:T(8,128)(2,1)}, bf16[1536,768]{1,0:T(8,128)(2,1)}, u32[]{:S(2)}, u32[]{:S(2)}) collective-permute-start(bf16[1536,768]{1,0:T(8,128)(2,1)} %all-gather.5.cloned.1.call-done), channel_id=1, source_target_pairs={{0,1},{1,0},{2,3},{3,2},{4,5},{5,4},{6,7},{7,6},{8,9},{9,8},{10,11... | collective-permute-start | bytes 7077896 | tf_op jit(solution)/shard_map/ppermute | solution.py:393
  333.3 184.8 %reduce-scatter.9.cloned.1.call-start = ((), (), s32[]{:S(2)}) async-start(), calls=%async_computation.24 | async-start | bytes 7864320 | tf_op jit(solution)/shard_map/reduce_scatter | solution.py:525
  431.5 247.5 %reduce-scatter.13.cloned.1.call-start = ((), (), s32[]{:S(2)}) async-start(), calls=%async_computation.26 | async-start | bytes 2949120 | tf_op jit(solution)/shard_map/reduce_scatter | solution.py:525
  495.8 183.1 %reduce-scatter.11.cloned.1.call-start = ((), (), s32[]{:S(2)}) async-start(), calls=%async_computation.25 | async-start | bytes 15728640 | tf_op jit(solution)/shard_map/reduce_scatter | solution.py:525
  519.4 65.2 %collective-permute-start.33 = (bf16[2,128,1536]{2,1,0:T(8,128)(2,1)S(1)}, bf16[2,128,1536]{2,1,0:T(8,128)(2,1)}, u32[]{:S(2)}, u32[]{:S(2)}) collective-permute-start(bf16[2,128,1536]{2,1,0:T(8,128)(2,1)S(1)} %dynamic-slice_bitcast_fusion.1), channel_id=1, source_target_pairs={{0,2},{2,0},{4,6},{6,4},{1,3},{3,1},{5,7},{7,5},{8,10},{10,8},{12,... | collective-permute-start | bytes 2359304 | tf_op jit(solution)/shard_map/ppermute | solution.py:393
  556.2 33.5 %all-to-all-start.12 = ((bf16[8,152,384]{2,1,0:T(8,128)(2,1)}), bf16[8,152,384]{2,1,0:T(8,128)(2,1)}, u32[]{:S(2)}, u32[]{:S(2)}) async-start(bf16[8,152,384]{2,1,0:T(8,128)(2,1)} %bitcast.231), calls=%async_computation.14 | async-start | bytes 1867776 | tf_op jit(solution)/shard_map/all_to_all | solution.py:631
  586.9 31.6 %collective-permute-start.34 = (bf16[1,128,1536]{2,1,0:T(8,128)(2,1)}, bf16[1,128,1536]{2,1,0:T(8,128)(2,1)S(1)}, u32[]{:S(2)}, u32[]{:S(2)}) collective-permute-start(bf16[1,128,1536]{2,1,0:T(8,128)(2,1)} %constant_dynamic-slice_fusion.11), channel_id=1, source_target_pairs={{0,4},{2,6},{4,0},{6,2},{1,5},{3,7},{5,1},{7,3},{8,12},{10,14},{12... | collective-permute-start | bytes 1179656 | tf_op jit(solution)/shard_map/ppermute | solution.py:393
  589.7 38.6 %all-to-all-start.8 = ((bf16[8,152,384]{2,1,0:T(8,128)(2,1)}), bf16[8,152,384]{2,1,0:T(8,128)(2,1)}, u32[]{:S(2)}, u32[]{:S(2)}) async-start(bf16[8,152,384]{2,1,0:T(8,128)(2,1)} %bitcast.229), calls=%async_computation.10 | async-start | bytes 1867776 | tf_op jit(solution)/shard_map/all_to_all | solution.py:631
  628.3 29.0 %all-to-all-start.10 = ((bf16[8,152,384]{2,1,0:T(8,128)(2,1)}), bf16[8,152,384]{2,1,0:T(8,128)(2,1)}, u32[]{:S(2)}, u32[]{:S(2)}) async-start(bf16[8,152,384]{2,1,0:T(8,128)(2,1)} %bitcast.230), calls=%async_computation.12 | async-start | bytes 1867776 | tf_op jit(solution)/shard_map/all_to_all | solution.py:631
  633.1 184.7 %reduce-scatter.15.cloned.1.call-start = ((), (), s32[]{:S(2)}) async-start(), calls=%async_computation.27 | async-start | bytes 4423680 | tf_op jit(solution)/shard_map/reduce_scatter | solution.py:525
  679.0 140.7 %reduce-scatter.17.cloned.1.call-start = ((), (), s32[]{:S(2)}) async-start(), calls=%async_computation.28 | async-start | bytes 4423680 | tf_op jit(solution)/shard_map/reduce_scatter | solution.py:525
  685.9 137.5 %all-gather.11.cloned.1.call-start = ((), (), s32[]{:S(2)}) async-start(), calls=%async_computation.29 | async-start | bytes 6488064 | tf_op jit(solution)/shard_map/all_gather | solution.py:754
  702.6 48.0 %collective-permute-start.35 = (bf16[2,96,4096]{2,1,0:T(8,128)(2,1)}, bf16[2,96,4096]{2,1,0:T(8,128)(2,1)}, u32[]{:S(2)}, u32[]{:S(2)}) collective-permute-start(bf16[2,96,4096]{2,1,0:T(8,128)(2,1)} %dynamic-slice_bitcast_fusion), channel_id=1, source_target_pairs={{0,2},{2,0},{4,6},{6,4},{1,3},{3,1},{5,7},{7,5},{8,10},{10,8},{12,... | collective-permute-start | bytes 4718600 | tf_op jit(solution)/shard_map/ppermute | solution.py:393
  771.1 40.5 %collective-permute-start.49 = (bf16[1,96,4096]{2,1,0:T(8,128)(2,1)S(1)}, bf16[1,96,4096]{2,1,0:T(8,128)(2,1)S(1)}, u32[]{:S(2)}, u32[]{:S(2)}) collective-permute-start(bf16[1,96,4096]{2,1,0:T(8,128)(2,1)S(1)} %constant_dynamic-slice_fusion.5), channel_id=1, source_target_pairs={{0,4},{2,6},{4,0},{6,2},{1,5},{3,7},{5,1},{7,3},{8,12},{10,14},{12... | collective-permute-start | bytes 2359304 | tf_op jit(solution)/shard_map/ppermute | solution.py:393
  (126 other events, 2020.8 us)
Sparse Core Ops, SparseCore 0:
  38.9 153.8 reduce-scatter.6
  700.0 76.6 all-gather.10
Sparse Core Ops, SparseCore 1:
  174.0 36.2 all-gather.4
  211.9 122.3 all-gather.6
  336.6 70.0 all-gather.8
  431.6 70.0 reduce-scatter.8
  504.7 37.2 reduce-scatter.12
  545.1 120.5 reduce-scatter.10
  679.0 45.3 reduce-scatter.14
  727.4 49.5 reduce-scatter.16

commit v5 on v4

--- a/solution.py
+++ b/solution.py
@@ -736,8 +736,7 @@
         "ungroup_heads", *grouped, joint, rope_gains, cosine, sine,
     )
     joint_left, joint_right = column_split(normed_low, joint_low)
-    piece = joint_right.shape[1] // 2
-    joint_parts = [grad_of(joint_left, joint_right[:, p * piece : (p + 1) * piece]) for p in range(2)]
+    joint_parts = [grad_of(joint_left, joint_right)]
     joint_parts = [reduce_dp(after(part, gate_up_part, mixer_part)) for part in joint_parts]
     gate_up_sum = Reduce(gate_up_part)
     later_low = after(joint_low, gate_up_sum.step(joint_low))
@@ -752,7 +751,7 @@
         [text_key_grad.astype(BF), from_groups(text_back[:, :, wide:])], axis=1
     )
     text_grad_all = lax.all_gather(after(text_grad_rows, joint_low), everyone, axis=0, tiled=True)
-    text_grad = contract(flat_text, after(text_grad_all, joint_parts[1]), 0, 0)
+    text_grad = contract(flat_text, after(text_grad_all, joint_parts[-1]), 0, 0)
 
     gates_own = jnp.concatenate([jnp.sum(v, axis=1) for v in dgates]) * (1.0 - own_gates * own_gates)
     gates_all = lax.dynamic_update_slice_in_dim(jnp.zeros((WIDTH,), F32), gates_own, first_head, 0)[None, :]

time: 889 us -> 890 us (level)
    ppermute x50 -> x48, waiting for transfers between devices: 250 us -> 257 us  [swap(): return lax.ppermute(v, axis, [(i, i ^ k) for i in range(n)])]
    dot_general x11 -> x10, matrix products: 74.7 us -> 70.9 us  [contract(): lax.dot_general(left, right, (((left_dim,), (right_dim,)), ((), ())), pre...]
    ppermute x50 -> x48, starting transfers between devices: 38.7 us -> 37.9 us  [swap(): return lax.ppermute(v, axis, [(i, i ^ k) for i in range(n)])]
    unnamed x180 -> x176, local copies, waits for them, and re-layouts: 18.2 us -> 18.1 us
  transfers between devices with their start and end apart: 74 -> 71, of which waited for: 37 -> 35; matrix products, arithmetic and copies ran while one was open for 24% -> 24% of each run, Pallas kernels for 17% -> 17%
where the time goes in v5:
time: 890 us; the launch traced here: 879 us
  waiting for transfers between devices  328 us (37%)
  Pallas kernels  152 us (17%)
  matrix products  99.6 us (11%)
  local copies, waits for them, and re-layouts  94 us (11%)
  starting transfers between devices  89.8 us (10%)
  other arithmetic  53.3 us (6%)
  blocking collectives  43.3 us (5%)
  between operations  19.2 us (2%)
    ppermute x48, waiting for transfers between devices, swap(): return lax.ppermute(v, axis, [(i, i ^ k) for i in range(n)])  257 us
    dot_general x10, matrix products, contract(): lax.dot_general(left, right, (((left_dim,), (right_dim,)), ((), ())), pre...  70.9 us
    pallas_call x3, Pallas kernels, attend_backward(): pl.pallas_call(functools.partial(attend_backward_kernel, index), grid=(ha...  69.6 us
    all_to_all x11, waiting for transfers between devices, exchange(): return lax.all_to_all(v, seq, 0, 0, tiled=True)  63.3 us
    pallas_call x3, Pallas kernels, attend_forward(): pl.pallas_call(functools.partial(attend_forward_kernel, index), grid=(hal...  45.2 us
    all_to_all x11, starting transfers between devices, exchange(): return lax.all_to_all(v, seq, 0, 0, tiled=True)  43.8 us
    all_to_all x3, blocking collectives, exchange(): return lax.all_to_all(v, seq, 0, 0, tiled=True)  43.3 us
    ppermute x48, starting transfers between devices, swap(): return lax.ppermute(v, axis, [(i, i ^ k) for i in range(n)])  37.9 us
  transfers between devices with their start and end apart: 71, of which 35 were waited for; matrix products, arithmetic and copies ran while one was open for 24% of the time, Pallas kernels for 17%

profile of v5, /device:TPU:0, one launch (start us, length us, event | category | flops | bytes accessed | tf_op | source)
XLA Modules:
  0.0 879.4 jit_solution(3278602080527395387)
XLA Ops:
  42.0 13.5 %collective-permute-done.4 = f32[1,19968]{1,0:T(1,128)S(1)} collective-permute-done((f32[1,19968]{1,0:T(1,128)S(1)}, f32[1,19968]{1,0:T(1,128)S(1)}, u32[]{:S(2)}, u32[]{:S(2)}) %collective-permute-start.4) | collective-permute-done | bytes 79904 | tf_op jit(solution)/shard_map/ppermute | solution.py:393
  78.6 42.1 %collective-permute-done.14 = bf16[1,96,4864]{2,1,0:T(8,128)(2,1)S(1)} collective-permute-done((bf16[1,96,4864]{2,1,0:T(8,128)(2,1)S(1)}, bf16[1,96,4864]{2,1,0:T(8,128)(2,1)S(1)}, u32[]{:S(2)}, u32[]{:S(2)}) %collective-permute-start.14) | collective-permute-done | bytes 933920 | tf_op jit(solution)/shard_map/ppermute | solution.py:393
  129.5 19.9 %collective-permute-done.18 = bf16[96,4608]{1,0:T(8,128)(2,1)S(1)} collective-permute-done((bf16[96,4608]{1,0:T(8,128)(2,1)S(1)}, bf16[96,4608]{1,0:T(8,128)(2,1)S(1)}, u32[]{:S(2)}, u32[]{:S(2)}) %collective-permute-start.18) | collective-permute-done | bytes 884768 | tf_op jit(solution)/shard_map/ppermute | solution.py:393
  159.8 7.6 collective-permute-done.22
  176.6 7.6 group_heads.1
  199.5 31.0 %collective-permute-done.26 = bf16[1,128,1536]{2,1,0:T(8,128)(2,1)S(1)} collective-permute-done((bf16[1,128,1536]{2,1,0:T(8,128)(2,1)S(1)}, bf16[1,128,1536]{2,1,0:T(8,128)(2,1)S(1)}, u32[]{:S(2)}, u32[]{:S(2)}) %collective-permute-start.26) | collective-permute-done | bytes 393248 | tf_op jit(solution)/shard_map/ppermute | solution.py:393
  239.0 16.4 %collective-permute-done.27 = bf16[2,128,1536]{2,1,0:T(8,128)(2,1)} collective-permute-done((bf16[2,128,1536]{2,1,0:T(8,128)(2,1)}, bf16[2,128,1536]{2,1,0:T(8,128)(2,1)}, u32[]{:S(2)}, u32[]{:S(2)}) %collective-permute-start.27) | collective-permute-done | bytes 786464 | tf_op jit(solution)/shard_map/ppermute | solution.py:393
  265.0 15.1 %attend_forward.3 = (bf16[1216,128]{1,0:T(8,128)(2,1)}, f32[1216,128]{1,0:T(8,128)}, f32[1216,128]{1,0:T(8,128)}, f32[1216,4]{1,0:T(8,128)}) custom-call(bf16[1216,384]{1,0:T(8,128)(2,1)} %bitcast.214, bf16[256,384]{1,0:T(8,128)(2,1)} %bitcast.242, bf16[2432,1]{1,0:T(8,128)(2,1)} %select_convert_fusion.bias_ref, ...), custom_call_target="tpu_custom_call" | custom-call | flops 6694109184 | bytes 2801664 | tf_op jit(solution)/shard_map/attend_forward/pallas_call | solution.py:188
  287.7 10.7 %all-to-all-done.2.refs_0_ = bf16[8,152,128]{2,1,0:T(8,128)(2,1)S(1)} async-done(((bf16[8,152,128]{2,1,0:T(8,128)(2,1)}), bf16[8,152,128]{2,1,0:T(8,128)(2,1)S(1)}, u32[]{:S(2)}, u32[]{:S(2)}) %all-to-all-start.2) | async-done | bytes 311328 | tf_op jit(solution)/shard_map/all_to_all | solution.py:631
  303.9 15.0 %attend_forward.5 = (bf16[1216,128]{1,0:T(8,128)(2,1)}, f32[1216,128]{1,0:T(8,128)}, f32[1216,128]{1,0:T(8,128)}, f32[1216,4]{1,0:T(8,128)}) custom-call(bf16[1216,384]{1,0:T(8,128)(2,1)} %bitcast.33.qkv_ref.q_ref, bf16[256,384]{1,0:T(8,128)(2,1)} %bitcast.243, bf16[2432,1]{1,0:T(8,128)(2,1)} %select_convert_fusion.bias_ref, ...), custom_call_target="tpu_custom_call" | custom-call | flops 6694109184 | bytes 2801664 | tf_op jit(solution)/shard_map/attend_forward/pallas_call | solution.py:188
  318.9 7.4 all-to-all-done.3
  330.9 15.2 %attend_forward.4 = (bf16[1216,128]{1,0:T(8,128)(2,1)}, f32[1216,128]{1,0:T(8,128)}, f32[1216,128]{1,0:T(8,128)}, f32[1216,4]{1,0:T(8,128)}) custom-call(bf16[1216,384]{1,0:T(8,128)(2,1)} %bitcast.218, bf16[256,384]{1,0:T(8,128)(2,1)} %bitcast.244, bf16[2432,1]{1,0:T(8,128)(2,1)} %select_convert_fusion.bias_ref, ...), custom_call_target="tpu_custom_call" | custom-call | flops 6694109184 | bytes 2801664 | tf_op jit(solution)/shard_map/attend_forward/pallas_call | solution.py:188
  346.1 16.6 %all_to_all.70.refs_1_ = bf16[8,152,128]{2,1,0:T(8,128)(2,1)} all-to-all(bf16[8,152,128]{2,1,0:T(8,128)(2,1)} %bitcast.241), channel_id=1, replica_groups=mesh['dp'=4,'z'=4,'core'=2] {'z','core'}, dimensions={0} | all-to-all | bytes 622592 | tf_op jit(solution)/shard_map/all_to_all | solution.py:631
  376.9 11.3 %fusion.49.gate_ref.up_ref = f32[608,4096]{1,0:T(8,128)S(1)} fusion(bf16[1536,4096]{1,0:T(8,128)(2,1)} %all-gather.7.cloned.1.call-done, bf16[304,1536]{1,0:T(8,128)(2,1)} %collective-permute-done.25, bf16[304,1536]{1,0:T(8,128)(2,1)} %copy-done.37), kind=kOutput, calls=%fused_computation.106 | convolution fusion | flops 7654146048 | bytes 24412160 | tf_op jit(solution)/shard_map/dot_general | solution.py:42
  429.4 14.1 %swiglu_back.1 = bf16[608,4096]{1,0:T(8,128)(2,1)} custom-call(bf16[608,1536]{1,0:T(8,128)(2,1)} %pad_maximum_fusion.7.grad_ref, bf16[2048,1536]{1,0:T(8,128)(2,1)} %all-gather.9.cloned.1.call-done.weight_ref, f32[608,4096]{1,0:T(8,128)} %copy-done.2, f32[608,4096]{1,0:T(8,128)} %copy-done.2), custom_call_target="tpu_custom_call" | custom-call | flops 3825205248 | bytes 21233664 | tf_op jit(solution)/shard_map/swiglu_back/pallas_call | solution.py:323
  443.4 13.0 %fusion.113 = f32[608,1536]{1,0:T(8,128)S(1)} fusion(bf16[608,4096]{1,0:T(8,128)(2,1)} %swiglu_back.1, bf16[1536,4096]{1,0:T(8,128)(2,1)} %all-gather.7.cloned.1.call-done), kind=kOutput, calls=%fused_computation.301 | convolution fusion | flops 7650410496 | bytes 21299200 | tf_op jit(solution)/shard_map/dot_general | solution.py:46
  460.2 13.5 %convolution_convert_fusion = bf16[1536,4096]{1,0:T(8,128)(2,1)} fusion(bf16[608,4096]{1,0:T(8,128)(2,1)S(1)} %copy-done.15, bf16[304,1536]{1,0:T(8,128)(2,1)} %collective-permute-done.25, bf16[304,1536]{1,0:T(8,128)(2,1)S(1)} %copy-done.38), kind=kOutput, calls=%fused_computation | convolution fusion | flops 7660437504 | bytes 19431424 | tf_op jit(solution)/shard_map/dot_general | solution.py:46
  494.0 15.7 %all_to_all.71 = bf16[8,152,128]{2,1,0:T(8,128)(2,1)} all-to-all(bf16[8,152,128]{2,1,0:T(8,128)(2,1)} %get-tuple-element.102), channel_id=1, replica_groups=mesh['dp'=4,'z'=4,'core'=2] {'z','core'}, dimensions={0} | all-to-all | bytes 622592 | tf_op jit(solution)/shard_map/all_to_all | solution.py:631
  516.3 7.6 all-to-all-done.11
  527.4 23.2 %attend_backward.5 = (bf16[1216,384]{1,0:T(8,128)(2,1)}, bf16[256,128]{1,0:T(8,128)(2,1)}, f32[1,64]{1,0:T(1,128)}) custom-call(bf16[1216,384]{1,0:T(8,128)(2,1)} %bitcast.33.qkv_ref.q_ref, bf16[256,384]{1,0:T(8,128)(2,1)} %bitcast.245, bf16[2432,1]{1,0:T(8,128)(2,1)} %select_convert_fusion.bias_ref, bf16[256,1]{1,0:T(8,128)(2,1)} %select_convert_fusion.1.text_bias_ref, ...), custom_call_target="tpu_custom_call" | custom-call | flops 16735272960 | bytes 4046848 | tf_op jit(solution)/shard_map/attend_backward/pallas_call | solution.py:213
  556.1 23.2 %attend_backward.3 = (bf16[1216,384]{1,0:T(8,128)(2,1)}, bf16[256,128]{1,0:T(8,128)(2,1)}, f32[1,64]{1,0:T(1,128)}) custom-call(bf16[1216,384]{1,0:T(8,128)(2,1)} %bitcast.216, bf16[256,384]{1,0:T(8,128)(2,1)} %bitcast.246, bf16[2432,1]{1,0:T(8,128)(2,1)} %select_convert_fusion.bias_ref, bf16[256,1]{1,0:T(8,128)(2,1)} %select_convert_fusion.1.text_bias_ref, ...), custom_call_target="tpu_custom_call" | custom-call | flops 16735272960 | bytes 4046848 | tf_op jit(solution)/shard_map/attend_backward/pallas_call | solution.py:213
  588.9 23.2 %attend_backward.4 = (bf16[1216,384]{1,0:T(8,128)(2,1)}, bf16[256,128]{1,0:T(8,128)(2,1)}, f32[1,64]{1,0:T(1,128)}) custom-call(bf16[1216,384]{1,0:T(8,128)(2,1)} %bitcast.220, bf16[256,384]{1,0:T(8,128)(2,1)} %bitcast.247, bf16[2432,1]{1,0:T(8,128)(2,1)} %select_convert_fusion.bias_ref, bf16[256,1]{1,0:T(8,128)(2,1)} %select_convert_fusion.1.text_bias_ref, ...), custom_call_target="tpu_custom_call" | custom-call | flops 16735272960 | bytes 4046848 | tf_op jit(solution)/shard_map/attend_backward/pallas_call | solution.py:213
  614.1 8.7 all-to-all-done.8.refs_0_
  627.9 24.0 %all-to-all-done.10.refs_1_ = bf16[8,152,384]{2,1,0:T(8,128)(2,1)} async-done(((bf16[8,152,384]{2,1,0:T(8,128)(2,1)}), bf16[8,152,384]{2,1,0:T(8,128)(2,1)}, u32[]{:S(2)}, u32[]{:S(2)}) %all-to-all-start.10) | async-done | bytes 933920 | tf_op jit(solution)/shard_map/all_to_all | solution.py:631
  651.9 9.0 %ungroup_heads.1 = (bf16[304,4608]{1,0:T(8,128)(2,1)}, f32[2,1536]{1,0:T(2,128)}) custom-call(bf16[8,152,384]{2,1,0:T(8,128)(2,1)} %all-to-all-done.8.refs_0_, bf16[8,152,384]{2,1,0:T(8,128)(2,1)} %all-to-all-done.10.refs_1_, bf16[8,152,384]{2,1,0:T(8,128)(2,1)} %all-to-all-done.12.refs_2_, f32[304,4608]{1,0:T(8,128)} %fusion.111.joint_ref.refs_3_, ...), custom_call_target="tpu_custom_call" | custom-call | flops 69828608 | bytes 11542528 | tf_op jit(solution)/shard_map/ungroup_heads/pallas_call | solution.py:348
  667.4 7.8 convolution_convert_fusion.1
  676.6 11.0 %all_to_all.72 = bf16[8,32,384]{2,1,0:T(8,128)(2,1)S(1)} all-to-all(bf16[8,32,384]{2,1,0:T(8,128)(2,1)S(1)} %bitcast.229), channel_id=1, replica_groups=mesh['dp'=4,'z'=4,'core'=2] {'z','core'}, dimensions={0} | all-to-all | bytes 393216 | tf_op jit(solution)/shard_map/all_to_all | solution.py:631
  703.7 28.0 %collective-permute-done.35 = bf16[2,96,4096]{2,1,0:T(8,128)(2,1)} collective-permute-done((bf16[2,96,4096]{2,1,0:T(8,128)(2,1)}, bf16[2,96,4096]{2,1,0:T(8,128)(2,1)}, u32[]{:S(2)}, u32[]{:S(2)}) %collective-permute-start.35) | collective-permute-done | bytes 1572896 | tf_op jit(solution)/shard_map/ppermute | solution.py:393
  734.2 12.3 %multiply_reduce_fusion.2 = (f32[1536]{0:T(1024)S(1)}, f32[1536]{0:T(1024)S(1)}, f32[1536]{0:T(1024)S(1)}, f32[304]{0:T(512)S(1)}, f32[304,1536]{1,0:T(8,128)}) fusion(f32[1536]{0:T(1024)S(1)} %copy-done.59, f32[304]{0:T(512)S(1)} %copy-done.66, bf16[294,1536]{1,0:T(8,128)(2,1)S(1)} %bitcast.188, f32[1536]{0:T(1024)S(1)} %copy-done.61, ...), kind=kOutput, calls=%fused_computation.55 | convolution fusion | flops 4308954112 | bytes 19761536 | tf_op jit(solution)/shard_map/dot_general | solution.py:46
  754.7 21.2 %collective-permute-done.41 = f32[16,1536]{1,0:T(8,128)S(1)} collective-permute-done((f32[16,1536]{1,0:T(8,128)S(1)}, f32[16,1536]{1,0:T(8,128)S(1)}, u32[]{:S(2)}, u32[]{:S(2)}) %collective-permute-start.41) | collective-permute-done | bytes 98336 | tf_op jit(solution)/shard_map/ppermute | solution.py:393
  780.1 32.4 %collective-permute-done.47 = bf16[1,96,4096]{2,1,0:T(8,128)(2,1)S(1)} collective-permute-done((bf16[1,96,4096]{2,1,0:T(8,128)(2,1)S(1)}, bf16[1,96,4096]{2,1,0:T(8,128)(2,1)S(1)}, u32[]{:S(2)}, u32[]{:S(2)}) %collective-permute-start.47) | collective-permute-done | bytes 786464 | tf_op jit(solution)/shard_map/ppermute | solution.py:393
  846.2 9.7 %collective-permute-done.44 = bf16[2,96,768]{2,1,0:T(8,128)(2,1)S(1)} collective-permute-done((bf16[2,96,768]{2,1,0:T(8,128)(2,1)S(1)}, bf16[2,96,768]{2,1,0:T(8,128)(2,1)S(1)}, u32[]{:S(2)}, u32[]{:S(2)}) %collective-permute-start.44) | collective-permute-done | bytes 294944 | tf_op jit(solution)/shard_map/ppermute | solution.py:393
  (504 shorter events, 333.4 us)
Async XLA Ops:
  8.0 222.4 %reduce-scatter.6.cloned.1.call-start = ((), (), s32[]{:S(2)}) async-start(), calls=%async_computation.19 | async-start | bytes 3342336 | tf_op jit(solution)/shard_map/reduce_scatter | solution.py:604
  8.1 47.6 %collective-permute-start.6 = (bf16[48,4608]{1,0:T(8,128)(2,1)}, bf16[48,4608]{1,0:T(8,128)(2,1)}, u32[]{:S(2)}, u32[]{:S(2)}) collective-permute-start(bf16[48,4608]{1,0:T(8,128)(2,1)} %param.21), channel_id=1, source_target_pairs={{0,2},{2,4},{4,6},{6,0},{1,3},{3,5},{5,7},{7,1},{8,10},{10,12},{12... | collective-permute-start | bytes 1327112 | tf_op jit(solution)/shard_map/ppermute | solution.py:421
  11.2 44.5 %collective-permute-start.8 = (bf16[48,4608]{1,0:T(8,128)(2,1)}, bf16[48,4608]{1,0:T(8,128)(2,1)}, u32[]{:S(2)}, u32[]{:S(2)}) collective-permute-start(bf16[48,4608]{1,0:T(8,128)(2,1)} %param.21), channel_id=1, source_target_pairs={{0,4},{2,6},{4,0},{6,2},{1,5},{3,7},{5,1},{7,3},{8,12},{10,14},{12... | collective-permute-start | bytes 1327112 | tf_op jit(solution)/shard_map/ppermute | solution.py:421
  41.7 260.5 %all-gather.5.cloned.1.call-start = ((), (), s32[]{:S(2)}) async-start(), calls=%async_computation.20 | async-start | bytes 2949120 | tf_op jit(solution)/shard_map/all_gather | solution.py:491
  65.2 60.1 %collective-permute-start.10 = (bf16[192,4608]{1,0:T(8,128)(2,1)}, bf16[192,4608]{1,0:T(8,128)(2,1)}, u32[]{:S(2)}, u32[]{:S(2)}) collective-permute-start(bf16[192,4608]{1,0:T(8,128)(2,1)} %bitcast.8), channel_id=1, source_target_pairs={{0,1},{1,0},{2,3},{3,2},{4,5},{5,4},{6,7},{7,6},{8,9},{9,8},{10,11... | collective-permute-start | bytes 5308424 | tf_op jit(solution)/shard_map/ppermute | solution.py:393
  65.3 55.6 %collective-permute-start.11 = (bf16[192,4608]{1,0:T(8,128)(2,1)}, bf16[192,4608]{1,0:T(8,128)(2,1)}, u32[]{:S(2)}, u32[]{:S(2)}) collective-permute-start(bf16[192,4608]{1,0:T(8,128)(2,1)} %bitcast.8), channel_id=1, source_target_pairs={{0,8},{8,0},{16,24},{24,16},{1,9},{9,1},{17,25},{25,17},{2,10},{10... | collective-permute-start | bytes 5308424 | tf_op jit(solution)/shard_map/ppermute | solution.py:393
  66.6 54.8 %collective-permute-start.16 = (bf16[192,4608]{1,0:T(8,128)(2,1)}, bf16[192,4608]{1,0:T(8,128)(2,1)}, u32[]{:S(2)}, u32[]{:S(2)}) collective-permute-start(bf16[192,4608]{1,0:T(8,128)(2,1)} %bitcast.8), channel_id=1, source_target_pairs={{0,16},{8,24},{16,0},{24,8},{1,17},{9,25},{17,1},{25,9},{2,18},{10... | collective-permute-start | bytes 5308424 | tf_op jit(solution)/shard_map/ppermute | solution.py:393
  68.4 52.3 %collective-permute-start.14 = (bf16[1,96,4864]{2,1,0:T(8,128)(2,1)S(1)}, bf16[1,96,4864]{2,1,0:T(8,128)(2,1)S(1)}, u32[]{:S(2)}, u32[]{:S(2)}) collective-permute-start(bf16[1,96,4864]{2,1,0:T(8,128)(2,1)S(1)} %bitcast.191), channel_id=1, source_target_pairs={{0,4},{2,6},{4,0},{6,2},{1,5},{3,7},{5,1},{7,3},{8,12},{10,14},{12... | collective-permute-start | bytes 2801672 | tf_op jit(solution)/shard_map/ppermute | solution.py:393
  120.9 29.1 %collective-permute-start.15 = (bf16[192,4608]{1,0:T(8,128)(2,1)}, bf16[192,4608]{1,0:T(8,128)(2,1)S(1)}, u32[]{:S(2)}, u32[]{:S(2)}) collective-permute-start(bf16[192,4608]{1,0:T(8,128)(2,1)} %collective-permute-done.11), channel_id=1, source_target_pairs={{0,1},{1,0},{2,3},{3,2},{4,5},{5,4},{6,7},{7,6},{8,9},{9,8},{10,11... | collective-permute-start | bytes 5308424 | tf_op jit(solution)/shard_map/ppermute | solution.py:393
  121.3 46.2 %collective-permute-start.22 = (bf16[2,96,4864]{2,1,0:T(8,128)(2,1)S(1)}, bf16[2,96,4864]{2,1,0:T(8,128)(2,1)S(1)}, u32[]{:S(2)}, u32[]{:S(2)}) collective-permute-start(bf16[2,96,4864]{2,1,0:T(8,128)(2,1)S(1)} %pad_maximum_fusion.5), channel_id=1, source_target_pairs={{0,2},{2,0},{4,6},{6,4},{1,3},{3,1},{5,7},{7,5},{8,10},{10,8},{12,... | collective-permute-start | bytes 5603336 | tf_op jit(solution)/shard_map/ppermute | solution.py:393
  121.4 30.5 %collective-permute-start.17 = (bf16[192,4608]{1,0:T(8,128)(2,1)}, bf16[192,4608]{1,0:T(8,128)(2,1)S(1)}, u32[]{:S(2)}, u32[]{:S(2)}) collective-permute-start(bf16[192,4608]{1,0:T(8,128)(2,1)} %collective-permute-done.16), channel_id=1, source_target_pairs={{0,1},{1,0},{2,3},{3,2},{4,5},{5,4},{6,7},{7,6},{8,9},{9,8},{10,11... | collective-permute-start | bytes 5308424 | tf_op jit(solution)/shard_map/ppermute | solution.py:393
  170.5 206.5 %all-gather.7.cloned.1.call-start = ((), (), s32[]{:S(2)}) async-start(), calls=%async_computation.21 | async-start | bytes 15728640 | tf_op jit(solution)/shard_map/all_gather | solution.py:491
  184.2 46.2 %all-to-all-start = ((bf16[8,152,384]{2,1,0:T(8,128)(2,1)}), bf16[8,152,384]{2,1,0:T(8,128)(2,1)S(1)}, u32[]{:S(2)}, u32[]{:S(2)}) async-start(bf16[8,152,384]{2,1,0:T(8,128)(2,1)} %get-tuple-element.89), calls=%async_computation | async-start | bytes 1867776 | tf_op jit(solution)/shard_map/all_to_all | solution.py:631
  192.9 37.6 %collective-permute-start.26 = (bf16[1,128,1536]{2,1,0:T(8,128)(2,1)S(1)}, bf16[1,128,1536]{2,1,0:T(8,128)(2,1)S(1)}, u32[]{:S(2)}, u32[]{:S(2)}) collective-permute-start(bf16[1,128,1536]{2,1,0:T(8,128)(2,1)S(1)} %bitcast.205), channel_id=1, source_target_pairs={{0,4},{2,6},{4,0},{6,2},{1,5},{3,7},{5,1},{7,3},{8,12},{10,14},{12... | collective-permute-start | bytes 1179656 | tf_op jit(solution)/shard_map/ppermute | solution.py:393
  255.9 28.4 %all-to-all-start.5 = ((bf16[8,152,384]{2,1,0:T(8,128)(2,1)}), bf16[8,152,384]{2,1,0:T(8,128)(2,1)}, u32[]{:S(2)}, u32[]{:S(2)}) async-start(bf16[8,152,384]{2,1,0:T(8,128)(2,1)} %get-tuple-element.95), calls=%async_computation.6 | async-start | bytes 1867776 | tf_op jit(solution)/shard_map/all_to_all | solution.py:631
  260.2 141.6 %all-gather.9.cloned.1.call-start = ((), (), s32[]{:S(2)}) async-start(), calls=%async_computation.22 | async-start | bytes 7864320 | tf_op jit(solution)/shard_map/all_gather | solution.py:491
  298.5 27.8 %all-to-all-start.3 = ((bf16[8,152,384]{2,1,0:T(8,128)(2,1)}), bf16[8,152,384]{2,1,0:T(8,128)(2,1)S(1)}, u32[]{:S(2)}, u32[]{:S(2)}) async-start(bf16[8,152,384]{2,1,0:T(8,128)(2,1)} %get-tuple-element.93), calls=%async_computation.4 | async-start | bytes 1867776 | tf_op jit(solution)/shard_map/all_to_all | solution.py:631
  302.2 63.1 %collective-permute-start.24 = (bf16[1536,768]{1,0:T(8,128)(2,1)}, bf16[1536,768]{1,0:T(8,128)(2,1)}, u32[]{:S(2)}, u32[]{:S(2)}) collective-permute-start(bf16[1536,768]{1,0:T(8,128)(2,1)} %all-gather.5.cloned.1.call-done), channel_id=1, source_target_pairs={{0,1},{1,0},{2,3},{3,2},{4,5},{5,4},{6,7},{7,6},{8,9},{9,8},{10,11... | collective-permute-start | bytes 7077896 | tf_op jit(solution)/shard_map/ppermute | solution.py:393
  329.7 183.5 %reduce-scatter.8.cloned.1.call-start = ((), (), s32[]{:S(2)}) async-start(), calls=%async_computation.23 | async-start | bytes 7864320 | tf_op jit(solution)/shard_map/reduce_scatter | solution.py:525
  426.5 248.8 %reduce-scatter.12.cloned.1.call-start = ((), (), s32[]{:S(2)}) async-start(), calls=%async_computation.25 | async-start | bytes 2949120 | tf_op jit(solution)/shard_map/reduce_scatter | solution.py:525
  490.8 184.5 %reduce-scatter.10.cloned.1.call-start = ((), (), s32[]{:S(2)}) async-start(), calls=%async_computation.24 | async-start | bytes 15728640 | tf_op jit(solution)/shard_map/reduce_scatter | solution.py:525
  514.4 64.9 %collective-permute-start.33 = (bf16[2,128,1536]{2,1,0:T(8,128)(2,1)S(1)}, bf16[2,128,1536]{2,1,0:T(8,128)(2,1)}, u32[]{:S(2)}, u32[]{:S(2)}) collective-permute-start(bf16[2,128,1536]{2,1,0:T(8,128)(2,1)S(1)} %dynamic-slice_bitcast_fusion.2), channel_id=1, source_target_pairs={{0,2},{2,0},{4,6},{6,4},{1,3},{3,1},{5,7},{7,5},{8,10},{10,8},{12,... | collective-permute-start | bytes 2359304 | tf_op jit(solution)/shard_map/ppermute | solution.py:393
  524.0 26.6 %all-to-all-start.9 = ((bf16[8,152,128]{2,1,0:T(8,128)(2,1)}), bf16[8,152,128]{2,1,0:T(8,128)(2,1)S(1)}, u32[]{:S(2)}, u32[]{:S(2)}) async-start(bf16[8,152,128]{2,1,0:T(8,128)(2,1)} %get-tuple-element.110), calls=%async_computation.11 | async-start | bytes 622592 | tf_op jit(solution)/shard_map/all_to_all | solution.py:631
  550.6 33.9 %all-to-all-start.12 = ((bf16[8,152,384]{2,1,0:T(8,128)(2,1)}), bf16[8,152,384]{2,1,0:T(8,128)(2,1)}, u32[]{:S(2)}, u32[]{:S(2)}) async-start(bf16[8,152,384]{2,1,0:T(8,128)(2,1)} %bitcast.224), calls=%async_computation.14 | async-start | bytes 1867776 | tf_op jit(solution)/shard_map/all_to_all | solution.py:631
  581.6 31.5 %collective-permute-start.34 = (bf16[1,128,1536]{2,1,0:T(8,128)(2,1)}, bf16[1,128,1536]{2,1,0:T(8,128)(2,1)S(1)}, u32[]{:S(2)}, u32[]{:S(2)}) collective-permute-start(bf16[1,128,1536]{2,1,0:T(8,128)(2,1)} %constant_dynamic-slice_fusion.10), channel_id=1, source_target_pairs={{0,4},{2,6},{4,0},{6,2},{1,5},{3,7},{5,1},{7,3},{8,12},{10,14},{12... | collective-permute-start | bytes 1179656 | tf_op jit(solution)/shard_map/ppermute | solution.py:393
  584.5 38.3 %all-to-all-start.8 = ((bf16[8,152,384]{2,1,0:T(8,128)(2,1)}), bf16[8,152,384]{2,1,0:T(8,128)(2,1)}, u32[]{:S(2)}, u32[]{:S(2)}) async-start(bf16[8,152,384]{2,1,0:T(8,128)(2,1)} %bitcast.222), calls=%async_computation.10 | async-start | bytes 1867776 | tf_op jit(solution)/shard_map/all_to_all | solution.py:631
  622.8 29.1 %all-to-all-start.10 = ((bf16[8,152,384]{2,1,0:T(8,128)(2,1)}), bf16[8,152,384]{2,1,0:T(8,128)(2,1)}, u32[]{:S(2)}, u32[]{:S(2)}) async-start(bf16[8,152,384]{2,1,0:T(8,128)(2,1)} %bitcast.223), calls=%async_computation.12 | async-start | bytes 1867776 | tf_op jit(solution)/shard_map/all_to_all | solution.py:631
  627.6 185.9 %reduce-scatter.14.cloned.1.call-start = ((), (), s32[]{:S(2)}) async-start(), calls=%async_computation.26 | async-start | bytes 8847360 | tf_op jit(solution)/shard_map/reduce_scatter | solution.py:525
  675.3 150.3 %all-gather.11.cloned.1.call-start = ((), (), s32[]{:S(2)}) async-start(), calls=%async_computation.27 | async-start | bytes 6488064 | tf_op jit(solution)/shard_map/all_gather | solution.py:753
  692.0 39.7 %collective-permute-start.35 = (bf16[2,96,4096]{2,1,0:T(8,128)(2,1)}, bf16[2,96,4096]{2,1,0:T(8,128)(2,1)}, u32[]{:S(2)}, u32[]{:S(2)}) collective-permute-start(bf16[2,96,4096]{2,1,0:T(8,128)(2,1)} %dynamic-slice_bitcast_fusion), channel_id=1, source_target_pairs={{0,2},{2,0},{4,6},{6,4},{1,3},{3,1},{5,7},{7,5},{8,10},{10,8},{12,... | collective-permute-start | bytes 4718600 | tf_op jit(solution)/shard_map/ppermute | solution.py:393
  749.9 62.6 %collective-permute-start.47 = (bf16[1,96,4096]{2,1,0:T(8,128)(2,1)S(1)}, bf16[1,96,4096]{2,1,0:T(8,128)(2,1)S(1)}, u32[]{:S(2)}, u32[]{:S(2)}) collective-permute-start(bf16[1,96,4096]{2,1,0:T(8,128)(2,1)S(1)} %constant_dynamic-slice_fusion.5), channel_id=1, source_target_pairs={{0,4},{2,6},{4,0},{6,2},{1,5},{3,7},{5,1},{7,3},{8,12},{10,14},{12... | collective-permute-start | bytes 2359304 | tf_op jit(solution)/shard_map/ppermute | solution.py:393
  775.9 43.1 %collective-permute-start.42 = (f32[16,1536]{1,0:T(8,128)S(1)}, f32[16,1536]{1,0:T(8,128)S(1)}, u32[]{:S(2)}, u32[]{:S(2)}) collective-permute-start(f32[16,1536]{1,0:T(8,128)S(1)} %add.578), channel_id=1, source_target_pairs={{0,4},{2,6},{4,0},{6,2},{1,5},{3,7},{5,1},{7,3},{8,12},{10,14},{12... | collective-permute-start | bytes 294920 | tf_op jit(solution)/shard_map/ppermute | solution.py:393
  (121 other events, 1877.5 us)
Sparse Core Ops, SparseCore 0:
  41.8 154.9 reduce-scatter.5
  689.4 124.5 all-gather.10
Sparse Core Ops, SparseCore 1:
  170.6 34.7 all-gather.4
  207.1 122.3 all-gather.6
  331.8 70.0 all-gather.8
  426.6 70.0 reduce-scatter.7
  499.7 37.2 reduce-scatter.11
  540.1 120.5 reduce-scatter.9
  675.4 76.4 reduce-scatter.13
